TPU v7x, 32 devices: a whole 2x2x4 slice. The times are simulated.
32 devices in a mesh: groups: 2 (over y), aa: 4 (over z), ba: 4 (over x, core).
Axes of the slice: x: 2, y: 2, z: 4, core: 2. Of those that a mesh axis runs over, the one named last changes fastest.
Arguments:
- alignment_state: bfloat16 [64, 128, 256], P(('groups', 'aa'), 'ba'), parts along dimension 0, may hold values from -1.5 to 1.5
- pair_state: bfloat16 [256, 128, 128], P(('groups', 'aa'), 'ba'), parts along dimension 0, may hold values from -1.796875 to 1.796875
- alignment_mask: int32 [64, 128], P(('groups', 'aa'), 'ba'), parts along dimension 0, may hold values from 0 to 1, as said below
- left_weight: bfloat16 [256, 32], replicated, may hold values from -0.375 to 0.375
- right_weight: bfloat16 [256, 32], replicated, may hold values from -0.375 to 0.375
- outer_output_weight: bfloat16 [1024, 128], replicated, may hold values from -0.75 to 0.75
- pair_bias_weight: bfloat16 [128, 8], replicated, may hold values from -40 to 40
- query_weight: bfloat16 [256, 256], replicated, may hold values from -0.375 to 0.375
- key_weight: bfloat16 [256, 256], replicated, may hold values from -0.375 to 0.375
- value_weight: bfloat16 [256, 256], replicated, may hold values from -0.375 to 0.375
- gate_weight: bfloat16 [256, 256], replicated, may hold values from -0.375 to 0.375
- output_weight: bfloat16 [256, 256], replicated, may hold values from -1.5 to 1.5
- up_weight: bfloat16 [256, 1024], replicated, may hold values from -0.375 to 0.375
- down_weight: bfloat16 [1024, 256], replicated, may hold values from -0.1875 to 0.1875
Outputs:
- alignment_output: bfloat16 [64, 128, 256], P(('groups', 'aa'), 'ba'), parts along dimension 0
- pair_output: bfloat16 [256, 128, 128], P(('groups', 'aa'), 'ba'), parts along dimension 0
There are 2 independent parts, one for each index of `groups`. A program takes and returns all parts, laid end to end along the dimension named above; an argument that names none is the same for every part. Nothing has to cross between parts.
Inputs may be any that keep to these rules, and one draw needn't show every extreme that they name: `alignment_mask`: every residue of the first sequence is kept (mask 1); other entries are kept at random.
All inputs are finite; a program needn't handle non-finite values.
Results may differ from a plain program's by a relative error of at most 0.013.
The roundings to bfloat16 on the way count: a program that leaves them out, or rounds other values in their place, can miss the bound.
Values may be sent and summed in bfloat16 or wider, within the bound.
No kernel may reach another device: no remote copies, remote signals or barrier semaphores. Data moves between devices by JAX's collectives and lax.ppermute only.
A program may use at most 128 MiB of HBM per device.

v0:
```python
import jax
import jax.numpy as jnp
from jax import lax
from jax.sharding import PartitionSpec as P


def from_root(x, axis, root):
    mine = lax.axis_index(axis) == root
    return lax.psum(jnp.where(mine, x, jnp.zeros_like(x)), axis)


def row_norm_input(values):
    center = values - jnp.mean(values, axis=-1, keepdims=True)
    spread = jnp.mean(center * center, axis=-1, keepdims=True)
    return center * lax.rsqrt(spread + 1e-05)


def attend_block(carried, query_all, key_piece, value_piece, valid_piece, bias_part):
    top_old, mass_old, accum_old = carried
    scores = (
        jnp.einsum("sihd,sjhd->shij", query_all, key_piece, preferred_element_type=jnp.float32)
        + bias_part[None]
    )
    scores = jnp.where(valid_piece[:, None, None, :] > 0, scores, -1000000000.0)
    new_top = jnp.maximum(top_old, jnp.max(scores, axis=-1))
    weights_raw = jnp.exp(scores - new_top[:, :, :, None])
    mass_new = jnp.sum(weights_raw, axis=-1)
    accum_new = jnp.einsum(
        "shij,sjhd->shid",
        weights_raw.astype(jnp.bfloat16),
        value_piece,
        preferred_element_type=jnp.float32,
    )
    return (new_top, mass_new, accum_new)


def per_device(
    alignment_state,
    pair_state,
    alignment_mask,
    left_weight,
    right_weight,
    outer_output_weight,
    pair_bias_weight,
    query_weight,
    key_weight,
    value_weight,
    gate_weight,
    output_weight,
    up_weight,
    down_weight,
):
    sequence_count, residue_count, channel_count = alignment_state.shape
    opm_width = left_weight.shape[1]
    num_heads = pair_bias_weight.shape[1]
    head_width = query_weight.shape[1] // num_heads
    layer_normed = row_norm_input(alignment_state.astype(jnp.float32)).astype(jnp.bfloat16)
    flat_rows = layer_normed.reshape(sequence_count * residue_count, channel_count)
    row_keep_mask = alignment_mask.astype(jnp.float32)
    keep_half = row_keep_mask.astype(jnp.bfloat16)
    left_fac = (
        jnp.dot(flat_rows, left_weight, preferred_element_type=jnp.float32).reshape(
            sequence_count, residue_count, opm_width
        )
        * row_keep_mask[:, :, None]
    ).astype(jnp.bfloat16)
    right_fac = (
        jnp.dot(flat_rows, right_weight, preferred_element_type=jnp.float32).reshape(
            sequence_count, residue_count, opm_width
        )
        * row_keep_mask[:, :, None]
    ).astype(jnp.bfloat16)
    col_left, col_right, col_keep = (
        lax.all_gather(left_fac, "aa", axis=0, tiled=True),
        lax.all_gather(right_fac, "aa", axis=0, tiled=True),
        lax.all_gather(keep_half, "aa", axis=0, tiled=True),
    )
    row_left, row_keep = (
        from_root(col_left, "ba", lax.axis_index("aa")),
        from_root(col_keep, "ba", lax.axis_index("aa")),
    )
    seq_total = col_right.shape[0]
    pair_count = jnp.dot(row_keep.T, col_keep, preferred_element_type=jnp.float32)
    left_flat = row_left.reshape(seq_total, residue_count * opm_width)
    right_flat = col_right.reshape(seq_total, residue_count * opm_width)
    row_block = 8

    def outer_block(block_index):
        left_part = lax.dynamic_slice_in_dim(
            left_flat, block_index * (row_block * opm_width), row_block * opm_width, 1
        )
        outer_sum = lax.dot_general(
            left_part, right_flat, (((0,), (0,)), ((), ())), preferred_element_type=jnp.float32
        )
        outer_sum = outer_sum.reshape(row_block, opm_width, residue_count, opm_width).transpose(
            0, 2, 1, 3
        )
        outer_sum = outer_sum.reshape(row_block * residue_count, opm_width * opm_width).astype(
            jnp.bfloat16
        )
        return jnp.dot(outer_sum, outer_output_weight, preferred_element_type=jnp.float32).reshape(
            row_block, residue_count, -1
        )

    update = lax.map(outer_block, jnp.arange(residue_count // row_block, dtype=jnp.int32)).reshape(
        residue_count, residue_count, -1
    )
    pair_output = (pair_state.astype(jnp.float32) + update / pair_count[:, :, None]).astype(
        jnp.bfloat16
    )
    pair_normed = row_norm_input(pair_output.astype(jnp.float32)).astype(jnp.bfloat16)
    tile_bias = jnp.dot(
        pair_normed.reshape(residue_count * residue_count, -1),
        pair_bias_weight,
        preferred_element_type=jnp.float32,
    )
    tile_bias = tile_bias.reshape(residue_count, residue_count, num_heads).transpose(2, 0, 1)
    rows_bias = lax.all_gather(tile_bias, "ba", axis=2, tiled=True)
    bias_here = from_root(rows_bias, "aa", lax.axis_index("ba"))
    score_scale = head_width ** (-0.5)
    query_all = (
        (jnp.dot(flat_rows, query_weight, preferred_element_type=jnp.float32) * score_scale)
        .astype(jnp.bfloat16)
        .reshape(sequence_count, residue_count, num_heads, head_width)
    )
    gate_act = jax.nn.sigmoid(jnp.dot(flat_rows, gate_weight, preferred_element_type=jnp.float32))
    start_state = (
        jnp.full((sequence_count, num_heads, residue_count), -1e30, jnp.float32),
        jnp.zeros((sequence_count, num_heads, residue_count), jnp.float32),
        jnp.zeros((sequence_count, num_heads, residue_count, head_width), jnp.float32),
    )
    w_pair = jnp.concatenate((key_weight, value_weight), axis=1)
    rows_in = lax.all_gather(layer_normed, "ba", axis=1, tiled=True)
    valid_piece = lax.all_gather(keep_half, "ba", axis=1, tiled=True)
    span_len = rows_in.shape[1]
    key_value = jnp.dot(
        rows_in.reshape(sequence_count * span_len, channel_count),
        w_pair,
        preferred_element_type=jnp.float32,
    ).astype(jnp.bfloat16)
    key_value = key_value.reshape(sequence_count, span_len, 2, num_heads, head_width)
    final_state = attend_block(
        start_state, query_all, key_value[:, :, 0], key_value[:, :, 1], valid_piece, bias_here
    )
    attended = final_state[2] / final_state[1][:, :, :, None]
    attended = attended.transpose(0, 2, 1, 3).reshape(
        sequence_count * residue_count, num_heads * head_width
    )
    gated_row_output = (attended * gate_act).astype(jnp.bfloat16)
    alignment_middle = alignment_state.astype(jnp.float32) + jnp.dot(
        gated_row_output, output_weight, preferred_element_type=jnp.float32
    ).reshape(sequence_count, residue_count, channel_count)
    middle_normed = (
        row_norm_input(alignment_middle)
        .astype(jnp.bfloat16)
        .reshape(sequence_count * residue_count, channel_count)
    )
    hidden_units = jax.nn.relu(
        jnp.dot(middle_normed, up_weight, preferred_element_type=jnp.float32)
    ).astype(jnp.bfloat16)
    alignment_output = (
        alignment_middle
        + jnp.dot(hidden_units, down_weight, preferred_element_type=jnp.float32).reshape(
            sequence_count, residue_count, channel_count
        )
    ).astype(jnp.bfloat16)
    return (alignment_output, pair_output)


def solution(mesh):
    return jax.shard_map(
        per_device,
        mesh=mesh,
        in_specs=(
            P(("groups", "aa"), "ba", None),
            P(("groups", "aa"), "ba", None),
            P(("groups", "aa"), "ba"),
            P(),
            P(),
            P(),
            P(),
            P(),
            P(),
            P(),
            P(),
            P(),
            P(),
            P(),
        ),
        out_specs=(P(("groups", "aa"), "ba", None), P(("groups", "aa"), "ba", None)),
        check_vma=False,
    )
```

profile of v0, /device:TPU:6, one launch (start us, length us, event | category | flops | bytes accessed | tf_op | source)
XLA Modules:
  0.0 186.6 jit_solution(4134955716603868108)
XLA Ops:
  7.3 1.1 convert_reduce_fusion.1
  8.4 1.1 fusion.30
  9.5 1.0 fusion.31
  10.5 0.7 convert_convert_fusion
  11.2 0.9 fusion.15
  12.1 14.2 %all_gather.20 = bf16[32,32,32]{2,1,0:T(8,128)(2,1)S(1)} all-gather(bf16[8,32,32]{2,1,0:T(8,128)(2,1)S(1)} %fusion.15), channel_id=1, replica_groups=mesh['groups'=2,'aa'=4,'ba'=4] {'aa'}, dimensions={0}, use_global_device_ids=true | all-gather | bytes 81920 | tf_op jit(solution)/shard_map/all_gather | solution.py:74
  26.3 0.9 reshape.112
  27.3 6.5 %all_gather.19 = bf16[8,128,256]{2,1,0:T(8,128)(2,1)S(1)} all-gather(bf16[8,32,256]{2,1,0:T(8,128)(2,1)S(1)} %fusion.31), channel_id=1, replica_groups=mesh['groups'=2,'aa'=4,'ba'=4] {'ba'}, dimensions={1}, use_global_device_ids=true | all-gather | bytes 655360 | tf_op jit(solution)/shard_map/all_gather | solution.py:133
  33.8 0.2 fusion.16
  34.0 12.0 %all_gather.22 = bf16[32,32]{1,0:T(8,128)(2,1)S(1)} all-gather(bf16[8,32]{1,0:T(8,128)(2,1)S(1)} %get-tuple-element.49), channel_id=1, replica_groups=mesh['groups'=2,'aa'=4,'ba'=4] {'aa'}, dimensions={0}, use_global_device_ids=true | all-gather | bytes 2560 | tf_op jit(solution)/shard_map/all_gather | solution.py:76
  46.0 5.8 %psum.22 = bf16[32,32]{1,0:T(8,128)(2,1)S(1)} all-reduce(bf16[32,32]{1,0:T(8,128)(2,1)S(1)} %broadcast_select_fusion.2), channel_id=1, replica_groups=mesh['groups'=2,'aa'=4,'ba'=4] {'ba'}, use_global_device_ids=true, to_apply=%region_5.6 | all-reduce | flops 1024 | bytes 4096 | tf_op jit(solution)/shard_map/psum | solution.py:9
  51.8 0.4 convolution_convert_fusion.1
  52.2 0.5 copy.31
  52.8 0.3 copy.40
  53.1 1.1 fusion.46
  54.2 0.2 fusion.13
  54.3 0.2 fusion.48
  54.5 13.9 %all_gather.21 = bf16[32,32,32]{2,1,0:T(8,128)(2,1)S(1)} all-gather(bf16[8,32,32]{2,1,0:T(8,128)(2,1)S(1)} %fusion.16), channel_id=1, replica_groups=mesh['groups'=2,'aa'=4,'ba'=4] {'aa'}, dimensions={0}, use_global_device_ids=true | all-gather | bytes 81920 | tf_op jit(solution)/shard_map/all_gather | solution.py:75
  68.4 0.9 reshape.113
  69.3 1.0 reshape.109
  70.3 5.6 %all-gather = bf16[4,32,8]{1,2,0:T(8,128)(2,1)} all-gather(bf16[1,32,8]{1,2,0:T(8,128)(2,1)S(1)} %bitcast.97), channel_id=1, replica_groups=mesh['groups'=2,'aa'=4,'ba'=4] {'ba'}, dimensions={0}, use_global_device_ids=true | all-gather | bytes 2560 | tf_op jit(solution)/shard_map/all_gather | solution.py:134
  76.0 0.5 iota.3
  76.5 45.7 %while.10 = (s32[]{:T(128)}, f32[4,8,32,128]{3,2,1,0:T(8,128)}, s32[4]{0:T(128)}, bf16[32,1024]{1,0:T(8,128)(2,1)}, bf16[32,1024]{1,0:T(8,128)(2,1)}, /*index=5*...) while((s32[]{:T(128)}, f32[4,8,32,128]{3,2,1,0:T(8,128)}, s32[4]{0:T(128)}, ...), condition=%wide.region_4.5_spmd, body=%wide.region_3.4_spmd.sunk | while | flops 84148224 | bytes 4670115 | solution.py:105
  76.5 1.3 dynamic_slice.12
  78.5 1.2 convolution_convert_fusion.3
  79.7 1.6 convert_element_type.141
  81.3 2.2 %copy.52 = bf16[8,32,32,32]{3,2,1,0:T(8,128)(2,1)} copy(bf16[8,32,32,32]{3,1,2,0:T(8,128)(2,1)S(1)} %bitcast.86) | data formatting | bytes 1048576 | tf_op jit(solution)/shard_map/while/body/eval_jaxpr/convert_element_type | solution.py:98
  83.4 3.5 %convert_element_type.142 = bf16[8,32,1024]{2,1,0:T(8,128)(2,1)S(1)} reshape(bf16[8,32,32,32]{3,2,1,0:T(8,128)(2,1)} %copy.52) | data formatting | bytes 1048576 | tf_op jit(solution)/shard_map/while/body/eval_jaxpr/convert_element_type | solution.py:98
  87.0 0.9 fusion.73
  87.9 1.3 dynamic_slice.12
  89.9 1.2 convolution_convert_fusion.3
  91.1 1.6 convert_element_type.141
  92.7 2.2 %copy.52 = bf16[8,32,32,32]{3,2,1,0:T(8,128)(2,1)} copy(bf16[8,32,32,32]{3,1,2,0:T(8,128)(2,1)S(1)} %bitcast.86) | data formatting | bytes 1048576 | tf_op jit(solution)/shard_map/while/body/eval_jaxpr/convert_element_type | solution.py:98
  94.8 3.5 %convert_element_type.142 = bf16[8,32,1024]{2,1,0:T(8,128)(2,1)S(1)} reshape(bf16[8,32,32,32]{3,2,1,0:T(8,128)(2,1)} %copy.52) | data formatting | bytes 1048576 | tf_op jit(solution)/shard_map/while/body/eval_jaxpr/convert_element_type | solution.py:98
  98.4 0.9 fusion.73
  99.3 1.3 dynamic_slice.12
  101.3 1.2 convolution_convert_fusion.3
  102.5 1.6 convert_element_type.141
  104.1 2.2 %copy.52 = bf16[8,32,32,32]{3,2,1,0:T(8,128)(2,1)} copy(bf16[8,32,32,32]{3,1,2,0:T(8,128)(2,1)S(1)} %bitcast.86) | data formatting | bytes 1048576 | tf_op jit(solution)/shard_map/while/body/eval_jaxpr/convert_element_type | solution.py:98
  106.3 3.5 %convert_element_type.142 = bf16[8,32,1024]{2,1,0:T(8,128)(2,1)S(1)} reshape(bf16[8,32,32,32]{3,2,1,0:T(8,128)(2,1)} %copy.52) | data formatting | bytes 1048576 | tf_op jit(solution)/shard_map/while/body/eval_jaxpr/convert_element_type | solution.py:98
  109.8 0.9 fusion.73
  110.7 1.3 dynamic_slice.12
  112.7 1.2 convolution_convert_fusion.3
  113.9 1.6 convert_element_type.141
  115.5 2.2 %copy.52 = bf16[8,32,32,32]{3,2,1,0:T(8,128)(2,1)} copy(bf16[8,32,32,32]{3,1,2,0:T(8,128)(2,1)S(1)} %bitcast.86) | data formatting | bytes 1048576 | tf_op jit(solution)/shard_map/while/body/eval_jaxpr/convert_element_type | solution.py:98
  117.7 3.5 %convert_element_type.142 = bf16[8,32,1024]{2,1,0:T(8,128)(2,1)S(1)} reshape(bf16[8,32,32,32]{3,2,1,0:T(8,128)(2,1)} %copy.52) | data formatting | bytes 1048576 | tf_op jit(solution)/shard_map/while/body/eval_jaxpr/convert_element_type | solution.py:98
  121.2 1.0 fusion.73
  122.2 1.3 fusion.24
  123.5 0.2 convert_reduce_fusion
  123.8 0.4 fusion.21
  124.2 1.2 convolution_bitcast_fusion.2
  125.5 7.3 %all_gather.23 = f32[8,32,128]{1,0,2:T(8,128)S(1)} all-gather(f32[8,32,32]{1,0,2:T(8,128)S(1)} %copy.34), channel_id=1, replica_groups=mesh['groups'=2,'aa'=4,'ba'=4] {'ba'}, dimensions={2}, use_global_device_ids=true | all-gather | bytes 163840 | tf_op jit(solution)/shard_map/all_gather | solution.py:118
  132.8 0.8 broadcast_select_fusion
  133.8 39.3 %all-reduce.5.cloned.1.call-done = f32[8,32,128]{1,0,2:T(8,128)} async-done(((f32[8,32,128]{1,0,2:T(8,128)}), f32[8,32,128]{1,0,2:T(8,128)}) %all-reduce.5.cloned.1.call-update) | async-done | bytes 131088 | tf_op jit(solution)/shard_map/psum | solution.py:9
  173.1 1.2 copy.35
  174.3 0.5 fusion.47
  174.8 0.7 fusion.17
  175.5 1.1 fusion.4
  176.6 0.6 copy.37
  177.3 0.3 reshape.115
  177.6 0.3 fusion.14
  178.1 0.2 multiply_reduce_fusion
  178.5 0.5 fusion.7
  179.0 0.7 add_convert_fusion
  (51 shorter events, 0.7 us)
Async XLA Ops:
  7.2 171.3 %copy-start = (bf16[1024,256]{1,0:T(8,128)(2,1)S(1)}, bf16[1024,256]{1,0:T(8,128)(2,1)}, u32[]{:S(2)}) copy-start(bf16[1024,256]{1,0:T(8,128)(2,1)} %param.29) | copy-start | bytes 1572868
  7.2 26.6 %copy-start.11 = (bf16[256,32]{0,1:T(8,128)(2,1)S(1)}, bf16[256,32]{0,1:T(8,128)(2,1)}, u32[]{:S(2)}) copy-start(bf16[256,32]{0,1:T(8,128)(2,1)} %param.20) | copy-start | bytes 49156
  7.2 44.6 %copy-start.8 = (bf16[256,256]{1,0:T(8,128)(2,1)S(1)}, bf16[256,256]{1,0:T(8,128)(2,1)}, u32[]{:S(2)}) copy-start(bf16[256,256]{1,0:T(8,128)(2,1)} %param.24) | copy-start | bytes 393220
  7.2 44.6 %copy-start.7 = (bf16[256,256]{1,0:T(8,128)(2,1)S(1)}, bf16[256,256]{1,0:T(8,128)(2,1)}, u32[]{:S(2)}) copy-start(bf16[256,256]{1,0:T(8,128)(2,1)} %param.25) | copy-start | bytes 393220
  7.2 68.8 %all-reduce.3.cloned.1.call-start = ((), (), s32[]{:S(2)}) async-start(), calls=%async_computation | async-start | bytes 131072 | tf_op jit(solution)/shard_map/psum | solution.py:9
  27.3 145.8 %all-reduce.5.cloned.1.call-start = ((), (), s32[]{:S(2)}) async-start(), calls=%async_computation.1 | async-start | bytes 1048576 | tf_op jit(solution)/shard_map/psum | solution.py:9
  52.8 1.4 copy-start.9
  53.1 23.4 %copy-start.1 = (bf16[1024,128]{1,0:T(8,128)(2,1)S(1)}, bf16[1024,128]{1,0:T(8,128)(2,1)}, u32[]{:S(2)}) copy-start(bf16[1024,128]{1,0:T(8,128)(2,1)} %param.21) | copy-start | bytes 786436
  123.5 50.8 %copy-start.3 = (bf16[32,32,128]{2,1,0:T(8,128)(2,1)}, bf16[32,32,128]{2,1,0:T(8,128)(2,1)S(1)}, u32[]{:S(2)}) copy-start(bf16[32,32,128]{2,1,0:T(8,128)(2,1)S(1)} %fusion.24) | copy-start | bytes 786436
  123.5 10.1 %copy-start.10 = (bf16[4,32,8]{1,2,0:T(8,128)(2,1)S(1)}, bf16[4,32,8]{1,2,0:T(8,128)(2,1)}, u32[]{:S(2)}) copy-start(bf16[4,32,8]{1,2,0:T(8,128)(2,1)} %all-gather) | copy-start | bytes 6148
  123.7 50.6 %copy-start.4 = (bf16[8,32,8,32]{3,2,1,0:T(8,128)(2,1)S(1)}, bf16[8,32,8,32]{3,2,1,0:T(8,128)(2,1)}, u32[]{:S(2)}) copy-start(bf16[8,32,8,32]{3,2,1,0:T(8,128)(2,1)} %reshape.109) | copy-start | bytes 393220
  123.7 50.6 %copy-start.6 = (bf16[8,128,1,8,32]{1,0,4,3,2:T(8,128)(2,1)S(1)}, bf16[8,128,1,8,32]{1,0,4,3,2:T(8,128)(2,1)}, u32[]{:S(2)}) copy-start(bf16[8,128,1,8,32]{1,0,4,3,2:T(8,128)(2,1)} %get-tuple-element.48) | copy-start | bytes 1572868
  133.8 41.7 %copy-start.5 = (bf16[8,128,1,8,32]{1,0,4,3,2:T(8,128)(2,1)S(1)}, bf16[8,128,1,8,32]{1,0,4,3,2:T(8,128)(2,1)}, u32[]{:S(2)}) copy-start(bf16[8,128,1,8,32]{1,0,4,3,2:T(8,128)(2,1)} %get-tuple-element.47) | copy-start | bytes 1572868
  176.6 1.0 copy-start.13
  176.6 1.0 copy-start.14
  176.6 1.3 copy-start.2
  177.3 1.2 copy-start.12
Sparse Core Ops, SparseCore 0:
  27.4 32.0 all-reduce.2
  133.8 39.2 all-reduce.4
where the time goes:
time: 189 us; the launch traced here: 187 us
  blocking collectives  65.3 us (35%)
  local copies, waits for them, and re-layouts  42 us (22%)
  waiting for transfers between devices  39.3 us (21%)
  between operations  14.5 us (8%)
  matrix products  14 us (7%)
  other arithmetic  8.53 us (5%)
  loops' own time  2.9 us (2%)
    psum x2, waiting for transfers between devices, from_root(): return lax.psum(jnp.where(mine, x, jnp.zeros_like(x)), axis)  39.3 us
    convert_element_type x12, local copies, waits for them, and re-layouts, outer_block(): outer_sum.reshape(row_block * residue_count, opm_width * opm_width)  29.1 us
    all_gather x1, blocking collectives, per_device(): lax.all_gather(left_fac, 'aa', axis=0, tiled=True)  14.2 us
    all_gather x1, blocking collectives, per_device(): lax.all_gather(right_fac, 'aa', axis=0, tiled=True)  13.9 us
    all_gather x1, blocking collectives, per_device(): lax.all_gather(keep_half, 'aa', axis=0, tiled=True)  12 us
    all_gather x1, blocking collectives, per_device(): rows_bias = lax.all_gather(tile_bias, 'ba', axis=2, tiled=True)  7.28 us
    all_gather x1, blocking collectives, per_device(): rows_in = lax.all_gather(layer_normed, 'ba', axis=1, tiled=True)  6.5 us
    psum x1, blocking collectives, from_root(): return lax.psum(jnp.where(mine, x, jnp.zeros_like(x)), axis)  5.78 us
  transfers between devices with their start and end apart: 2, of which 1 were waited for; matrix products, arithmetic and copies ran while one was open for 3% of the time, Pallas kernels for 0%

commit v1 on v0

v1 whole, which is shorter than its diff:
```python
import functools

import jax
import jax.numpy as jnp
from jax import lax
from jax.experimental import pallas as pl
from jax.experimental.pallas import tpu as pltpu
from jax.sharding import PartitionSpec as P

F32 = jnp.float32
BF16 = jnp.bfloat16
LANES = 128
EPS = 1e-05
VMEM_LIMIT = 56 * 1024 * 1024


def layer_norm(values):
    center = values - jnp.mean(values, axis=-1, keepdims=True)
    spread = jnp.mean(center * center, axis=-1, keepdims=True)
    return center * lax.rsqrt(spread + EPS)


def iota(shape, dim):
    return lax.broadcasted_iota(jnp.int32, shape, dim)


def spread_matrix(rows, cols, row_of_col):
    return (iota((rows, cols), 0) == row_of_col(iota((rows, cols), 1))).astype(F32).astype(BF16)


def dot(x, y):
    return jnp.dot(x, y, preferred_element_type=F32)


def dot_tn(x, y):
    return lax.dot_general(x, y, (((0,), (0,)), ((), ())), preferred_element_type=F32)


def dot_nt(x, y):
    return lax.dot_general(x, y, (((1,), (1,)), ((), ())), preferred_element_type=F32)


def factor_kernel(seqs, res, x_ref, mask_ref, wl_ref, wr_ref, rows_ref, fac_ref, y_scr):
    width = wl_ref.shape[1]
    per = LANES // width
    normed = layer_norm(x_ref[...].astype(F32)).astype(BF16)
    keep = (mask_ref[...] > 0).astype(F32).astype(BF16)
    rows_ref[: seqs * res, :] = normed
    tail = rows_ref.shape[0] - seqs * res
    keep_wide = dot(keep, spread_matrix(res, rows_ref.shape[1], lambda c: c))
    rows_ref[seqs * res :, :] = jnp.concatenate(
        [keep_wide, jnp.zeros((tail - seqs, rows_ref.shape[1]), F32)], axis=0
    ).astype(BF16)
    repeat = spread_matrix(width, LANES, lambda c: c % width)
    w_left = dot(wl_ref[...], repeat).astype(BF16)
    w_right = dot(wr_ref[...], repeat).astype(BF16)
    y_scr[0] = dot(normed, w_left)
    y_scr[1] = dot(normed, w_right)
    keep_rep = dot(keep, spread_matrix(res, res * width, lambda c: c // width))
    segment = iota((seqs, LANES), 1) // width
    span = res * width
    for side in range(2):
        for group in range(res // per):
            value = None
            for k in range(per):
                piece = y_scr.at[side][pl.ds(group * per + k, seqs, stride=res), :]
                value = piece if value is None else jnp.where(segment == k, piece, value)
            lanes = slice(group * LANES, (group + 1) * LANES)
            fac_ref[:, side * span + group * LANES : side * span + (group + 1) * LANES] = (
                value * keep_rep[:, lanes]
            ).astype(BF16)
    fac_ref[:, 2 * span :] = keep_wide[:, :LANES].astype(BF16)


def pick_kernel(count_a, count_b, span, *refs):
    ins, outs, scr = refs[:count_b], refs[count_b : count_b + count_a], refs[-1]
    row, col = lax.axis_index("aa"), lax.axis_index("ba")
    for k in range(count_b):
        scr[lax.bitwise_xor(col, k)] = ins[k][...]
    own = ins[0][...]
    for k in range(count_a):
        theirs = scr[lax.bitwise_xor(row, k)]
        outs[k][:, :span] = theirs[:, :span]
        outs[k][:, span : 2 * span] = own[:, span : 2 * span]
        outs[k][:, 2 * span : 2 * span + LANES] = theirs[:, 2 * span :]
        outs[k][:, 2 * span + LANES :] = own[:, 2 * span :]


def pair_kernel(count_a, res, width, *refs):
    msgs = refs[:count_a]
    pair_ref, wout_ref, wbias_ref, out_ref, bias_ref, rt_scr, wf_scr, wp_scr, a_scr = refs[count_a:]
    span = res * width
    per = LANES // width
    msg = jnp.concatenate([m[...].astype(F32) for m in msgs], axis=0)
    left = msg[:, :span].astype(BF16)
    keep_row = msg[:, 2 * span : 2 * span + res].astype(BF16)
    keep_col = msg[:, 2 * span + LANES : 2 * span + LANES + res].astype(BF16)
    seq_total = msg.shape[0]
    for t in range(rt_scr.shape[0]):
        rows = msg[t * LANES : (t + 1) * LANES, span : 2 * span].T
        rt_scr[t, :, : rows.shape[1]] = rows
    wf_scr[...] = wout_ref[...].astype(F32)
    for d in range(width):
        wp_scr[d * width : (d + 1) * width, :] = wf_scr[pl.ds(d, width, stride=width), :].astype(BF16)
    lane = iota((res, LANES), 1)
    segment = lane // width
    for block in range(width // per):
        lhs = jnp.concatenate(
            [
                jnp.concatenate(
                    [rt_scr.at[t][pl.ds(block * per + k, res, stride=width), :] for k in range(per)],
                    axis=0,
                )
                for t in range(rt_scr.shape[0])
            ],
            axis=1,
        )[:, :seq_total].astype(BF16)
        prod = dot(lhs, left).astype(BF16)
        for group in range(span // LANES):
            tiles = [
                prod[k * res : (k + 1) * res, group * LANES : (group + 1) * LANES] for k in range(per)
            ]
            step = per // 2
            while step >= 1:
                low = (segment & step) == 0
                for k in range(per):
                    if k & step:
                        continue
                    first, second = tiles[k], tiles[k + step]
                    tiles[k] = jnp.where(low, first, pltpu.roll(second, step * width, 1))
                    tiles[k + step] = jnp.where(
                        low, pltpu.roll(first, LANES - step * width, 1), second
                    )
                step //= 2
            for k in range(per):
                i = group * per + k
                a_scr[i * res : (i + 1) * res, block * LANES : (block + 1) * LANES] = tiles[k]
    counts = dot_tn(keep_col, keep_row)
    inverse = 1.0 / counts
    heads = wbias_ref.shape[1]
    w_rep = dot(wbias_ref[...], spread_matrix(heads, heads * res, lambda c: c // res)).astype(BF16)
    query = iota((res, heads * res), 1) % res
    bias = jnp.zeros((res, heads * res), F32)
    chunk = 8
    for start in range(0, res, chunk):
        upd = dot(a_scr[start * res : (start + chunk) * res, :], wp_scr[...])
        for i in range(start, start + chunk):
            mine = upd[(i - start) * res : (i - start + 1) * res]
            total = (pair_ref[i].astype(F32) + mine * inverse[:, i : i + 1]).astype(BF16)
            out_ref[i] = total
            normed = layer_norm(total.astype(F32)).astype(BF16)
            bias = jnp.where(query == i, dot(normed, w_rep), bias)
    bias_ref[...] = bias


def attention_kernel(seqs, res, heads, count_b, *refs):
    rows_refs, bias_refs = refs[:count_b], refs[count_b : 2 * count_b]
    (x_ref, wq_ref, wk_ref, wv_ref, wg_ref, wo_ref, up_ref, down_ref, out_ref) = refs[
        2 * count_b : 2 * count_b + 9
    ]
    bias_scr, kv_scr, att_scr = refs[2 * count_b + 9 :]
    row, col = lax.axis_index("aa"), lax.axis_index("ba")
    channels = wq_ref.shape[1]
    head_width = channels // heads
    wide = heads * res
    offset = lax.bitwise_xor(row, col)
    for k in range(count_b):
        at = pl.multiple_of(lax.bitwise_xor(offset, k) * res, res)
        bias_scr[pl.ds(at, res), :] = bias_refs[k][...]
    own = rows_refs[0][: seqs * res, :]
    w_kv = jnp.concatenate([wk_ref[...], wv_ref[...]], axis=1)
    spread = spread_matrix(seqs, seqs * LANES, lambda c: c // LANES)
    keeps = []
    for k in range(count_b):
        kv = dot(rows_refs[k][: seqs * res, :], w_kv).astype(BF16)
        for s in range(seqs):
            kv_scr[s, k * res : (k + 1) * res, :] = kv[s * res : (s + 1) * res]
        keeps.append(dot_tn(rows_refs[k][seqs * res : seqs * res + seqs, :res], spread))
    query = (dot(own, wq_ref[...]) * (head_width ** (-0.5))).astype(BF16)
    gate = jax.nn.sigmoid(dot(own, wg_ref[...]))
    same_head = iota((wide, channels), 0) // res == iota((wide, channels), 1) // head_width
    lane_head = iota((res, channels), 1) // head_width
    masses = []
    for s in range(seqs):
        query_s = query[s * res : (s + 1) * res]
        query_wide = jnp.where(
            same_head, jnp.concatenate([query_s] * heads, axis=0), jnp.zeros((), BF16)
        )
        scores = dot_nt(kv_scr[s, :, :channels], query_wide) + bias_scr[...]
        keep = jnp.concatenate([m[:, s * LANES : (s + 1) * LANES] for m in keeps], axis=0)
        keep = jnp.concatenate([keep] * (wide // LANES), axis=1)
        scores = jnp.where(keep > 0, scores, -1000000000.0)
        raw = jnp.exp(scores - jnp.max(scores, axis=0, keepdims=True))
        masses.append(jnp.sum(raw, axis=0, keepdims=True))
        mixed = dot_tn(raw.astype(BF16), kv_scr[s, :, channels:])
        picked = mixed[:res]
        for h in range(1, heads):
            picked = jnp.where(lane_head == h, mixed[h * res : (h + 1) * res], picked)
        att_scr[s * res : (s + 1) * res, :] = picked
    mass_rows = jnp.concatenate([jnp.broadcast_to(1.0 / m, (res, wide)) for m in masses], axis=0)
    diag = iota((seqs * res, wide), 0) % res == iota((seqs * res, wide), 1) % res
    head_pick = (iota((wide, channels), 0) // res == iota((wide, channels), 1) // head_width).astype(F32)
    inverse = jnp.dot(
        jnp.where(diag, mass_rows, 0.0),
        head_pick,
        preferred_element_type=F32,
        precision=lax.Precision.HIGHEST,
    )
    gated = (att_scr[...] * inverse * gate).astype(BF16)
    middle = x_ref[...].astype(F32) + dot(gated, wo_ref[...])
    hidden = jnp.maximum(dot(layer_norm(middle).astype(BF16), up_ref[...]), 0.0).astype(BF16)
    out_ref[...] = (middle + dot(hidden, down_ref[...])).astype(BF16)


def call(kernel, outs, scratch=()):
    return pl.pallas_call(
        kernel,
        out_shape=outs,
        scratch_shapes=scratch,
        compiler_params=pltpu.CompilerParams(vmem_limit_bytes=VMEM_LIMIT),
    )


def per_device(
    count_a,
    count_b,
    alignment_state,
    pair_state,
    alignment_mask,
    left_weight,
    right_weight,
    outer_output_weight,
    pair_bias_weight,
    query_weight,
    key_weight,
    value_weight,
    gate_weight,
    output_weight,
    up_weight,
    down_weight,
):
    seqs, res, channels = alignment_state.shape
    width = left_weight.shape[1]
    heads = pair_bias_weight.shape[1]
    span = res * width
    shape = jax.ShapeDtypeStruct

    def permute(value, target):
        pairs = [
            (a * count_b + b, target(a, b)[0] * count_b + target(a, b)[1])
            for a in range(count_a)
            for b in range(count_b)
        ]
        return lax.ppermute(value, ("aa", "ba"), pairs)

    flat = alignment_state.reshape(seqs * res, channels)
    tail = -(-seqs // 16) * 16
    rows, factors = call(
        functools.partial(factor_kernel, seqs, res),
        (
            shape((seqs * res + tail, channels), BF16),
            shape((seqs, 2 * span + LANES), BF16),
        ),
        [pltpu.VMEM((2, seqs * res, LANES), F32)],
    )(flat, alignment_mask, left_weight, right_weight)

    blocks = [factors] + [
        permute(factors, lambda a, b, k=k: (a, b ^ k)) for k in range(1, count_b)
    ]
    picked = call(
        functools.partial(pick_kernel, count_a, count_b, span),
        tuple(shape((seqs, 2 * span + 2 * LANES), BF16) for _ in range(count_a)),
        [pltpu.VMEM((count_b, seqs, 2 * span + LANES), BF16)],
    )(*blocks)
    msgs = [picked[0]] + [
        permute(picked[k], lambda a, b, k=k: (a ^ k, b)) for k in range(1, count_a)
    ]
    all_rows = [rows] + [permute(rows, lambda a, b, k=k: (a, b ^ k)) for k in range(1, count_b)]

    seq_total = seqs * count_a
    pair_output, bias = call(
        functools.partial(pair_kernel, count_a, res, width),
        (shape(pair_state.shape, BF16), shape((res, heads * res), F32)),
        [
            pltpu.VMEM((pl.cdiv(seq_total, LANES), span, LANES), F32),
            pltpu.VMEM(outer_output_weight.shape, F32),
            pltpu.VMEM(outer_output_weight.shape, BF16),
            pltpu.VMEM((res * res, width * width), BF16),
        ],
    )(*msgs, pair_state, outer_output_weight, pair_bias_weight)

    biases = [permute(bias, lambda a, b, k=k: (b ^ k, a)) for k in range(count_b)]
    keys = res * count_b
    (out,) = call(
        functools.partial(attention_kernel, seqs, res, heads, count_b),
        (shape((seqs * res, channels), BF16),),
        [
            pltpu.VMEM((keys, heads * res), F32),
            pltpu.VMEM((seqs, keys, 2 * channels), BF16),
            pltpu.VMEM((seqs * res, channels), F32),
        ],
    )(
        *all_rows,
        *biases,
        flat,
        query_weight,
        key_weight,
        value_weight,
        gate_weight,
        output_weight,
        up_weight,
        down_weight,
    )
    return (out.reshape(seqs, res, channels), pair_output)


def solution(mesh):
    return jax.shard_map(
        functools.partial(per_device, mesh.shape["aa"], mesh.shape["ba"]),
        mesh=mesh,
        in_specs=(
            P(("groups", "aa"), "ba", None),
            P(("groups", "aa"), "ba", None),
            P(("groups", "aa"), "ba"),
        )
        + (P(),) * 11,
        out_specs=(P(("groups", "aa"), "ba", None), P(("groups", "aa"), "ba", None)),
        check_vma=False,
    )
```

time: 189 us -> 56.7 us (0.30); the launches traced: 187 us -> 56.3 us
  blocking collectives: 65.3 us -> 0 us
  local copies, waits for them, and re-layouts: 42 us -> 6.06 us
  waiting for transfers between devices: 39.3 us -> 14.1 us
  starting transfers between devices: 0.08 us -> 17.8 us
  Pallas kernels: 0 us -> 17.6 us
  matrix products: 14 us -> 0 us
  between operations: 14.5 us -> 0.72 us
  other arithmetic: 8.53 us -> 0 us
  loops' own time: 2.9 us -> 0 us
    all_gather x6 -> x0, blocking collectives: 59.5 us -> none  [the longest x1 14.2 us: per_device(): lax.all_gather(left_fac, 'aa', axis=0, tiled=True)]
    psum x2 -> x0, waiting for transfers between devices: 39.3 us -> none  [from_root(): return lax.psum(jnp.where(mine, x, jnp.zeros_like(x)), axis)]
    convert_element_type x13 -> x0, local copies, waits for them, and re-layouts: 29.6 us -> none  [the longest x12 29.1 us: outer_block(): outer_sum.reshape(row_block * residue_count, opm_width * opm_width)]
    ppermute x0 -> x13, starting transfers between devices: none -> 17.8 us  [permute(): return lax.ppermute(value, ('aa', 'ba'), pairs)]
    pallas_call x0 -> x4, Pallas kernels: none -> 17.6 us  [the longest x1 8.5 us: per_device(): call(functools.partial(pair_kernel, count_a, res, width), (shape(pair_sta...]
    ppermute x0 -> x13, waiting for transfers between devices: none -> 14.1 us  [permute(): return lax.ppermute(value, ('aa', 'ba'), pairs)]
    dot_general x18 -> x0, matrix products: 14 us -> none  [the longest x4 4.69 us: outer_block(): lax.dot_general(left_part, right_flat, (((0,), (0,)), ((), ())), preferre...]
    psum x1 -> x0, blocking collectives: 5.78 us -> none  [from_root(): return lax.psum(jnp.where(mine, x, jnp.zeros_like(x)), axis)]
  transfers between devices with their start and end apart: 2 -> 13, of which waited for: 1 -> 7; matrix products, arithmetic and copies ran while one was open for 3% -> 1% of each run, Pallas kernels for 0% -> 15%
where the time goes in v1:
time: 56.7 us; the launch traced here: 56.3 us
  starting transfers between devices  17.8 us (31%)
  Pallas kernels  17.6 us (31%)
  waiting for transfers between devices  14.1 us (25%)
  local copies, waits for them, and re-layouts  6.06 us (11%)
  between operations  0.72 us (1%)
    ppermute x13, starting transfers between devices, permute(): return lax.ppermute(value, ('aa', 'ba'), pairs)  17.8 us
    ppermute x13, waiting for transfers between devices, permute(): return lax.ppermute(value, ('aa', 'ba'), pairs)  14.1 us
    pallas_call x1, Pallas kernels, per_device(): call(functools.partial(pair_kernel, count_a, res, width), (shape(pair_sta...  8.5 us
    unnamed x35, local copies, waits for them, and re-layouts  6.06 us
    pallas_call x1, Pallas kernels, per_device(): call(functools.partial(attention_kernel, seqs, res, heads, count_b), (sha...  5.57 us
    pallas_call x1, Pallas kernels, per_device(): call(functools.partial(factor_kernel, seqs, res), (shape((seqs * res + ta...  2.07 us
    pallas_call x1, Pallas kernels, per_device(): call(functools.partial(pick_kernel, count_a, count_b, span), tuple((shape...  1.49 us
  transfers between devices with their start and end apart: 13, of which 7 were waited for; matrix products, arithmetic and copies ran while one was open for 1% of the time, Pallas kernels for 15%

profile of v1, /device:TPU:6, one launch (start us, length us, event | category | flops | bytes accessed | tf_op | source)
XLA Modules:
  0.0 56.3 jit_solution(17556606469069790330)
XLA Ops:
  0.6 0.0 copy-start.14
  0.6 1.5 %copy.16.wl_ref = bf16[256,32]{1,0:T(8,128)(2,1)} copy(bf16[256,32]{0,1:T(8,128)(2,1)} %param.17) | data formatting | bytes 32768 | tf_op args[3]
  2.1 0.0 copy-done.14
  2.1 0.7 %copy.17.wr_ref = bf16[256,32]{1,0:T(8,128)(2,1)} copy(bf16[256,32]{0,1:T(8,128)(2,1)S(1)} %copy-done.14) | data formatting | bytes 32768 | tf_op args[4]
  2.8 2.1 %shard_map.149 = (bf16[272,256]{1,0:T(8,128)(2,1)}, bf16[8,2176]{1,0:T(8,128)(2,1)}) custom-call(bf16[256,256]{1,0:T(8,128)(2,1)} %bitcast.2, s32[8,32]{1,0:T(8,128)} %mask_ref.1, bf16[256,32]{1,0:T(8,128)(2,1)} %copy.16.wl_ref, bf16[256,32]{1,0:T(8,128)(2,1)} %copy.17.wr_ref), custom_call_target="tpu_custom_call" | custom-call | tf_op jit(solution)/shard_map/pallas_call | solution.py:258
  4.9 0.0 copy-start
  4.9 0.0 collective-permute-start.5
  4.9 1.5 %collective-permute-start.4 = (bf16[8,2176]{1,0:T(8,128)(2,1)}, bf16[8,2176]{1,0:T(8,128)(2,1)S(1)}, u32[]{:S(2)}, u32[]{:S(2)}) collective-permute-start(bf16[8,2176]{1,0:T(8,128)(2,1)} %get-tuple-element.11.refs_0_), channel_id=1, source_target_pairs={{0,2},{1,3},{2,0},{3,1},{4,6},{5,7},{6,4},{7,5},{8,10},{9,11},{10,... | collective-permute-start | bytes 104456 | tf_op jit(solution)/shard_map/ppermute | solution.py:254
  6.4 0.4 collective-permute-start.3
  6.8 2.1 %collective-permute-done.5.refs_3_ = bf16[8,2176]{1,0:T(8,128)(2,1)S(1)} collective-permute-done((bf16[8,2176]{1,0:T(8,128)(2,1)}, bf16[8,2176]{1,0:T(8,128)(2,1)S(1)}, u32[]{:S(2)}, u32[]{:S(2)}) %collective-permute-start.5) | collective-permute-done | bytes 34848 | tf_op jit(solution)/shard_map/ppermute | solution.py:254
  8.8 0.0 copy-start.7
  8.8 0.8 %collective-permute-done.4.refs_2_ = bf16[8,2176]{1,0:T(8,128)(2,1)S(1)} collective-permute-done((bf16[8,2176]{1,0:T(8,128)(2,1)}, bf16[8,2176]{1,0:T(8,128)(2,1)S(1)}, u32[]{:S(2)}, u32[]{:S(2)}) %collective-permute-start.4) | collective-permute-done | bytes 34848 | tf_op jit(solution)/shard_map/ppermute | solution.py:254
  9.6 0.0 copy-start.8
  9.6 0.0 collective-permute-done.3.refs_1_
  9.6 0.0 copy-done.7
  9.6 0.6 %copy-done.8 = bf16[8,2176]{1,0:T(8,128)(2,1)} copy-done((bf16[8,2176]{1,0:T(8,128)(2,1)}, bf16[8,2176]{1,0:T(8,128)(2,1)S(1)}, u32[]{:S(2)}) %copy-start.8) | copy-done | bytes 34840
  10.2 0.0 copy-start.9
  10.2 0.6 %copy-done.9 = bf16[8,2176]{1,0:T(8,128)(2,1)} copy-done((bf16[8,2176]{1,0:T(8,128)(2,1)}, bf16[8,2176]{1,0:T(8,128)(2,1)S(1)}, u32[]{:S(2)}) %copy-start.9) | copy-done | bytes 34840
  10.8 1.5 %shard_map.150 = (bf16[8,2304]{1,0:T(8,128)(2,1)}, bf16[8,2304]{1,0:T(8,128)(2,1)}, bf16[8,2304]{1,0:T(8,128)(2,1)}, bf16[8,2304]{1,0:T(8,128)(2,1)}) custom-call(bf16[8,2176]{1,0:T(8,128)(2,1)} %get-tuple-element.11.refs_0_, bf16[8,2176]{1,0:T(8,128)(2,1)} %copy-done.9, bf16[8,2176]{1,0:T(8,128)(2,1)} %copy-done.8, bf16[8,2176]{1,0:T(8,128)(2,1)} %copy-done.7), custom_call_target="tpu_custom_call" | custom-call | tf_op jit(solution)/shard_map/pallas_call | solution.py:270
  12.3 1.6 %collective-permute-start.6 = (bf16[8,2304]{1,0:T(8,128)(2,1)}, bf16[8,2304]{1,0:T(8,128)(2,1)S(1)}, u32[]{:S(2)}, u32[]{:S(2)}) collective-permute-start(bf16[8,2304]{1,0:T(8,128)(2,1)} %get-tuple-element.13), channel_id=1, source_target_pairs={{0,4},{1,5},{2,6},{3,7},{4,0},{5,1},{6,2},{7,3},{8,12},{9,13},{10,... | collective-permute-start | bytes 110600 | tf_op jit(solution)/shard_map/ppermute | solution.py:254
  13.9 0.0 copy-done
  13.9 0.0 copy-start.15
  13.9 0.1 collective-permute-start.2
  14.0 1.3 %collective-permute-start.1 = (bf16[272,256]{1,0:T(8,128)(2,1)S(1)}, bf16[272,256]{1,0:T(8,128)(2,1)S(1)}, u32[]{:S(2)}, u32[]{:S(2)}) collective-permute-start(bf16[272,256]{1,0:T(8,128)(2,1)S(1)} %copy-done), channel_id=1, source_target_pairs={{0,2},{1,3},{2,0},{3,1},{4,6},{5,7},{6,4},{7,5},{8,10},{9,11},{10,... | collective-permute-start | bytes 417800 | tf_op jit(solution)/shard_map/ppermute | solution.py:254
  15.3 0.4 collective-permute-start
  15.8 2.6 %collective-permute-start.7 = (bf16[8,2304]{1,0:T(8,128)(2,1)}, bf16[8,2304]{1,0:T(8,128)(2,1)S(1)}, u32[]{:S(2)}, u32[]{:S(2)}) collective-permute-start(bf16[8,2304]{1,0:T(8,128)(2,1)} %get-tuple-element.14), channel_id=1, source_target_pairs={{0,8},{1,9},{2,10},{3,11},{4,12},{5,13},{6,14},{7,15},{8,0},{9,1},... | collective-permute-start | bytes 110600 | tf_op jit(solution)/shard_map/ppermute | solution.py:254
  18.3 0.0 collective-permute-done.6.refs_1_
  18.3 0.0 copy-start.4
  18.3 1.7 %collective-permute-start.8 = (bf16[8,2304]{1,0:T(8,128)(2,1)}, bf16[8,2304]{1,0:T(8,128)(2,1)S(1)}, u32[]{:S(2)}, u32[]{:S(2)}) collective-permute-start(bf16[8,2304]{1,0:T(8,128)(2,1)} %get-tuple-element.15), channel_id=1, source_target_pairs={{0,12},{1,13},{2,14},{3,15},{4,8},{5,9},{6,10},{7,11},{8,4},{9,5},... | collective-permute-start | bytes 110600 | tf_op jit(solution)/shard_map/ppermute | solution.py:254
  20.1 0.0 copy-done.15
  20.1 0.7 %copy.18.refs_6_ = bf16[128,8]{1,0:T(8,128)(2,1)} copy(bf16[128,8]{0,1:T(8,128)(2,1)S(1)} %copy-done.15) | data formatting | bytes 4096 | tf_op args[6]
  20.8 0.6 %collective-permute-done.7.refs_2_ = bf16[8,2304]{1,0:T(8,128)(2,1)S(1)} collective-permute-done((bf16[8,2304]{1,0:T(8,128)(2,1)}, bf16[8,2304]{1,0:T(8,128)(2,1)S(1)}, u32[]{:S(2)}, u32[]{:S(2)}) %collective-permute-start.7) | collective-permute-done | bytes 36896 | tf_op jit(solution)/shard_map/ppermute | solution.py:254
  21.3 0.0 copy-start.5
  21.4 3.0 %collective-permute-done.8.refs_3_ = bf16[8,2304]{1,0:T(8,128)(2,1)S(1)} collective-permute-done((bf16[8,2304]{1,0:T(8,128)(2,1)}, bf16[8,2304]{1,0:T(8,128)(2,1)S(1)}, u32[]{:S(2)}, u32[]{:S(2)}) %collective-permute-start.8) | collective-permute-done | bytes 36896 | tf_op jit(solution)/shard_map/ppermute | solution.py:254
  24.3 0.0 copy-start.6
  24.3 0.0 copy-done.4
  24.3 0.0 copy-done.5
  24.3 0.6 %copy-done.6 = bf16[8,2304]{1,0:T(8,128)(2,1)} copy-done((bf16[8,2304]{1,0:T(8,128)(2,1)}, bf16[8,2304]{1,0:T(8,128)(2,1)S(1)}, u32[]{:S(2)}) %copy-start.6) | copy-done | bytes 36888
  24.9 8.5 %shard_map.151 = (bf16[32,32,128]{2,1,0:T(8,128)(2,1)}, f32[32,256]{1,0:T(8,128)}) custom-call(bf16[8,2304]{1,0:T(8,128)(2,1)} %get-tuple-element.12.refs_0_, bf16[8,2304]{1,0:T(8,128)(2,1)} %copy-done.4, bf16[8,2304]{1,0:T(8,128)(2,1)} %copy-done.5, bf16[8,2304]{1,0:T(8,128)(2,1)} %copy-done.6, bf16[32,32,128]{2,1,0:T(8,128)(2,1)} %refs_4_.1, ...), custom_call_target="tpu_custom_call" | custom-call | tf_op jit(solution)/shard_map/pallas_call | solution.py:281
  33.4 0.0 collective-permute-start.12
  33.4 2.7 %collective-permute-start.11 = (f32[32,256]{1,0:T(8,128)}, f32[32,256]{1,0:T(8,128)S(1)}, u32[]{:S(2)}, u32[]{:S(2)}) collective-permute-start(f32[32,256]{1,0:T(8,128)} %get-tuple-element.16), channel_id=1, source_target_pairs={{0,8},{1,12},{2,0},{3,4},{4,9},{5,13},{6,1},{7,5},{8,10},{9,14},{1... | collective-permute-start | bytes 98312 | tf_op jit(solution)/shard_map/ppermute | solution.py:254
  36.2 1.9 %collective-permute-done.12.refs_7_ = f32[32,256]{1,0:T(8,128)S(1)} collective-permute-done((f32[32,256]{1,0:T(8,128)}, f32[32,256]{1,0:T(8,128)S(1)}, u32[]{:S(2)}, u32[]{:S(2)}) %collective-permute-start.12) | collective-permute-done | bytes 32800 | tf_op jit(solution)/shard_map/ppermute | solution.py:254
  38.1 0.0 copy-start.10
  38.1 3.4 %collective-permute-start.10 = (f32[32,256]{1,0:T(8,128)}, f32[32,256]{1,0:T(8,128)S(1)}, u32[]{:S(2)}, u32[]{:S(2)}) collective-permute-start(f32[32,256]{1,0:T(8,128)} %get-tuple-element.16), channel_id=1, source_target_pairs={{0,4},{1,0},{2,12},{3,8},{4,5},{5,1},{6,13},{7,9},{8,6},{9,2},{10,... | collective-permute-start | bytes 98312 | tf_op jit(solution)/shard_map/ppermute | solution.py:254
  41.5 0.0 collective-permute-done.11.refs_6_
  41.5 0.0 copy-start.11
  41.5 2.0 %collective-permute-start.9 = (f32[32,256]{1,0:T(8,128)}, f32[32,256]{1,0:T(8,128)S(1)}, u32[]{:S(2)}, u32[]{:S(2)}) collective-permute-start(f32[32,256]{1,0:T(8,128)} %get-tuple-element.16), channel_id=1, source_target_pairs={{0,0},{1,4},{2,8},{3,12},{4,1},{5,5},{6,9},{7,13},{8,2},{9,6},{10,... | collective-permute-start | bytes 98312 | tf_op jit(solution)/shard_map/ppermute | solution.py:254
  43.6 0.3 collective-permute-done.10.refs_5_
  43.9 0.0 copy-start.12
  43.9 5.5 %collective-permute-done.9.refs_4_ = f32[32,256]{1,0:T(8,128)S(1)} collective-permute-done((f32[32,256]{1,0:T(8,128)}, f32[32,256]{1,0:T(8,128)S(1)}, u32[]{:S(2)}, u32[]{:S(2)}) %collective-permute-start.9) | collective-permute-done | bytes 32800 | tf_op jit(solution)/shard_map/ppermute | solution.py:254
  49.3 0.0 copy-start.13
  49.3 0.0 collective-permute-done.2.refs_3_
  49.3 0.0 collective-permute-done.1.refs_2_
  49.4 0.0 copy-start.2
  49.4 0.0 collective-permute-done.refs_1_
  49.4 0.0 copy-done.10
  49.4 0.0 copy-done.11
  49.4 0.0 copy-done.12
  49.4 0.5 copy-done.13
  49.9 0.1 copy-done.1
  50.0 0.0 copy-done.2
  50.1 0.0 copy-start.3
  50.1 0.7 %copy-done.3 = bf16[272,256]{1,0:T(8,128)(2,1)} copy-done((bf16[272,256]{1,0:T(8,128)(2,1)}, bf16[272,256]{1,0:T(8,128)(2,1)S(1)}, u32[]{:S(2)}) %copy-start.3) | copy-done | bytes 139288
  50.7 5.6 %shard_map.152 = bf16[256,256]{1,0:T(8,128)(2,1)} custom-call(bf16[272,256]{1,0:T(8,128)(2,1)} %get-tuple-element.10.refs_0_, bf16[272,256]{1,0:T(8,128)(2,1)} %copy-done.3, bf16[272,256]{1,0:T(8,128)(2,1)} %copy-done.2, bf16[272,256]{1,0:T(8,128)(2,1)} %copy-done.1, f32[32,256]{1,0:T(8,128)} %copy-done.13, f32[32,256]{1,0:T(8,128)} %copy-done.12, ...), custom_call_target="tpu_custom_call" | custom-call | tf_op jit(solution)/shard_map/pallas_call | solution.py:294
  (1 shorter events, 0.0 us)
Async XLA Ops:
  0.6 1.5 %copy-start.14 = (bf16[256,32]{0,1:T(8,128)(2,1)S(1)}, bf16[256,32]{0,1:T(8,128)(2,1)}, u32[]{:S(2)}) copy-start(bf16[256,32]{0,1:T(8,128)(2,1)} %param.18) | copy-start | bytes 49156
  4.9 9.0 %copy-start = (bf16[272,256]{1,0:T(8,128)(2,1)S(1)}, bf16[272,256]{1,0:T(8,128)(2,1)}, u32[]{:S(2)}) copy-start(bf16[272,256]{1,0:T(8,128)(2,1)} %get-tuple-element.10.refs_0_) | copy-start | bytes 417796
  4.9 3.9 %collective-permute-start.5 = (bf16[8,2176]{1,0:T(8,128)(2,1)}, bf16[8,2176]{1,0:T(8,128)(2,1)S(1)}, u32[]{:S(2)}, u32[]{:S(2)}) collective-permute-start(bf16[8,2176]{1,0:T(8,128)(2,1)} %get-tuple-element.11.refs_0_), channel_id=1, source_target_pairs={{0,3},{1,2},{2,1},{3,0},{4,7},{5,6},{6,5},{7,4},{8,11},{9,10},{10,... | collective-permute-start | bytes 104456 | tf_op jit(solution)/shard_map/ppermute | solution.py:254
  4.9 4.7 %collective-permute-start.4 = (bf16[8,2176]{1,0:T(8,128)(2,1)}, bf16[8,2176]{1,0:T(8,128)(2,1)S(1)}, u32[]{:S(2)}, u32[]{:S(2)}) collective-permute-start(bf16[8,2176]{1,0:T(8,128)(2,1)} %get-tuple-element.11.refs_0_), channel_id=1, source_target_pairs={{0,2},{1,3},{2,0},{3,1},{4,6},{5,7},{6,4},{7,5},{8,10},{9,11},{10,... | collective-permute-start | bytes 104456 | tf_op jit(solution)/shard_map/ppermute | solution.py:254
  6.4 3.2 %collective-permute-start.3 = (bf16[8,2176]{1,0:T(8,128)(2,1)}, bf16[8,2176]{1,0:T(8,128)(2,1)S(1)}, u32[]{:S(2)}, u32[]{:S(2)}) collective-permute-start(bf16[8,2176]{1,0:T(8,128)(2,1)} %get-tuple-element.11.refs_0_), channel_id=1, source_target_pairs={{0,1},{1,0},{2,3},{3,2},{4,5},{5,4},{6,7},{7,6},{8,9},{9,8},{10,11... | collective-permute-start | bytes 104456 | tf_op jit(solution)/shard_map/ppermute | solution.py:254
  8.8 0.8 %copy-start.7 = (bf16[8,2176]{1,0:T(8,128)(2,1)}, bf16[8,2176]{1,0:T(8,128)(2,1)S(1)}, u32[]{:S(2)}) copy-start(bf16[8,2176]{1,0:T(8,128)(2,1)S(1)} %collective-permute-done.5.refs_3_) | copy-start | bytes 104452
  9.6 0.6 %copy-start.8 = (bf16[8,2176]{1,0:T(8,128)(2,1)}, bf16[8,2176]{1,0:T(8,128)(2,1)S(1)}, u32[]{:S(2)}) copy-start(bf16[8,2176]{1,0:T(8,128)(2,1)S(1)} %collective-permute-done.4.refs_2_) | copy-start | bytes 104452
  10.2 0.6 %copy-start.9 = (bf16[8,2176]{1,0:T(8,128)(2,1)}, bf16[8,2176]{1,0:T(8,128)(2,1)S(1)}, u32[]{:S(2)}) copy-start(bf16[8,2176]{1,0:T(8,128)(2,1)S(1)} %collective-permute-done.3.refs_1_) | copy-start | bytes 104452
  12.3 6.0 %collective-permute-start.6 = (bf16[8,2304]{1,0:T(8,128)(2,1)}, bf16[8,2304]{1,0:T(8,128)(2,1)S(1)}, u32[]{:S(2)}, u32[]{:S(2)}) collective-permute-start(bf16[8,2304]{1,0:T(8,128)(2,1)} %get-tuple-element.13), channel_id=1, source_target_pairs={{0,4},{1,5},{2,6},{3,7},{4,0},{5,1},{6,2},{7,3},{8,12},{9,13},{10,... | collective-permute-start | bytes 110600 | tf_op jit(solution)/shard_map/ppermute | solution.py:254
  13.9 6.2 %copy-start.15 = (bf16[128,8]{0,1:T(8,128)(2,1)S(1)}, bf16[128,8]{0,1:T(8,128)(2,1)}, u32[]{:S(2)}) copy-start(bf16[128,8]{0,1:T(8,128)(2,1)} %param.20) | copy-start | bytes 6148
  13.9 35.5 %collective-permute-start.2 = (bf16[272,256]{1,0:T(8,128)(2,1)S(1)}, bf16[272,256]{1,0:T(8,128)(2,1)S(1)}, u32[]{:S(2)}, u32[]{:S(2)}) collective-permute-start(bf16[272,256]{1,0:T(8,128)(2,1)S(1)} %copy-done), channel_id=1, source_target_pairs={{0,3},{1,2},{2,1},{3,0},{4,7},{5,6},{6,5},{7,4},{8,11},{9,10},{10,... | collective-permute-start | bytes 417800 | tf_op jit(solution)/shard_map/ppermute | solution.py:254
  14.0 35.3 %collective-permute-start.1 = (bf16[272,256]{1,0:T(8,128)(2,1)S(1)}, bf16[272,256]{1,0:T(8,128)(2,1)S(1)}, u32[]{:S(2)}, u32[]{:S(2)}) collective-permute-start(bf16[272,256]{1,0:T(8,128)(2,1)S(1)} %copy-done), channel_id=1, source_target_pairs={{0,2},{1,3},{2,0},{3,1},{4,6},{5,7},{6,4},{7,5},{8,10},{9,11},{10,... | collective-permute-start | bytes 417800 | tf_op jit(solution)/shard_map/ppermute | solution.py:254
  15.3 34.0 %collective-permute-start = (bf16[272,256]{1,0:T(8,128)(2,1)S(1)}, bf16[272,256]{1,0:T(8,128)(2,1)S(1)}, u32[]{:S(2)}, u32[]{:S(2)}) collective-permute-start(bf16[272,256]{1,0:T(8,128)(2,1)S(1)} %copy-done), channel_id=1, source_target_pairs={{0,1},{1,0},{2,3},{3,2},{4,5},{5,4},{6,7},{7,6},{8,9},{9,8},{10,11... | collective-permute-start | bytes 417800 | tf_op jit(solution)/shard_map/ppermute | solution.py:254
  15.8 5.6 %collective-permute-start.7 = (bf16[8,2304]{1,0:T(8,128)(2,1)}, bf16[8,2304]{1,0:T(8,128)(2,1)S(1)}, u32[]{:S(2)}, u32[]{:S(2)}) collective-permute-start(bf16[8,2304]{1,0:T(8,128)(2,1)} %get-tuple-element.14), channel_id=1, source_target_pairs={{0,8},{1,9},{2,10},{3,11},{4,12},{5,13},{6,14},{7,15},{8,0},{9,1},... | collective-permute-start | bytes 110600 | tf_op jit(solution)/shard_map/ppermute | solution.py:254
  18.3 6.0 %copy-start.4 = (bf16[8,2304]{1,0:T(8,128)(2,1)}, bf16[8,2304]{1,0:T(8,128)(2,1)S(1)}, u32[]{:S(2)}) copy-start(bf16[8,2304]{1,0:T(8,128)(2,1)S(1)} %collective-permute-done.6.refs_1_) | copy-start | bytes 110596
  18.3 6.0 %collective-permute-start.8 = (bf16[8,2304]{1,0:T(8,128)(2,1)}, bf16[8,2304]{1,0:T(8,128)(2,1)S(1)}, u32[]{:S(2)}, u32[]{:S(2)}) collective-permute-start(bf16[8,2304]{1,0:T(8,128)(2,1)} %get-tuple-element.15), channel_id=1, source_target_pairs={{0,12},{1,13},{2,14},{3,15},{4,8},{5,9},{6,10},{7,11},{8,4},{9,5},... | collective-permute-start | bytes 110600 | tf_op jit(solution)/shard_map/ppermute | solution.py:254
  21.3 3.0 %copy-start.5 = (bf16[8,2304]{1,0:T(8,128)(2,1)}, bf16[8,2304]{1,0:T(8,128)(2,1)S(1)}, u32[]{:S(2)}) copy-start(bf16[8,2304]{1,0:T(8,128)(2,1)S(1)} %collective-permute-done.7.refs_2_) | copy-start | bytes 110596
  24.3 0.6 %copy-start.6 = (bf16[8,2304]{1,0:T(8,128)(2,1)}, bf16[8,2304]{1,0:T(8,128)(2,1)S(1)}, u32[]{:S(2)}) copy-start(bf16[8,2304]{1,0:T(8,128)(2,1)S(1)} %collective-permute-done.8.refs_3_) | copy-start | bytes 110596
  33.4 4.7 %collective-permute-start.12 = (f32[32,256]{1,0:T(8,128)}, f32[32,256]{1,0:T(8,128)S(1)}, u32[]{:S(2)}, u32[]{:S(2)}) collective-permute-start(f32[32,256]{1,0:T(8,128)} %get-tuple-element.16), channel_id=1, source_target_pairs={{0,12},{1,8},{2,4},{3,0},{4,13},{5,9},{6,5},{7,1},{8,14},{9,10},{1... | collective-permute-start | bytes 98312 | tf_op jit(solution)/shard_map/ppermute | solution.py:254
  33.4 8.1 %collective-permute-start.11 = (f32[32,256]{1,0:T(8,128)}, f32[32,256]{1,0:T(8,128)S(1)}, u32[]{:S(2)}, u32[]{:S(2)}) collective-permute-start(f32[32,256]{1,0:T(8,128)} %get-tuple-element.16), channel_id=1, source_target_pairs={{0,8},{1,12},{2,0},{3,4},{4,9},{5,13},{6,1},{7,5},{8,10},{9,14},{1... | collective-permute-start | bytes 98312 | tf_op jit(solution)/shard_map/ppermute | solution.py:254
  38.1 11.3 %copy-start.10 = (f32[32,256]{1,0:T(8,128)}, f32[32,256]{1,0:T(8,128)S(1)}, u32[]{:S(2)}) copy-start(f32[32,256]{1,0:T(8,128)S(1)} %collective-permute-done.12.refs_7_) | copy-start | bytes 98308
  38.1 5.8 %collective-permute-start.10 = (f32[32,256]{1,0:T(8,128)}, f32[32,256]{1,0:T(8,128)S(1)}, u32[]{:S(2)}, u32[]{:S(2)}) collective-permute-start(f32[32,256]{1,0:T(8,128)} %get-tuple-element.16), channel_id=1, source_target_pairs={{0,4},{1,0},{2,12},{3,8},{4,5},{5,1},{6,13},{7,9},{8,6},{9,2},{10,... | collective-permute-start | bytes 98312 | tf_op jit(solution)/shard_map/ppermute | solution.py:254
  41.5 7.9 %copy-start.11 = (f32[32,256]{1,0:T(8,128)}, f32[32,256]{1,0:T(8,128)S(1)}, u32[]{:S(2)}) copy-start(f32[32,256]{1,0:T(8,128)S(1)} %collective-permute-done.11.refs_6_) | copy-start | bytes 98308
  41.5 7.8 %collective-permute-start.9 = (f32[32,256]{1,0:T(8,128)}, f32[32,256]{1,0:T(8,128)S(1)}, u32[]{:S(2)}, u32[]{:S(2)}) collective-permute-start(f32[32,256]{1,0:T(8,128)} %get-tuple-element.16), channel_id=1, source_target_pairs={{0,0},{1,4},{2,8},{3,12},{4,1},{5,5},{6,9},{7,13},{8,2},{9,6},{10,... | collective-permute-start | bytes 98312 | tf_op jit(solution)/shard_map/ppermute | solution.py:254
  43.9 5.5 %copy-start.12 = (f32[32,256]{1,0:T(8,128)}, f32[32,256]{1,0:T(8,128)S(1)}, u32[]{:S(2)}) copy-start(f32[32,256]{1,0:T(8,128)S(1)} %collective-permute-done.10.refs_5_) | copy-start | bytes 98308
  49.3 0.6 %copy-start.13 = (f32[32,256]{1,0:T(8,128)}, f32[32,256]{1,0:T(8,128)S(1)}, u32[]{:S(2)}) copy-start(f32[32,256]{1,0:T(8,128)S(1)} %collective-permute-done.9.refs_4_) | copy-start | bytes 98308
  49.3 0.7 %copy-start.1 = (bf16[272,256]{1,0:T(8,128)(2,1)}, bf16[272,256]{1,0:T(8,128)(2,1)S(1)}, u32[]{:S(2)}) copy-start(bf16[272,256]{1,0:T(8,128)(2,1)S(1)} %collective-permute-done.2.refs_3_) | copy-start | bytes 417796
  49.4 0.7 %copy-start.2 = (bf16[272,256]{1,0:T(8,128)(2,1)}, bf16[272,256]{1,0:T(8,128)(2,1)S(1)}, u32[]{:S(2)}) copy-start(bf16[272,256]{1,0:T(8,128)(2,1)S(1)} %collective-permute-done.1.refs_2_) | copy-start | bytes 417796
  50.1 0.7 %copy-start.3 = (bf16[272,256]{1,0:T(8,128)(2,1)}, bf16[272,256]{1,0:T(8,128)(2,1)S(1)}, u32[]{:S(2)}) copy-start(bf16[272,256]{1,0:T(8,128)(2,1)S(1)} %collective-permute-done.refs_1_) | copy-start | bytes 417796

commit v2 on v1

--- a/solution.py
+++ b/solution.py
@@ -7,11 +7,12 @@
 from jax.experimental.pallas import tpu as pltpu
 from jax.sharding import PartitionSpec as P
 
+
 F32 = jnp.float32
 BF16 = jnp.bfloat16
 LANES = 128
 EPS = 1e-05
-VMEM_LIMIT = 56 * 1024 * 1024
+MIB = 1024 * 1024
 
 
 def layer_norm(values):
@@ -40,22 +41,36 @@
     return lax.dot_general(x, y, (((1,), (1,)), ((), ())), preferred_element_type=F32)
 
 
-def factor_kernel(seqs, res, x_ref, mask_ref, wl_ref, wr_ref, rows_ref, fac_ref, y_scr):
-    width = wl_ref.shape[1]
+def fetch(sources, buffers, sems):
+    copies = [pltpu.make_async_copy(s, b, sems.at[n]) for n, (s, b) in enumerate(zip(sources, buffers))]
+    for copy in copies:
+        copy.start()
+
+    def ready(n):
+        def get():
+            copies[n].wait()
+            return buffers[n][...]
+
+        return get
+
+    return [ready(n) for n in range(len(copies))]
+
+
+def factor_kernel(seqs, res, *refs):
+    sources, (rows_ref, fac_ref, y_scr, *buffers, sems) = refs[:4], refs[4:]
+    get_x, get_left, get_right, get_mask = fetch(sources, buffers, sems)
+    width = sources[1].shape[0]
     per = LANES // width
-    normed = layer_norm(x_ref[...].astype(F32)).astype(BF16)
-    keep = (mask_ref[...] > 0).astype(F32).astype(BF16)
+    normed = layer_norm(get_x().astype(F32)).astype(BF16)
+    keep = (get_mask() > 0).astype(F32).astype(BF16)
     rows_ref[: seqs * res, :] = normed
     tail = rows_ref.shape[0] - seqs * res
     keep_wide = dot(keep, spread_matrix(res, rows_ref.shape[1], lambda c: c))
     rows_ref[seqs * res :, :] = jnp.concatenate(
         [keep_wide, jnp.zeros((tail - seqs, rows_ref.shape[1]), F32)], axis=0
     ).astype(BF16)
-    repeat = spread_matrix(width, LANES, lambda c: c % width)
-    w_left = dot(wl_ref[...], repeat).astype(BF16)
-    w_right = dot(wr_ref[...], repeat).astype(BF16)
-    y_scr[0] = dot(normed, w_left)
-    y_scr[1] = dot(normed, w_right)
+    y_scr[0] = dot_nt(normed, jnp.concatenate([get_left()] * per, axis=0))
+    y_scr[1] = dot_nt(normed, jnp.concatenate([get_right()] * per, axis=0))
     keep_rep = dot(keep, spread_matrix(res, res * width, lambda c: c // width))
     segment = iota((seqs, LANES), 1) // width
     span = res * width
@@ -86,9 +101,20 @@
         outs[k][:, 2 * span + LANES :] = own[:, 2 * span :]
 
 
+def spread_kernel(count_a, count_b, *refs):
+    ins, outs, scr = refs[:count_a], refs[count_a : count_a + count_b], refs[-1]
+    row, col = lax.axis_index("aa"), lax.axis_index("ba")
+    for k in range(count_a):
+        scr[lax.bitwise_xor(row, k)] = ins[k][...]
+    for k in range(count_b):
+        outs[k][...] = scr[lax.bitwise_xor(col, k)]
+
+
 def pair_kernel(count_a, res, width, *refs):
     msgs = refs[:count_a]
-    pair_ref, wout_ref, wbias_ref, out_ref, bias_ref, rt_scr, wf_scr, wp_scr, a_scr = refs[count_a:]
+    sources, (out_ref, bias_ref) = refs[count_a : count_a + 3], refs[count_a + 3 : count_a + 5]
+    rt_scr, wf_scr, wp_scr, a_scr, *buffers, sems = refs[count_a + 5 :]
+    get_wout, get_wbias, get_pair = fetch(sources, buffers, sems)
     span = res * width
     per = LANES // width
     msg = jnp.concatenate([m[...].astype(F32) for m in msgs], axis=0)
@@ -99,9 +125,6 @@
     for t in range(rt_scr.shape[0]):
         rows = msg[t * LANES : (t + 1) * LANES, span : 2 * span].T
         rt_scr[t, :, : rows.shape[1]] = rows
-    wf_scr[...] = wout_ref[...].astype(F32)
-    for d in range(width):
-        wp_scr[d * width : (d + 1) * width, :] = wf_scr[pl.ds(d, width, stride=width), :].astype(BF16)
     lane = iota((res, LANES), 1)
     segment = lane // width
     for block in range(width // per):
@@ -135,10 +158,14 @@
             for k in range(per):
                 i = group * per + k
                 a_scr[i * res : (i + 1) * res, block * LANES : (block + 1) * LANES] = tiles[k]
+    wf_scr[...] = get_wout().astype(F32)
+    for d in range(width):
+        wp_scr[d * width : (d + 1) * width, :] = wf_scr[pl.ds(d, width, stride=width), :].astype(BF16)
     counts = dot_tn(keep_col, keep_row)
     inverse = 1.0 / counts
-    heads = wbias_ref.shape[1]
-    w_rep = dot(wbias_ref[...], spread_matrix(heads, heads * res, lambda c: c // res)).astype(BF16)
+    heads = sources[1].shape[0]
+    pair = get_pair()
+    w_rep = dot_tn(get_wbias(), spread_matrix(heads, heads * res, lambda c: c // res)).astype(BF16)
     query = iota((res, heads * res), 1) % res
     bias = jnp.zeros((res, heads * res), F32)
     chunk = 8
@@ -146,7 +173,7 @@
         upd = dot(a_scr[start * res : (start + chunk) * res, :], wp_scr[...])
         for i in range(start, start + chunk):
             mine = upd[(i - start) * res : (i - start + 1) * res]
-            total = (pair_ref[i].astype(F32) + mine * inverse[:, i : i + 1]).astype(BF16)
+            total = (pair[i].astype(F32) + mine * inverse[:, i : i + 1]).astype(BF16)
             out_ref[i] = total
             normed = layer_norm(total.astype(F32)).astype(BF16)
             bias = jnp.where(query == i, dot(normed, w_rep), bias)
@@ -155,20 +182,16 @@
 
 def attention_kernel(seqs, res, heads, count_b, *refs):
     rows_refs, bias_refs = refs[:count_b], refs[count_b : 2 * count_b]
-    (x_ref, wq_ref, wk_ref, wv_ref, wg_ref, wo_ref, up_ref, down_ref, out_ref) = refs[
-        2 * count_b : 2 * count_b + 9
-    ]
-    bias_scr, kv_scr, att_scr = refs[2 * count_b + 9 :]
-    row, col = lax.axis_index("aa"), lax.axis_index("ba")
-    channels = wq_ref.shape[1]
+    sources, out_ref = refs[2 * count_b : 2 * count_b + 8], refs[2 * count_b + 8]
+    bias_scr, kv_scr, att_scr, *buffers, sems = refs[2 * count_b + 9 :]
+    get_k, get_v, get_q, get_g, get_o, get_up, get_down, get_x = fetch(sources, buffers, sems)
+    channels = out_ref.shape[1]
     head_width = channels // heads
     wide = heads * res
-    offset = lax.bitwise_xor(row, col)
     for k in range(count_b):
-        at = pl.multiple_of(lax.bitwise_xor(offset, k) * res, res)
-        bias_scr[pl.ds(at, res), :] = bias_refs[k][...]
+        bias_scr[k * res : (k + 1) * res, :] = bias_refs[k][...]
     own = rows_refs[0][: seqs * res, :]
-    w_kv = jnp.concatenate([wk_ref[...], wv_ref[...]], axis=1)
+    w_kv = jnp.concatenate([get_k(), get_v()], axis=1)
     spread = spread_matrix(seqs, seqs * LANES, lambda c: c // LANES)
     keeps = []
     for k in range(count_b):
@@ -176,8 +199,8 @@
         for s in range(seqs):
             kv_scr[s, k * res : (k + 1) * res, :] = kv[s * res : (s + 1) * res]
         keeps.append(dot_tn(rows_refs[k][seqs * res : seqs * res + seqs, :res], spread))
-    query = (dot(own, wq_ref[...]) * (head_width ** (-0.5))).astype(BF16)
-    gate = jax.nn.sigmoid(dot(own, wg_ref[...]))
+    query = (dot(own, get_q()) * (head_width ** (-0.5))).astype(BF16)
+    gate = jax.nn.sigmoid(dot(own, get_g()))
     same_head = iota((wide, channels), 0) // res == iota((wide, channels), 1) // head_width
     lane_head = iota((res, channels), 1) // head_width
     masses = []
@@ -207,18 +230,29 @@
         precision=lax.Precision.HIGHEST,
     )
     gated = (att_scr[...] * inverse * gate).astype(BF16)
-    middle = x_ref[...].astype(F32) + dot(gated, wo_ref[...])
-    hidden = jnp.maximum(dot(layer_norm(middle).astype(BF16), up_ref[...]), 0.0).astype(BF16)
-    out_ref[...] = (middle + dot(hidden, down_ref[...])).astype(BF16)
-
-
-def call(kernel, outs, scratch=()):
+    middle = get_x().astype(F32) + dot(gated, get_o())
+    hidden = jnp.maximum(dot(layer_norm(middle).astype(BF16), get_up()), 0.0).astype(BF16)
+    out_ref[...] = (middle + dot(hidden, get_down())).astype(BF16)
+
+
+def call(kernel, mib, outs, scratch=(), blocks=0, hbm=()):
+    specs = {}
+    if hbm:
+        vmem_spec = pl.BlockSpec(memory_space=pltpu.VMEM)
+        specs["in_specs"] = [vmem_spec] * blocks + [pl.BlockSpec(memory_space=pltpu.HBM)] * len(hbm)
+        scratch = list(scratch) + [pltpu.VMEM(h.shape, h.dtype) for h in hbm]
+        scratch.append(pltpu.SemaphoreType.DMA((len(hbm),)))
     return pl.pallas_call(
         kernel,
         out_shape=outs,
         scratch_shapes=scratch,
-        compiler_params=pltpu.CompilerParams(vmem_limit_bytes=VMEM_LIMIT),
+        **specs,
+        compiler_params=pltpu.CompilerParams(vmem_limit_bytes=mib * MIB),
     )
+
+
+def in_hbm(arrays):
+    return [pltpu.with_memory_space_constraint(x, pltpu.HBM) for x in arrays]
 
 
 def per_device(
@@ -253,33 +287,42 @@
         ]
         return lax.ppermute(value, ("aa", "ba"), pairs)
 
+    def along_a(value, k):
+        return permute(value, lambda a, b: (a ^ k, b))
+
+    def along_b(value, k):
+        return permute(value, lambda a, b: (a, b ^ k))
+
     flat = alignment_state.reshape(seqs * res, channels)
     tail = -(-seqs // 16) * 16
+    inputs = [flat, left_weight.T, right_weight.T, alignment_mask]
     rows, factors = call(
         functools.partial(factor_kernel, seqs, res),
+        4,
         (
             shape((seqs * res + tail, channels), BF16),
             shape((seqs, 2 * span + LANES), BF16),
         ),
         [pltpu.VMEM((2, seqs * res, LANES), F32)],
-    )(flat, alignment_mask, left_weight, right_weight)
-
-    blocks = [factors] + [
-        permute(factors, lambda a, b, k=k: (a, b ^ k)) for k in range(1, count_b)
-    ]
+        0,
+        inputs,
+    )(*in_hbm(inputs))
+
+    blocks = [factors] + [along_b(factors, k) for k in range(1, count_b)]
     picked = call(
         functools.partial(pick_kernel, count_a, count_b, span),
+        4,
         tuple(shape((seqs, 2 * span + 2 * LANES), BF16) for _ in range(count_a)),
         [pltpu.VMEM((count_b, seqs, 2 * span + LANES), BF16)],
     )(*blocks)
-    msgs = [picked[0]] + [
-        permute(picked[k], lambda a, b, k=k: (a ^ k, b)) for k in range(1, count_a)
-    ]
-    all_rows = [rows] + [permute(rows, lambda a, b, k=k: (a, b ^ k)) for k in range(1, count_b)]
+    msgs = [picked[0]] + [along_a(picked[k], k) for k in range(1, count_a)]
+    all_rows = [rows] + [along_b(rows, k) for k in range(1, count_b)]
 
     seq_total = seqs * count_a
+    weights = [outer_output_weight, pair_bias_weight.T, pair_state]
     pair_output, bias = call(
         functools.partial(pair_kernel, count_a, res, width),
+        16,
         (shape(pair_state.shape, BF16), shape((res, heads * res), F32)),
         [
             pltpu.VMEM((pl.cdiv(seq_total, LANES), span, LANES), F32),
@@ -287,36 +330,52 @@
             pltpu.VMEM(outer_output_weight.shape, BF16),
             pltpu.VMEM((res * res, width * width), BF16),
         ],
-    )(*msgs, pair_state, outer_output_weight, pair_bias_weight)
-
-    biases = [permute(bias, lambda a, b, k=k: (b ^ k, a)) for k in range(count_b)]
+        count_a,
+        weights,
+    )(*msgs, *in_hbm(weights))
+
+    tiles = [bias] + [along_a(bias, k) for k in range(1, count_a)]
+    biases = call(
+        functools.partial(spread_kernel, count_a, count_b),
+        4,
+        tuple(shape(bias.shape, F32) for _ in range(count_b)),
+        [pltpu.VMEM((count_a,) + bias.shape, F32)],
+    )(*tiles)
+    biases = [biases[0]] + [along_b(biases[k], k) for k in range(1, count_b)]
     keys = res * count_b
+    weights = [
+        key_weight,
+        value_weight,
+        query_weight,
+        gate_weight,
+        output_weight,
+        up_weight,
+        down_weight,
+        flat,
+    ]
     (out,) = call(
         functools.partial(attention_kernel, seqs, res, heads, count_b),
+        24,
         (shape((seqs * res, channels), BF16),),
         [
             pltpu.VMEM((keys, heads * res), F32),
             pltpu.VMEM((seqs, keys, 2 * channels), BF16),
             pltpu.VMEM((seqs * res, channels), F32),
         ],
-    )(
-        *all_rows,
-        *biases,
-        flat,
-        query_weight,
-        key_weight,
-        value_weight,
-        gate_weight,
-        output_weight,
-        up_weight,
-        down_weight,
-    )
+        2 * count_b,
+        weights,
+    )(*all_rows, *biases, *in_hbm(weights))
     return (out.reshape(seqs, res, channels), pair_output)
 
 
 def solution(mesh):
+    count_a, count_b = mesh.shape["aa"], mesh.shape["ba"]
+
+    def body(*args):
+        return per_device(count_a, count_b, *args)
+
     return jax.shard_map(
-        functools.partial(per_device, mesh.shape["aa"], mesh.shape["ba"]),
+        body,
         mesh=mesh,
         in_specs=(
             P(("groups", "aa"), "ba", None),

time: 56.7 us -> 46.2 us (0.81)
  the two profiles are of different devices: /device:TPU:6 before, /device:TPU:0 now
where the time goes in v2:
time: 46.2 us; the launch traced here: 46.1 us
  waiting for transfers between devices  18.9 us (41%)
  Pallas kernels  14.4 us (31%)
  starting transfers between devices  12.2 us (26%)
  between operations  0.68 us (1%)
    ppermute x15, waiting for transfers between devices, permute(): return lax.ppermute(value, ('aa', 'ba'), pairs)  18.9 us
    ppermute x15, starting transfers between devices, permute(): return lax.ppermute(value, ('aa', 'ba'), pairs)  12.2 us
    pallas_call x1, Pallas kernels, per_device(): call(functools.partial(pair_kernel, count_a, res, width), 16, (shape(pair...  7.19 us
    pallas_call x1, Pallas kernels, per_device(): call(functools.partial(attention_kernel, seqs, res, heads, count_b), 24,...  5.33 us
    pallas_call x1, Pallas kernels, per_device(): call(functools.partial(factor_kernel, seqs, res), 4, (shape((seqs * res +...  1.8 us
  transfers between devices with their start and end apart: 15, of which 8 were waited for; matrix products, arithmetic and copies ran while one was open for 0% of the time, Pallas kernels for 16%

profile of v2, /device:TPU:0, one launch (start us, length us, event | category | flops | bytes accessed | tf_op | source)
XLA Modules:
  0.0 46.1 jit_solution(2393153254940054611)
XLA Ops:
  0.6 1.8 %shard_map.149 = (bf16[272,256]{1,0:T(8,128)(2,1)S(1)}, bf16[8,2176]{1,0:T(8,128)(2,1)S(1)}) custom-call(bf16[256,256]{1,0:T(8,128)(2,1)} %bitcast.5, bf16[32,256]{1,0:T(8,128)(2,1)} %bitcast.8, bf16[32,256]{1,0:T(8,128)(2,1)} %bitcast.9, s32[8,32]{1,0:T(8,128)} %refs_3_.1), custom_call_target="tpu_custom_call" | custom-call | tf_op jit(solution)/shard_map/pallas_call | solution.py:299
  2.4 2.5 %collective-permute-start.5 = (bf16[8,2176]{1,0:T(8,128)(2,1)S(1)}, bf16[8,2176]{1,0:T(8,128)(2,1)S(1)}, u32[]{:S(2)}, u32[]{:S(2)}) collective-permute-start(bf16[8,2176]{1,0:T(8,128)(2,1)S(1)} %get-tuple-element.15.refs_0_), channel_id=1, source_target_pairs={{0,3},{1,2},{2,1},{3,0},{4,7},{5,6},{6,5},{7,4},{8,11},{9,10},{10,... | collective-permute-start | bytes 104456 | tf_op jit(solution)/shard_map/ppermute | solution.py:288
  4.9 0.6 %collective-permute-start.4 = (bf16[8,2176]{1,0:T(8,128)(2,1)S(1)}, bf16[8,2176]{1,0:T(8,128)(2,1)S(1)}, u32[]{:S(2)}, u32[]{:S(2)}) collective-permute-start(bf16[8,2176]{1,0:T(8,128)(2,1)S(1)} %get-tuple-element.15.refs_0_), channel_id=1, source_target_pairs={{0,2},{1,3},{2,0},{3,1},{4,6},{5,7},{6,4},{7,5},{8,10},{9,11},{10,... | collective-permute-start | bytes 104456 | tf_op jit(solution)/shard_map/ppermute | solution.py:288
  5.5 0.0 collective-permute-start.3
  5.6 1.1 %collective-permute-done.5.refs_3_ = bf16[8,2176]{1,0:T(8,128)(2,1)S(1)} collective-permute-done((bf16[8,2176]{1,0:T(8,128)(2,1)S(1)}, bf16[8,2176]{1,0:T(8,128)(2,1)S(1)}, u32[]{:S(2)}, u32[]{:S(2)}) %collective-permute-start.5) | collective-permute-done | bytes 34848 | tf_op jit(solution)/shard_map/ppermute | solution.py:288
  6.7 2.2 %collective-permute-done.4.refs_2_ = bf16[8,2176]{1,0:T(8,128)(2,1)S(1)} collective-permute-done((bf16[8,2176]{1,0:T(8,128)(2,1)S(1)}, bf16[8,2176]{1,0:T(8,128)(2,1)S(1)}, u32[]{:S(2)}, u32[]{:S(2)}) %collective-permute-start.4) | collective-permute-done | bytes 34848 | tf_op jit(solution)/shard_map/ppermute | solution.py:288
  8.9 0.0 collective-permute-done.3.refs_1_
  9.0 1.6 %collective-permute-start.6 = (bf16[8,2304]{1,0:T(8,128)(2,1)S(1)}, bf16[8,2304]{1,0:T(8,128)(2,1)S(1)}, u32[]{:S(2)}, u32[]{:S(2)}) collective-permute-start(bf16[8,2304]{1,0:T(8,128)(2,1)S(1)} %get-tuple-element.17), channel_id=1, source_target_pairs={{0,4},{1,5},{2,6},{3,7},{4,0},{5,1},{6,2},{7,3},{8,12},{9,13},{10,... | collective-permute-start | bytes 110600 | tf_op jit(solution)/shard_map/ppermute | solution.py:288
  10.6 2.6 %collective-permute-start.7 = (bf16[8,2304]{1,0:T(8,128)(2,1)S(1)}, bf16[8,2304]{1,0:T(8,128)(2,1)S(1)}, u32[]{:S(2)}, u32[]{:S(2)}) collective-permute-start(bf16[8,2304]{1,0:T(8,128)(2,1)S(1)} %get-tuple-element.18), channel_id=1, source_target_pairs={{0,8},{1,9},{2,10},{3,11},{4,12},{5,13},{6,14},{7,15},{8,0},{9,1},... | collective-permute-start | bytes 110600 | tf_op jit(solution)/shard_map/ppermute | solution.py:288
  13.2 0.2 collective-permute-start.8
  13.4 0.0 collective-permute-start.2
  13.4 1.0 %collective-permute-start.1 = (bf16[272,256]{1,0:T(8,128)(2,1)S(1)}, bf16[272,256]{1,0:T(8,128)(2,1)S(1)}, u32[]{:S(2)}, u32[]{:S(2)}) collective-permute-start(bf16[272,256]{1,0:T(8,128)(2,1)S(1)} %get-tuple-element.14.refs_0_), channel_id=1, source_target_pairs={{0,2},{1,3},{2,0},{3,1},{4,6},{5,7},{6,4},{7,5},{8,10},{9,11},{10,... | collective-permute-start | bytes 417800 | tf_op jit(solution)/shard_map/ppermute | solution.py:288
  14.4 0.0 collective-permute-done.6.refs_1_
  14.4 0.8 %collective-permute-start = (bf16[272,256]{1,0:T(8,128)(2,1)S(1)}, bf16[272,256]{1,0:T(8,128)(2,1)S(1)}, u32[]{:S(2)}, u32[]{:S(2)}) collective-permute-start(bf16[272,256]{1,0:T(8,128)(2,1)S(1)} %get-tuple-element.14.refs_0_), channel_id=1, source_target_pairs={{0,1},{1,0},{2,3},{3,2},{4,5},{5,4},{6,7},{7,6},{8,9},{9,8},{10,11... | collective-permute-start | bytes 417800 | tf_op jit(solution)/shard_map/ppermute | solution.py:288
  15.3 0.8 %collective-permute-done.7.refs_2_ = bf16[8,2304]{1,0:T(8,128)(2,1)S(1)} collective-permute-done((bf16[8,2304]{1,0:T(8,128)(2,1)S(1)}, bf16[8,2304]{1,0:T(8,128)(2,1)S(1)}, u32[]{:S(2)}, u32[]{:S(2)}) %collective-permute-start.7) | collective-permute-done | bytes 36896 | tf_op jit(solution)/shard_map/ppermute | solution.py:288
  16.1 2.8 %collective-permute-done.8.refs_3_ = bf16[8,2304]{1,0:T(8,128)(2,1)S(1)} collective-permute-done((bf16[8,2304]{1,0:T(8,128)(2,1)S(1)}, bf16[8,2304]{1,0:T(8,128)(2,1)S(1)}, u32[]{:S(2)}, u32[]{:S(2)}) %collective-permute-start.8) | collective-permute-done | bytes 36896 | tf_op jit(solution)/shard_map/ppermute | solution.py:288
  18.9 7.2 %shard_map.151 = (bf16[32,32,128]{2,1,0:T(8,128)(2,1)}, f32[32,256]{1,0:T(8,128)S(1)}) custom-call(bf16[8,2304]{1,0:T(8,128)(2,1)S(1)} %get-tuple-element.16.refs_0_, bf16[8,2304]{1,0:T(8,128)(2,1)S(1)} %collective-permute-done.6.refs_1_, bf16[8,2304]{1,0:T(8,128)(2,1)S(1)} %collective-permute-done.7.refs_2_, ...), custom_call_target="tpu_custom_call" | custom-call | tf_op jit(solution)/shard_map/pallas_call | solution.py:323
  26.1 0.6 %collective-permute-start.11 = (f32[32,256]{1,0:T(8,128)S(1)}, f32[32,256]{1,0:T(8,128)S(1)}, u32[]{:S(2)}, u32[]{:S(2)}) collective-permute-start(f32[32,256]{1,0:T(8,128)S(1)} %get-tuple-element.20.refs_0_), channel_id=1, source_target_pairs={{0,12},{1,13},{2,14},{3,15},{4,8},{5,9},{6,10},{7,11},{8,4},{9,5},... | collective-permute-start | bytes 98312 | tf_op jit(solution)/shard_map/ppermute | solution.py:288
  26.7 0.0 collective-permute-start.10
  26.7 5.4 %collective-permute-done.11.refs_3_ = f32[32,256]{1,0:T(8,128)S(1)} collective-permute-done((f32[32,256]{1,0:T(8,128)S(1)}, f32[32,256]{1,0:T(8,128)S(1)}, u32[]{:S(2)}, u32[]{:S(2)}) %collective-permute-start.11) | collective-permute-done | bytes 32800 | tf_op jit(solution)/shard_map/ppermute | solution.py:288
  32.2 0.0 collective-permute-start.9
  32.2 0.0 collective-permute-done.10.refs_2_
  32.2 3.9 %collective-permute-done.9.refs_1_ = f32[32,256]{1,0:T(8,128)S(1)} collective-permute-done((f32[32,256]{1,0:T(8,128)S(1)}, f32[32,256]{1,0:T(8,128)S(1)}, u32[]{:S(2)}, u32[]{:S(2)}) %collective-permute-start.9) | collective-permute-done | bytes 32800 | tf_op jit(solution)/shard_map/ppermute | solution.py:288
  36.1 0.1 collective-permute-start.12
  36.2 1.2 %collective-permute-start.13 = (f32[32,256]{1,0:T(8,128)S(1)}, f32[32,256]{1,0:T(8,128)S(1)}, u32[]{:S(2)}, u32[]{:S(2)}) collective-permute-start(f32[32,256]{1,0:T(8,128)S(1)} %get-tuple-element.23), channel_id=1, source_target_pairs={{0,2},{1,3},{2,0},{3,1},{4,6},{5,7},{6,4},{7,5},{8,10},{9,11},{10,... | collective-permute-start | bytes 98312 | tf_op jit(solution)/shard_map/ppermute | solution.py:288
  37.4 0.0 collective-permute-done.12.refs_5_
  37.4 0.9 %collective-permute-start.14 = (f32[32,256]{1,0:T(8,128)S(1)}, f32[32,256]{1,0:T(8,128)S(1)}, u32[]{:S(2)}, u32[]{:S(2)}) collective-permute-start(f32[32,256]{1,0:T(8,128)S(1)} %get-tuple-element.24), channel_id=1, source_target_pairs={{0,3},{1,2},{2,1},{3,0},{4,7},{5,6},{6,5},{7,4},{8,11},{9,10},{10,... | collective-permute-start | bytes 98312 | tf_op jit(solution)/shard_map/ppermute | solution.py:288
  38.2 1.9 %collective-permute-done.13.refs_6_ = f32[32,256]{1,0:T(8,128)S(1)} collective-permute-done((f32[32,256]{1,0:T(8,128)S(1)}, f32[32,256]{1,0:T(8,128)S(1)}, u32[]{:S(2)}, u32[]{:S(2)}) %collective-permute-start.13) | collective-permute-done | bytes 32800 | tf_op jit(solution)/shard_map/ppermute | solution.py:288
  40.2 0.6 %collective-permute-done.14.refs_7_ = f32[32,256]{1,0:T(8,128)S(1)} collective-permute-done((f32[32,256]{1,0:T(8,128)S(1)}, f32[32,256]{1,0:T(8,128)S(1)}, u32[]{:S(2)}, u32[]{:S(2)}) %collective-permute-start.14) | collective-permute-done | bytes 32800 | tf_op jit(solution)/shard_map/ppermute | solution.py:288
  40.7 0.0 collective-permute-done.2.refs_3_
  40.7 0.0 collective-permute-done.1.refs_2_
  40.7 0.0 collective-permute-done.refs_1_
  40.7 5.3 %shard_map.153 = bf16[256,256]{1,0:T(8,128)(2,1)} custom-call(bf16[272,256]{1,0:T(8,128)(2,1)S(1)} %get-tuple-element.14.refs_0_, bf16[272,256]{1,0:T(8,128)(2,1)S(1)} %collective-permute-done.refs_1_, bf16[272,256]{1,0:T(8,128)(2,1)S(1)} %collective-permute-done.1.refs_2_, bf16[272,256]{1,0:T(8,128)(2,1)S(1)} %collective-permute-done.2.refs_3_, ...), custom_call_target="tpu_custom_call" | custom-call | tf_op jit(solution)/shard_map/pallas_call | solution.py:356
  (2 shorter events, 0.1 us)
Async XLA Ops:
  2.4 4.3 %collective-permute-start.5 = (bf16[8,2176]{1,0:T(8,128)(2,1)S(1)}, bf16[8,2176]{1,0:T(8,128)(2,1)S(1)}, u32[]{:S(2)}, u32[]{:S(2)}) collective-permute-start(bf16[8,2176]{1,0:T(8,128)(2,1)S(1)} %get-tuple-element.15.refs_0_), channel_id=1, source_target_pairs={{0,3},{1,2},{2,1},{3,0},{4,7},{5,6},{6,5},{7,4},{8,11},{9,10},{10,... | collective-permute-start | bytes 104456 | tf_op jit(solution)/shard_map/ppermute | solution.py:288
  4.9 4.0 %collective-permute-start.4 = (bf16[8,2176]{1,0:T(8,128)(2,1)S(1)}, bf16[8,2176]{1,0:T(8,128)(2,1)S(1)}, u32[]{:S(2)}, u32[]{:S(2)}) collective-permute-start(bf16[8,2176]{1,0:T(8,128)(2,1)S(1)} %get-tuple-element.15.refs_0_), channel_id=1, source_target_pairs={{0,2},{1,3},{2,0},{3,1},{4,6},{5,7},{6,4},{7,5},{8,10},{9,11},{10,... | collective-permute-start | bytes 104456 | tf_op jit(solution)/shard_map/ppermute | solution.py:288
  5.5 3.4 %collective-permute-start.3 = (bf16[8,2176]{1,0:T(8,128)(2,1)S(1)}, bf16[8,2176]{1,0:T(8,128)(2,1)S(1)}, u32[]{:S(2)}, u32[]{:S(2)}) collective-permute-start(bf16[8,2176]{1,0:T(8,128)(2,1)S(1)} %get-tuple-element.15.refs_0_), channel_id=1, source_target_pairs={{0,1},{1,0},{2,3},{3,2},{4,5},{5,4},{6,7},{7,6},{8,9},{9,8},{10,11... | collective-permute-start | bytes 104456 | tf_op jit(solution)/shard_map/ppermute | solution.py:288
  9.0 5.5 %collective-permute-start.6 = (bf16[8,2304]{1,0:T(8,128)(2,1)S(1)}, bf16[8,2304]{1,0:T(8,128)(2,1)S(1)}, u32[]{:S(2)}, u32[]{:S(2)}) collective-permute-start(bf16[8,2304]{1,0:T(8,128)(2,1)S(1)} %get-tuple-element.17), channel_id=1, source_target_pairs={{0,4},{1,5},{2,6},{3,7},{4,0},{5,1},{6,2},{7,3},{8,12},{9,13},{10,... | collective-permute-start | bytes 110600 | tf_op jit(solution)/shard_map/ppermute | solution.py:288
  10.6 5.5 %collective-permute-start.7 = (bf16[8,2304]{1,0:T(8,128)(2,1)S(1)}, bf16[8,2304]{1,0:T(8,128)(2,1)S(1)}, u32[]{:S(2)}, u32[]{:S(2)}) collective-permute-start(bf16[8,2304]{1,0:T(8,128)(2,1)S(1)} %get-tuple-element.18), channel_id=1, source_target_pairs={{0,8},{1,9},{2,10},{3,11},{4,12},{5,13},{6,14},{7,15},{8,0},{9,1},... | collective-permute-start | bytes 110600 | tf_op jit(solution)/shard_map/ppermute | solution.py:288
  13.2 5.8 %collective-permute-start.8 = (bf16[8,2304]{1,0:T(8,128)(2,1)S(1)}, bf16[8,2304]{1,0:T(8,128)(2,1)S(1)}, u32[]{:S(2)}, u32[]{:S(2)}) collective-permute-start(bf16[8,2304]{1,0:T(8,128)(2,1)S(1)} %get-tuple-element.19), channel_id=1, source_target_pairs={{0,12},{1,13},{2,14},{3,15},{4,8},{5,9},{6,10},{7,11},{8,4},{9,5},... | collective-permute-start | bytes 110600 | tf_op jit(solution)/shard_map/ppermute | solution.py:288
  13.4 27.3 %collective-permute-start.2 = (bf16[272,256]{1,0:T(8,128)(2,1)S(1)}, bf16[272,256]{1,0:T(8,128)(2,1)S(1)}, u32[]{:S(2)}, u32[]{:S(2)}) collective-permute-start(bf16[272,256]{1,0:T(8,128)(2,1)S(1)} %get-tuple-element.14.refs_0_), channel_id=1, source_target_pairs={{0,3},{1,2},{2,1},{3,0},{4,7},{5,6},{6,5},{7,4},{8,11},{9,10},{10,... | collective-permute-start | bytes 417800 | tf_op jit(solution)/shard_map/ppermute | solution.py:288
  13.4 27.3 %collective-permute-start.1 = (bf16[272,256]{1,0:T(8,128)(2,1)S(1)}, bf16[272,256]{1,0:T(8,128)(2,1)S(1)}, u32[]{:S(2)}, u32[]{:S(2)}) collective-permute-start(bf16[272,256]{1,0:T(8,128)(2,1)S(1)} %get-tuple-element.14.refs_0_), channel_id=1, source_target_pairs={{0,2},{1,3},{2,0},{3,1},{4,6},{5,7},{6,4},{7,5},{8,10},{9,11},{10,... | collective-permute-start | bytes 417800 | tf_op jit(solution)/shard_map/ppermute | solution.py:288
  14.4 26.3 %collective-permute-start = (bf16[272,256]{1,0:T(8,128)(2,1)S(1)}, bf16[272,256]{1,0:T(8,128)(2,1)S(1)}, u32[]{:S(2)}, u32[]{:S(2)}) collective-permute-start(bf16[272,256]{1,0:T(8,128)(2,1)S(1)} %get-tuple-element.14.refs_0_), channel_id=1, source_target_pairs={{0,1},{1,0},{2,3},{3,2},{4,5},{5,4},{6,7},{7,6},{8,9},{9,8},{10,11... | collective-permute-start | bytes 417800 | tf_op jit(solution)/shard_map/ppermute | solution.py:288
  26.1 6.0 %collective-permute-start.11 = (f32[32,256]{1,0:T(8,128)S(1)}, f32[32,256]{1,0:T(8,128)S(1)}, u32[]{:S(2)}, u32[]{:S(2)}) collective-permute-start(f32[32,256]{1,0:T(8,128)S(1)} %get-tuple-element.20.refs_0_), channel_id=1, source_target_pairs={{0,12},{1,13},{2,14},{3,15},{4,8},{5,9},{6,10},{7,11},{8,4},{9,5},... | collective-permute-start | bytes 98312 | tf_op jit(solution)/shard_map/ppermute | solution.py:288
  26.7 5.5 %collective-permute-start.10 = (f32[32,256]{1,0:T(8,128)S(1)}, f32[32,256]{1,0:T(8,128)S(1)}, u32[]{:S(2)}, u32[]{:S(2)}) collective-permute-start(f32[32,256]{1,0:T(8,128)S(1)} %get-tuple-element.20.refs_0_), channel_id=1, source_target_pairs={{0,8},{1,9},{2,10},{3,11},{4,12},{5,13},{6,14},{7,15},{8,0},{9,1},... | collective-permute-start | bytes 98312 | tf_op jit(solution)/shard_map/ppermute | solution.py:288
  32.2 3.9 %collective-permute-start.9 = (f32[32,256]{1,0:T(8,128)S(1)}, f32[32,256]{1,0:T(8,128)S(1)}, u32[]{:S(2)}, u32[]{:S(2)}) collective-permute-start(f32[32,256]{1,0:T(8,128)S(1)} %get-tuple-element.20.refs_0_), channel_id=1, source_target_pairs={{0,4},{1,5},{2,6},{3,7},{4,0},{5,1},{6,2},{7,3},{8,12},{9,13},{10,... | collective-permute-start | bytes 98312 | tf_op jit(solution)/shard_map/ppermute | solution.py:288
  36.1 1.3 %collective-permute-start.12 = (f32[32,256]{1,0:T(8,128)S(1)}, f32[32,256]{1,0:T(8,128)S(1)}, u32[]{:S(2)}, u32[]{:S(2)}) collective-permute-start(f32[32,256]{1,0:T(8,128)S(1)} %get-tuple-element.22), channel_id=1, source_target_pairs={{0,1},{1,0},{2,3},{3,2},{4,5},{5,4},{6,7},{7,6},{8,9},{9,8},{10,11... | collective-permute-start | bytes 98312 | tf_op jit(solution)/shard_map/ppermute | solution.py:288
  36.2 4.0 %collective-permute-start.13 = (f32[32,256]{1,0:T(8,128)S(1)}, f32[32,256]{1,0:T(8,128)S(1)}, u32[]{:S(2)}, u32[]{:S(2)}) collective-permute-start(f32[32,256]{1,0:T(8,128)S(1)} %get-tuple-element.23), channel_id=1, source_target_pairs={{0,2},{1,3},{2,0},{3,1},{4,6},{5,7},{6,4},{7,5},{8,10},{9,11},{10,... | collective-permute-start | bytes 98312 | tf_op jit(solution)/shard_map/ppermute | solution.py:288
  37.4 3.3 %collective-permute-start.14 = (f32[32,256]{1,0:T(8,128)S(1)}, f32[32,256]{1,0:T(8,128)S(1)}, u32[]{:S(2)}, u32[]{:S(2)}) collective-permute-start(f32[32,256]{1,0:T(8,128)S(1)} %get-tuple-element.24), channel_id=1, source_target_pairs={{0,3},{1,2},{2,1},{3,0},{4,7},{5,6},{6,5},{7,4},{8,11},{9,10},{10,... | collective-permute-start | bytes 98312 | tf_op jit(solution)/shard_map/ppermute | solution.py:288

commit v3 on v2

--- a/solution.py
+++ b/solution.py
@@ -110,11 +110,21 @@
         outs[k][...] = scr[lax.bitwise_xor(col, k)]
 
 
+def order_kernel(res, width, *refs):
+    sources, (wout_ref, wrep_ref, wf_scr, *buffers, sems) = refs[:2], refs[2:]
+    get_wout, get_wbias = fetch(sources, buffers, sems)
+    heads = sources[1].shape[0]
+    wf_scr[...] = get_wout().astype(F32)
+    for d in range(width):
+        wout_ref[d * width : (d + 1) * width, :] = wf_scr[pl.ds(d, width, stride=width), :].astype(BF16)
+    repeat = spread_matrix(heads, heads * res, lambda c: c // res)
+    wrep_ref[...] = dot_tn(get_wbias(), repeat).astype(BF16)
+
+
 def pair_kernel(count_a, res, width, *refs):
     msgs = refs[:count_a]
-    sources, (out_ref, bias_ref) = refs[count_a : count_a + 3], refs[count_a + 3 : count_a + 5]
-    rt_scr, wf_scr, wp_scr, a_scr, *buffers, sems = refs[count_a + 5 :]
-    get_wout, get_wbias, get_pair = fetch(sources, buffers, sems)
+    wout_ref, wrep_ref, pair_hbm, out_ref, bias_ref, rt_scr, a_scr, pair_buf, sems = refs[count_a:]
+    (get_pair,) = fetch([pair_hbm], [pair_buf], sems)
     span = res * width
     per = LANES // width
     msg = jnp.concatenate([m[...].astype(F32) for m in msgs], axis=0)
@@ -122,114 +132,142 @@
     keep_row = msg[:, 2 * span : 2 * span + res].astype(BF16)
     keep_col = msg[:, 2 * span + LANES : 2 * span + LANES + res].astype(BF16)
     seq_total = msg.shape[0]
+    copies = max(1, LANES // seq_total)
+    many = max(per, 256 // seq_total)
+    right = msg[:, span : 2 * span]
     for t in range(rt_scr.shape[0]):
-        rows = msg[t * LANES : (t + 1) * LANES, span : 2 * span].T
-        rt_scr[t, :, : rows.shape[1]] = rows
-    lane = iota((res, LANES), 1)
-    segment = lane // width
-    for block in range(width // per):
-        lhs = jnp.concatenate(
+        rt_scr[t] = jnp.concatenate([right[t * LANES : (t + 1) * LANES]] * copies, axis=0).T
+    place = iota((res, LANES), 1) // seq_total
+    streams = []
+    for first in range(0, width, many):
+        tiles = []
+        for d in range(first, first + many, copies):
+            for t in range(rt_scr.shape[0]):
+                tile = rt_scr.at[t][pl.ds(d, res, stride=width), :]
+                for k in range(1, copies):
+                    other = rt_scr.at[t][pl.ds(d + k, res, stride=width), :]
+                    tile = jnp.where(place == k, other, tile)
+                tiles.append(tile.astype(BF16))
+        streams.append(jnp.concatenate(tiles, axis=1))
+    streams = jnp.concatenate(streams, axis=0)
+    segment = iota((seq_total, LANES), 1) // width
+    zero = jnp.zeros((seq_total, LANES), BF16)
+    for i in range(res):
+        group, k = i // per, i % per
+        only = jnp.where(segment == k, left[:, group * LANES : (group + 1) * LANES], zero)
+        moved = [
+            only if d == k else pltpu.roll(only, ((d - k) % per) * width, 1) for d in range(per)
+        ]
+        diagonal = jnp.concatenate(
             [
                 jnp.concatenate(
-                    [rt_scr.at[t][pl.ds(block * per + k, res, stride=width), :] for k in range(per)],
-                    axis=0,
+                    [moved[d % per] if u == d // per else zero for u in range(many // per)], axis=1
                 )
-                for t in range(rt_scr.shape[0])
+                for d in range(many)
             ],
-            axis=1,
-        )[:, :seq_total].astype(BF16)
-        prod = dot(lhs, left).astype(BF16)
-        for group in range(span // LANES):
-            tiles = [
-                prod[k * res : (k + 1) * res, group * LANES : (group + 1) * LANES] for k in range(per)
+            axis=0,
+        )
+        prod = dot(streams, diagonal).astype(BF16)
+        for n in range(width // many):
+            a_scr[i * res : (i + 1) * res, n * many * width : (n + 1) * many * width] = prod[
+                n * res : (n + 1) * res
             ]
-            step = per // 2
-            while step >= 1:
-                low = (segment & step) == 0
-                for k in range(per):
-                    if k & step:
-                        continue
-                    first, second = tiles[k], tiles[k + step]
-                    tiles[k] = jnp.where(low, first, pltpu.roll(second, step * width, 1))
-                    tiles[k + step] = jnp.where(
-                        low, pltpu.roll(first, LANES - step * width, 1), second
-                    )
-                step //= 2
-            for k in range(per):
-                i = group * per + k
-                a_scr[i * res : (i + 1) * res, block * LANES : (block + 1) * LANES] = tiles[k]
-    wf_scr[...] = get_wout().astype(F32)
-    for d in range(width):
-        wp_scr[d * width : (d + 1) * width, :] = wf_scr[pl.ds(d, width, stride=width), :].astype(BF16)
-    counts = dot_tn(keep_col, keep_row)
-    inverse = 1.0 / counts
-    heads = sources[1].shape[0]
+    inverse = 1.0 / dot_tn(keep_col, keep_row)
+    wide = wrep_ref.shape[1]
+    query = iota((res, wide), 1) % res
     pair = get_pair()
-    w_rep = dot_tn(get_wbias(), spread_matrix(heads, heads * res, lambda c: c // res)).astype(BF16)
-    query = iota((res, heads * res), 1) % res
-    bias = jnp.zeros((res, heads * res), F32)
+    bias = jnp.zeros((res, wide), F32)
     chunk = 8
     for start in range(0, res, chunk):
-        upd = dot(a_scr[start * res : (start + chunk) * res, :], wp_scr[...])
-        for i in range(start, start + chunk):
-            mine = upd[(i - start) * res : (i - start + 1) * res]
-            total = (pair[i].astype(F32) + mine * inverse[:, i : i + 1]).astype(BF16)
-            out_ref[i] = total
-            normed = layer_norm(total.astype(F32)).astype(BF16)
-            bias = jnp.where(query == i, dot(normed, w_rep), bias)
+        upd = dot(a_scr[start * res : (start + chunk) * res, :], wout_ref[...])
+        total = jnp.concatenate(
+            [
+                pair[start + i].astype(F32)
+                + upd[i * res : (i + 1) * res] * inverse[:, start + i : start + i + 1]
+                for i in range(chunk)
+            ],
+            axis=0,
+        ).astype(BF16)
+        out_ref[start : start + chunk] = total.reshape(chunk, res, total.shape[1])
+        spread = dot(layer_norm(total.astype(F32)).astype(BF16), wrep_ref[...])
+        for i in range(chunk):
+            bias = jnp.where(query == start + i, spread[i * res : (i + 1) * res], bias)
     bias_ref[...] = bias
 
 
+def query_kernel(seqs, res, heads, rows_ref, wq_hbm, wg_hbm, query_ref, gate_ref, *scratch):
+    get_q, get_g = fetch([wq_hbm, wg_hbm], scratch[:2], scratch[2])
+    own = rows_ref[: seqs * res, :]
+    head_width = query_ref.shape[1] // heads
+    query_ref[...] = (dot(own, get_q()) * (head_width ** (-0.5))).astype(BF16)
+    gate_ref[...] = jax.nn.sigmoid(dot(own, get_g()))
+
+
+def key_kernel(seqs, res, count_b, *refs):
+    rows_refs, refs = refs[:count_b], refs[count_b:]
+    wk_hbm, wv_hbm, key_ref, value_ref, limit_ref, wk_buf, wv_buf, sems = refs
+    get_k, get_v = fetch([wk_hbm, wv_hbm], [wk_buf, wv_buf], sems)
+    spread = spread_matrix(seqs, seqs * LANES, lambda c: c // LANES)
+    for get, ref in ((get_k, key_ref), (get_v, value_ref)):
+        weight = get()
+        for k in range(count_b):
+            made = dot(rows_refs[k][: seqs * res, :], weight).astype(BF16)
+            for s in range(seqs):
+                ref[s, k * res : (k + 1) * res, :] = made[s * res : (s + 1) * res]
+    for k in range(count_b):
+        keep = dot_tn(rows_refs[k][seqs * res : seqs * res + seqs, :res], spread)
+        keep = jnp.where(keep > 0, 3e38, -1000000000.0)
+        for s in range(seqs):
+            limit_ref[s, k * res : (k + 1) * res, :] = keep[:, s * LANES : (s + 1) * LANES]
+
+
+def score_kernel(seqs, res, heads, query_ref, key_ref, score_ref):
+    channels = query_ref.shape[1]
+    wide = heads * res
+    same_head = iota((wide, channels), 0) // res == iota((wide, channels), 1) // (channels // heads)
+    for s in range(seqs):
+        query_wide = jnp.where(
+            same_head,
+            jnp.concatenate([query_ref[s * res : (s + 1) * res, :]] * heads, axis=0),
+            jnp.zeros((), BF16),
+        )
+        score_ref[s] = dot_nt(key_ref[s], query_wide)
+
+
 def attention_kernel(seqs, res, heads, count_b, *refs):
-    rows_refs, bias_refs = refs[:count_b], refs[count_b : 2 * count_b]
-    sources, out_ref = refs[2 * count_b : 2 * count_b + 8], refs[2 * count_b + 8]
-    bias_scr, kv_scr, att_scr, *buffers, sems = refs[2 * count_b + 9 :]
-    get_k, get_v, get_q, get_g, get_o, get_up, get_down, get_x = fetch(sources, buffers, sems)
+    score_ref, value_ref, limit_ref, gate_ref = refs[:4]
+    bias_refs, refs = refs[4 : 4 + count_b], refs[4 + count_b :]
+    sources, out_ref, refs = refs[:4], refs[4], refs[5:]
+    bias_scr, att_scr, diag_scr, *buffers, sems = refs
+    get_o, get_up, get_down, get_x = fetch(sources, buffers, sems)
     channels = out_ref.shape[1]
     head_width = channels // heads
     wide = heads * res
+    per = LANES // head_width
     for k in range(count_b):
         bias_scr[k * res : (k + 1) * res, :] = bias_refs[k][...]
-    own = rows_refs[0][: seqs * res, :]
-    w_kv = jnp.concatenate([get_k(), get_v()], axis=1)
-    spread = spread_matrix(seqs, seqs * LANES, lambda c: c // LANES)
-    keeps = []
-    for k in range(count_b):
-        kv = dot(rows_refs[k][: seqs * res, :], w_kv).astype(BF16)
-        for s in range(seqs):
-            kv_scr[s, k * res : (k + 1) * res, :] = kv[s * res : (s + 1) * res]
-        keeps.append(dot_tn(rows_refs[k][seqs * res : seqs * res + seqs, :res], spread))
-    query = (dot(own, get_q()) * (head_width ** (-0.5))).astype(BF16)
-    gate = jax.nn.sigmoid(dot(own, get_g()))
-    same_head = iota((wide, channels), 0) // res == iota((wide, channels), 1) // head_width
-    lane_head = iota((res, channels), 1) // head_width
-    masses = []
+    lane_head = iota((res, LANES), 1) // head_width
+    diag = iota((res, wide), 0) == iota((res, wide), 1) % res
     for s in range(seqs):
-        query_s = query[s * res : (s + 1) * res]
-        query_wide = jnp.where(
-            same_head, jnp.concatenate([query_s] * heads, axis=0), jnp.zeros((), BF16)
-        )
-        scores = dot_nt(kv_scr[s, :, :channels], query_wide) + bias_scr[...]
-        keep = jnp.concatenate([m[:, s * LANES : (s + 1) * LANES] for m in keeps], axis=0)
-        keep = jnp.concatenate([keep] * (wide // LANES), axis=1)
-        scores = jnp.where(keep > 0, scores, -1000000000.0)
+        top = jnp.concatenate([limit_ref[s]] * (wide // LANES), axis=1)
+        scores = jnp.minimum(score_ref[s] + bias_scr[...], top)
         raw = jnp.exp(scores - jnp.max(scores, axis=0, keepdims=True))
-        masses.append(jnp.sum(raw, axis=0, keepdims=True))
-        mixed = dot_tn(raw.astype(BF16), kv_scr[s, :, channels:])
-        picked = mixed[:res]
-        for h in range(1, heads):
-            picked = jnp.where(lane_head == h, mixed[h * res : (h + 1) * res], picked)
-        att_scr[s * res : (s + 1) * res, :] = picked
-    mass_rows = jnp.concatenate([jnp.broadcast_to(1.0 / m, (res, wide)) for m in masses], axis=0)
-    diag = iota((seqs * res, wide), 0) % res == iota((seqs * res, wide), 1) % res
+        mass = jnp.sum(raw, axis=0, keepdims=True)
+        diag_scr[s * res : (s + 1) * res, :] = jnp.where(diag, 1.0 / mass, 0.0)
+        probs = raw.astype(BF16)
+        for u in range(channels // LANES):
+            lanes = slice(u * LANES, (u + 1) * LANES)
+            rows = slice(u * per * res, (u + 1) * per * res)
+            mixed = dot_tn(probs[:, rows], value_ref[s, :, lanes])
+            picked = mixed[:res]
+            for h in range(1, per):
+                picked = jnp.where(lane_head == h, mixed[h * res : (h + 1) * res], picked)
+            att_scr[s * res : (s + 1) * res, lanes] = picked
     head_pick = (iota((wide, channels), 0) // res == iota((wide, channels), 1) // head_width).astype(F32)
     inverse = jnp.dot(
-        jnp.where(diag, mass_rows, 0.0),
-        head_pick,
-        preferred_element_type=F32,
-        precision=lax.Precision.HIGHEST,
+        diag_scr[...], head_pick, preferred_element_type=F32, precision=lax.Precision.HIGHEST
     )
-    gated = (att_scr[...] * inverse * gate).astype(BF16)
+    gated = (att_scr[...] * inverse * gate_ref[...]).astype(BF16)
     middle = get_x().astype(F32) + dot(gated, get_o())
     hidden = jnp.maximum(dot(layer_norm(middle).astype(BF16), get_up()), 0.0).astype(BF16)
     out_ref[...] = (middle + dot(hidden, get_down())).astype(BF16)
@@ -319,20 +357,58 @@
     all_rows = [rows] + [along_b(rows, k) for k in range(1, count_b)]
 
     seq_total = seqs * count_a
-    weights = [outer_output_weight, pair_bias_weight.T, pair_state]
+    weights = [outer_output_weight, pair_bias_weight.T]
+    w_out, w_rep = call(
+        functools.partial(order_kernel, res, width),
+        4,
+        (
+            shape(outer_output_weight.shape, BF16),
+            shape((pair_bias_weight.shape[0], heads * res), BF16),
+        ),
+        [pltpu.VMEM(outer_output_weight.shape, F32)],
+        0,
+        weights,
+    )(*in_hbm(weights))
     pair_output, bias = call(
         functools.partial(pair_kernel, count_a, res, width),
         16,
         (shape(pair_state.shape, BF16), shape((res, heads * res), F32)),
         [
             pltpu.VMEM((pl.cdiv(seq_total, LANES), span, LANES), F32),
-            pltpu.VMEM(outer_output_weight.shape, F32),
-            pltpu.VMEM(outer_output_weight.shape, BF16),
             pltpu.VMEM((res * res, width * width), BF16),
         ],
-        count_a,
+        count_a + 2,
+        [pair_state],
+    )(*msgs, w_out, w_rep, *in_hbm([pair_state]))
+
+    weights = [query_weight, gate_weight]
+    query, gate = call(
+        functools.partial(query_kernel, seqs, res, heads),
+        4,
+        (shape((seqs * res, channels), BF16), shape((seqs * res, channels), F32)),
+        [],
+        1,
         weights,
-    )(*msgs, *in_hbm(weights))
+    )(rows, *in_hbm(weights))
+    keys = res * count_b
+    weights = [key_weight, value_weight]
+    key, value, limit = call(
+        functools.partial(key_kernel, seqs, res, count_b),
+        8,
+        (
+            shape((seqs, keys, channels), BF16),
+            shape((seqs, keys, channels), BF16),
+            shape((seqs, keys, LANES), F32),
+        ),
+        [],
+        count_b,
+        weights,
+    )(*all_rows, *in_hbm(weights))
+    (scores,) = call(
+        functools.partial(score_kernel, seqs, res, heads),
+        8,
+        (shape((seqs, keys, heads * res), F32),),
+    )(query, key)
 
     tiles = [bias] + [along_a(bias, k) for k in range(1, count_a)]
     biases = call(
@@ -342,29 +418,19 @@
         [pltpu.VMEM((count_a,) + bias.shape, F32)],
     )(*tiles)
     biases = [biases[0]] + [along_b(biases[k], k) for k in range(1, count_b)]
-    keys = res * count_b
-    weights = [
-        key_weight,
-        value_weight,
-        query_weight,
-        gate_weight,
-        output_weight,
-        up_weight,
-        down_weight,
-        flat,
-    ]
+    weights = [output_weight, up_weight, down_weight, flat]
     (out,) = call(
         functools.partial(attention_kernel, seqs, res, heads, count_b),
-        24,
+        16,
         (shape((seqs * res, channels), BF16),),
         [
             pltpu.VMEM((keys, heads * res), F32),
-            pltpu.VMEM((seqs, keys, 2 * channels), BF16),
             pltpu.VMEM((seqs * res, channels), F32),
+            pltpu.VMEM((seqs * res, heads * res), F32),
         ],
-        2 * count_b,
+        4 + count_b,
         weights,
-    )(*all_rows, *biases, *in_hbm(weights))
+    )(scores, value, limit, gate, *biases, *in_hbm(weights))
     return (out.reshape(seqs, res, channels), pair_output)
 
 

time: 46.2 us -> 44.6 us (0.965)
  waiting for transfers between devices: 18.9 us -> 12.1 us
  starting transfers between devices: 12.2 us -> 16.4 us
  Pallas kernels: 14.4 us -> 15.1 us
    ppermute x15, waiting for transfers between devices: 18.9 us -> 12.1 us  [permute(): return lax.ppermute(value, ('aa', 'ba'), pairs)]
    ppermute x15, starting transfers between devices: 12.2 us -> 16.4 us  [permute(): return lax.ppermute(value, ('aa', 'ba'), pairs)]
    pallas_call x1 -> x5, Pallas kernels: 5.33 us -> 8.86 us  [the longest x1 3.92 us: per_device(): call(functools.partial(attention_kernel, seqs, res, heads, count_b), 16,...]
    pallas_call x1, Pallas kernels: 7.19 us -> 4.4 us  [per_device(): call(functools.partial(pair_kernel, count_a, res, width), 16, (shape(pair...]
  transfers between devices with their start and end apart: 15 -> 15, of which waited for: 8 -> 5; matrix products, arithmetic and copies ran while one was open for 0% -> 0% of each run, Pallas kernels for 16% -> 21%
where the time goes in v3:
time: 44.6 us; the launch traced here: 44.3 us
  starting transfers between devices  16.4 us (37%)
  Pallas kernels  15.1 us (34%)
  waiting for transfers between devices  12.1 us (27%)
  between operations  0.75 us (2%)
    ppermute x15, starting transfers between devices, permute(): return lax.ppermute(value, ('aa', 'ba'), pairs)  16.4 us
    ppermute x15, waiting for transfers between devices, permute(): return lax.ppermute(value, ('aa', 'ba'), pairs)  12.1 us
    pallas_call x1, Pallas kernels, per_device(): call(functools.partial(pair_kernel, count_a, res, width), 16, (shape(pair...  4.4 us
    pallas_call x1, Pallas kernels, per_device(): call(functools.partial(attention_kernel, seqs, res, heads, count_b), 16,...  3.92 us
    pallas_call x1, Pallas kernels, per_device(): call(functools.partial(factor_kernel, seqs, res), 4, (shape((seqs * res +...  1.8 us
    pallas_call x1, Pallas kernels, per_device(): call(functools.partial(key_kernel, seqs, res, count_b), 8, (shape((seqs,...  1.61 us
    pallas_call x1, Pallas kernels, per_device(): call(functools.partial(order_kernel, res, width), 4, (shape(outer_output_...  1.5 us
    pallas_call x1, Pallas kernels, per_device(): call(functools.partial(query_kernel, seqs, res, heads), 4, (shape((seqs *...  1.36 us
  transfers between devices with their start and end apart: 15, of which 5 were waited for; matrix products, arithmetic and copies ran while one was open for 0% of the time, Pallas kernels for 21%

profile of v3, /device:TPU:0, one launch (start us, length us, event | category | flops | bytes accessed | tf_op | source)
XLA Modules:
  0.0 44.3 jit_solution(9042376064084564573)
XLA Ops:
  0.6 1.8 %shard_map.149 = (bf16[272,256]{1,0:T(8,128)(2,1)S(1)}, bf16[8,2176]{1,0:T(8,128)(2,1)S(1)}) custom-call(bf16[256,256]{1,0:T(8,128)(2,1)} %bitcast.5, bf16[32,256]{1,0:T(8,128)(2,1)} %bitcast.8, bf16[32,256]{1,0:T(8,128)(2,1)} %bitcast.9, s32[8,32]{1,0:T(8,128)} %refs_3_.1), custom_call_target="tpu_custom_call" | custom-call | tf_op jit(solution)/shard_map/pallas_call | solution.py:337
  2.4 0.6 %collective-permute-start.3 = (bf16[8,2176]{1,0:T(8,128)(2,1)S(1)}, bf16[8,2176]{1,0:T(8,128)(2,1)S(1)}, u32[]{:S(2)}, u32[]{:S(2)}) collective-permute-start(bf16[8,2176]{1,0:T(8,128)(2,1)S(1)} %get-tuple-element.27.refs_0_), channel_id=1, source_target_pairs={{0,1},{1,0},{2,3},{3,2},{4,5},{5,4},{6,7},{7,6},{8,9},{9,8},{10,11... | collective-permute-start | bytes 104456 | tf_op jit(solution)/shard_map/ppermute | solution.py:326
  3.0 2.6 %collective-permute-start.4 = (bf16[8,2176]{1,0:T(8,128)(2,1)S(1)}, bf16[8,2176]{1,0:T(8,128)(2,1)S(1)}, u32[]{:S(2)}, u32[]{:S(2)}) collective-permute-start(bf16[8,2176]{1,0:T(8,128)(2,1)S(1)} %get-tuple-element.27.refs_0_), channel_id=1, source_target_pairs={{0,2},{1,3},{2,0},{3,1},{4,6},{5,7},{6,4},{7,5},{8,10},{9,11},{10,... | collective-permute-start | bytes 104456 | tf_op jit(solution)/shard_map/ppermute | solution.py:326
  5.5 0.0 collective-permute-start.5
  5.6 0.0 collective-permute-done.3.refs_1_
  5.6 2.0 %collective-permute-done.4.refs_2_ = bf16[8,2176]{1,0:T(8,128)(2,1)S(1)} collective-permute-done((bf16[8,2176]{1,0:T(8,128)(2,1)S(1)}, bf16[8,2176]{1,0:T(8,128)(2,1)S(1)}, u32[]{:S(2)}, u32[]{:S(2)}) %collective-permute-start.4) | collective-permute-done | bytes 34848 | tf_op jit(solution)/shard_map/ppermute | solution.py:326
  7.6 1.4 %collective-permute-done.5.refs_3_ = bf16[8,2176]{1,0:T(8,128)(2,1)S(1)} collective-permute-done((bf16[8,2176]{1,0:T(8,128)(2,1)S(1)}, bf16[8,2176]{1,0:T(8,128)(2,1)S(1)}, u32[]{:S(2)}, u32[]{:S(2)}) %collective-permute-start.5) | collective-permute-done | bytes 34848 | tf_op jit(solution)/shard_map/ppermute | solution.py:326
  9.0 1.6 %collective-permute-start.6 = (bf16[8,2304]{1,0:T(8,128)(2,1)S(1)}, bf16[8,2304]{1,0:T(8,128)(2,1)S(1)}, u32[]{:S(2)}, u32[]{:S(2)}) collective-permute-start(bf16[8,2304]{1,0:T(8,128)(2,1)S(1)} %get-tuple-element.29), channel_id=1, source_target_pairs={{0,4},{1,5},{2,6},{3,7},{4,0},{5,1},{6,2},{7,3},{8,12},{9,13},{10,... | collective-permute-start | bytes 110600 | tf_op jit(solution)/shard_map/ppermute | solution.py:326
  10.6 0.0 collective-permute-start
  10.6 0.9 %collective-permute-start.1 = (bf16[272,256]{1,0:T(8,128)(2,1)S(1)}, bf16[272,256]{1,0:T(8,128)(2,1)S(1)}, u32[]{:S(2)}, u32[]{:S(2)}) collective-permute-start(bf16[272,256]{1,0:T(8,128)(2,1)S(1)} %get-tuple-element.21.rows_ref.refs_0_), channel_id=1, source_target_pairs={{0,2},{1,3},{2,0},{3,1},{4,6},{5,7},{6,4},{7,5},{8,10},{9,11},{10,... | collective-permute-start | bytes 417800 | tf_op jit(solution)/shard_map/ppermute | solution.py:326
  11.5 1.0 %collective-permute-start.2 = (bf16[272,256]{1,0:T(8,128)(2,1)S(1)}, bf16[272,256]{1,0:T(8,128)(2,1)S(1)}, u32[]{:S(2)}, u32[]{:S(2)}) collective-permute-start(bf16[272,256]{1,0:T(8,128)(2,1)S(1)} %get-tuple-element.21.rows_ref.refs_0_), channel_id=1, source_target_pairs={{0,3},{1,2},{2,1},{3,0},{4,7},{5,6},{6,5},{7,4},{8,11},{9,10},{10,... | collective-permute-start | bytes 417800 | tf_op jit(solution)/shard_map/ppermute | solution.py:326
  12.5 2.6 %collective-permute-start.7 = (bf16[8,2304]{1,0:T(8,128)(2,1)S(1)}, bf16[8,2304]{1,0:T(8,128)(2,1)S(1)}, u32[]{:S(2)}, u32[]{:S(2)}) collective-permute-start(bf16[8,2304]{1,0:T(8,128)(2,1)S(1)} %get-tuple-element.30), channel_id=1, source_target_pairs={{0,8},{1,9},{2,10},{3,11},{4,12},{5,13},{6,14},{7,15},{8,0},{9,1},... | collective-permute-start | bytes 110600 | tf_op jit(solution)/shard_map/ppermute | solution.py:326
  15.1 0.0 collective-permute-done.6.refs_1_
  15.1 1.5 %collective-permute-start.8 = (bf16[8,2304]{1,0:T(8,128)(2,1)S(1)}, bf16[8,2304]{1,0:T(8,128)(2,1)S(1)}, u32[]{:S(2)}, u32[]{:S(2)}) collective-permute-start(bf16[8,2304]{1,0:T(8,128)(2,1)S(1)} %get-tuple-element.31), channel_id=1, source_target_pairs={{0,12},{1,13},{2,14},{3,15},{4,8},{5,9},{6,10},{7,11},{8,4},{9,5},... | collective-permute-start | bytes 110600 | tf_op jit(solution)/shard_map/ppermute | solution.py:326
  16.6 1.5 %shard_map.154 = (bf16[1024,128]{1,0:T(8,128)(2,1)S(1)}, bf16[128,256]{1,0:T(8,128)(2,1)S(1)}) custom-call(bf16[1024,128]{1,0:T(8,128)(2,1)} %refs_0_.1, bf16[8,128]{1,0:T(8,128)(2,1)} %bitcast.10), custom_call_target="tpu_custom_call" | custom-call | tf_op jit(solution)/shard_map/pallas_call | solution.py:361
  18.1 0.0 collective-permute-done.7.refs_2_
  18.1 2.7 %collective-permute-done.8.refs_3_ = bf16[8,2304]{1,0:T(8,128)(2,1)S(1)} collective-permute-done((bf16[8,2304]{1,0:T(8,128)(2,1)S(1)}, bf16[8,2304]{1,0:T(8,128)(2,1)S(1)}, u32[]{:S(2)}, u32[]{:S(2)}) %collective-permute-start.8) | collective-permute-done | bytes 36896 | tf_op jit(solution)/shard_map/ppermute | solution.py:326
  20.8 4.4 %shard_map.155 = (bf16[32,32,128]{2,1,0:T(8,128)(2,1)}, f32[32,256]{1,0:T(8,128)S(1)}) custom-call(bf16[8,2304]{1,0:T(8,128)(2,1)S(1)} %get-tuple-element.28.refs_0_, bf16[8,2304]{1,0:T(8,128)(2,1)S(1)} %collective-permute-done.6.refs_1_, bf16[8,2304]{1,0:T(8,128)(2,1)S(1)} %collective-permute-done.7.refs_2_, ...), custom_call_target="tpu_custom_call" | custom-call | tf_op jit(solution)/shard_map/pallas_call | solution.py:372
  25.2 0.1 collective-permute-start.9
  25.3 2.1 %collective-permute-start.10 = (f32[32,256]{1,0:T(8,128)S(1)}, f32[32,256]{1,0:T(8,128)S(1)}, u32[]{:S(2)}, u32[]{:S(2)}) collective-permute-start(f32[32,256]{1,0:T(8,128)S(1)} %get-tuple-element.34.refs_0_), channel_id=1, source_target_pairs={{0,8},{1,9},{2,10},{3,11},{4,12},{5,13},{6,14},{7,15},{8,0},{9,1},... | collective-permute-start | bytes 98312 | tf_op jit(solution)/shard_map/ppermute | solution.py:326
  27.4 1.8 %collective-permute-done.9.refs_1_ = f32[32,256]{1,0:T(8,128)S(1)} collective-permute-done((f32[32,256]{1,0:T(8,128)S(1)}, f32[32,256]{1,0:T(8,128)S(1)}, u32[]{:S(2)}, u32[]{:S(2)}) %collective-permute-start.9) | collective-permute-done | bytes 32800 | tf_op jit(solution)/shard_map/ppermute | solution.py:326
  29.2 1.5 %collective-permute-start.11 = (f32[32,256]{1,0:T(8,128)S(1)}, f32[32,256]{1,0:T(8,128)S(1)}, u32[]{:S(2)}, u32[]{:S(2)}) collective-permute-start(f32[32,256]{1,0:T(8,128)S(1)} %get-tuple-element.34.refs_0_), channel_id=1, source_target_pairs={{0,12},{1,13},{2,14},{3,15},{4,8},{5,9},{6,10},{7,11},{8,4},{9,5},... | collective-permute-start | bytes 98312 | tf_op jit(solution)/shard_map/ppermute | solution.py:326
  30.8 0.0 collective-permute-done.10.refs_2_
  30.8 4.2 %collective-permute-done.11.refs_3_ = f32[32,256]{1,0:T(8,128)S(1)} collective-permute-done((f32[32,256]{1,0:T(8,128)S(1)}, f32[32,256]{1,0:T(8,128)S(1)}, u32[]{:S(2)}, u32[]{:S(2)}) %collective-permute-start.11) | collective-permute-done | bytes 32800 | tf_op jit(solution)/shard_map/ppermute | solution.py:326
  35.0 0.1 collective-permute-start.12
  35.0 0.9 %collective-permute-start.13 = (f32[32,256]{1,0:T(8,128)S(1)}, f32[32,256]{1,0:T(8,128)S(1)}, u32[]{:S(2)}, u32[]{:S(2)}) collective-permute-start(f32[32,256]{1,0:T(8,128)S(1)} %get-tuple-element.37), channel_id=1, source_target_pairs={{0,2},{1,3},{2,0},{3,1},{4,6},{5,7},{6,4},{7,5},{8,10},{9,11},{10,... | collective-permute-start | bytes 98312 | tf_op jit(solution)/shard_map/ppermute | solution.py:326
  36.0 0.0 collective-permute-done.refs_1_
  36.0 0.9 %collective-permute-start.14 = (f32[32,256]{1,0:T(8,128)S(1)}, f32[32,256]{1,0:T(8,128)S(1)}, u32[]{:S(2)}, u32[]{:S(2)}) collective-permute-start(f32[32,256]{1,0:T(8,128)S(1)} %get-tuple-element.38), channel_id=1, source_target_pairs={{0,3},{1,2},{2,1},{3,0},{4,7},{5,6},{6,5},{7,4},{8,11},{9,10},{10,... | collective-permute-start | bytes 98312 | tf_op jit(solution)/shard_map/ppermute | solution.py:326
  36.9 1.4 %shard_map.150 = (bf16[256,256]{1,0:T(8,128)(2,1)S(1)}, f32[256,256]{1,0:T(8,128)S(1)}) custom-call(bf16[272,256]{1,0:T(8,128)(2,1)S(1)} %get-tuple-element.21.rows_ref.refs_0_, bf16[256,256]{1,0:T(8,128)(2,1)} %wq_hbm.1, bf16[256,256]{1,0:T(8,128)(2,1)} %wg_hbm.1), custom_call_target="tpu_custom_call" | custom-call | tf_op jit(solution)/shard_map/pallas_call | solution.py:385
  38.3 0.0 collective-permute-done.1.refs_2_
  38.3 0.0 collective-permute-done.2.refs_3_
  38.3 1.6 %shard_map.151 = (bf16[8,128,256]{2,1,0:T(8,128)(2,1)S(1)}, bf16[8,128,256]{2,1,0:T(8,128)(2,1)S(1)}, f32[8,128,128]{2,1,0:T(8,128)S(1)}) custom-call(bf16[272,256]{1,0:T(8,128)(2,1)S(1)} %get-tuple-element.21.rows_ref.refs_0_, bf16[272,256]{1,0:T(8,128)(2,1)S(1)} %collective-permute-done.refs_1_, bf16[272,256]{1,0:T(8,128)(2,1)S(1)} %collective-permute-done.1.refs_2_, ...), custom_call_target="tpu_custom_call" | custom-call | tf_op jit(solution)/shard_map/pallas_call | solution.py:395
  39.9 0.5 %shard_map.152.refs_0_ = f32[8,128,256]{2,1,0:T(8,128)S(1)} custom-call(bf16[256,256]{1,0:T(8,128)(2,1)S(1)} %get-tuple-element.22.query_ref, bf16[8,128,256]{2,1,0:T(8,128)(2,1)S(1)} %get-tuple-element.23.key_ref), custom_call_target="tpu_custom_call" | custom-call | tf_op jit(solution)/shard_map/pallas_call | solution.py:407
  40.4 0.0 collective-permute-done.12.refs_5_
  40.4 0.0 collective-permute-done.13.refs_6_
  40.4 0.0 collective-permute-done.14.refs_7_
  40.4 3.9 %shard_map.157 = bf16[256,256]{1,0:T(8,128)(2,1)} custom-call(f32[8,128,256]{2,1,0:T(8,128)S(1)} %shard_map.152.refs_0_, bf16[8,128,256]{2,1,0:T(8,128)(2,1)S(1)} %get-tuple-element.24.refs_1_, f32[8,128,128]{2,1,0:T(8,128)S(1)} %get-tuple-element.25.refs_2_, f32[256,256]{1,0:T(8,128)S(1)} %get-tuple-element.26.refs_3_, ...), custom_call_target="tpu_custom_call" | custom-call | tf_op jit(solution)/shard_map/pallas_call | solution.py:422
  (2 shorter events, 0.1 us)
Async XLA Ops:
  2.4 3.2 %collective-permute-start.3 = (bf16[8,2176]{1,0:T(8,128)(2,1)S(1)}, bf16[8,2176]{1,0:T(8,128)(2,1)S(1)}, u32[]{:S(2)}, u32[]{:S(2)}) collective-permute-start(bf16[8,2176]{1,0:T(8,128)(2,1)S(1)} %get-tuple-element.27.refs_0_), channel_id=1, source_target_pairs={{0,1},{1,0},{2,3},{3,2},{4,5},{5,4},{6,7},{7,6},{8,9},{9,8},{10,11... | collective-permute-start | bytes 104456 | tf_op jit(solution)/shard_map/ppermute | solution.py:326
  3.0 4.6 %collective-permute-start.4 = (bf16[8,2176]{1,0:T(8,128)(2,1)S(1)}, bf16[8,2176]{1,0:T(8,128)(2,1)S(1)}, u32[]{:S(2)}, u32[]{:S(2)}) collective-permute-start(bf16[8,2176]{1,0:T(8,128)(2,1)S(1)} %get-tuple-element.27.refs_0_), channel_id=1, source_target_pairs={{0,2},{1,3},{2,0},{3,1},{4,6},{5,7},{6,4},{7,5},{8,10},{9,11},{10,... | collective-permute-start | bytes 104456 | tf_op jit(solution)/shard_map/ppermute | solution.py:326
  5.5 3.4 %collective-permute-start.5 = (bf16[8,2176]{1,0:T(8,128)(2,1)S(1)}, bf16[8,2176]{1,0:T(8,128)(2,1)S(1)}, u32[]{:S(2)}, u32[]{:S(2)}) collective-permute-start(bf16[8,2176]{1,0:T(8,128)(2,1)S(1)} %get-tuple-element.27.refs_0_), channel_id=1, source_target_pairs={{0,3},{1,2},{2,1},{3,0},{4,7},{5,6},{6,5},{7,4},{8,11},{9,10},{10,... | collective-permute-start | bytes 104456 | tf_op jit(solution)/shard_map/ppermute | solution.py:326
  9.0 6.1 %collective-permute-start.6 = (bf16[8,2304]{1,0:T(8,128)(2,1)S(1)}, bf16[8,2304]{1,0:T(8,128)(2,1)S(1)}, u32[]{:S(2)}, u32[]{:S(2)}) collective-permute-start(bf16[8,2304]{1,0:T(8,128)(2,1)S(1)} %get-tuple-element.29), channel_id=1, source_target_pairs={{0,4},{1,5},{2,6},{3,7},{4,0},{5,1},{6,2},{7,3},{8,12},{9,13},{10,... | collective-permute-start | bytes 110600 | tf_op jit(solution)/shard_map/ppermute | solution.py:326
  10.6 25.4 %collective-permute-start = (bf16[272,256]{1,0:T(8,128)(2,1)S(1)}, bf16[272,256]{1,0:T(8,128)(2,1)S(1)}, u32[]{:S(2)}, u32[]{:S(2)}) collective-permute-start(bf16[272,256]{1,0:T(8,128)(2,1)S(1)} %get-tuple-element.21.rows_ref.refs_0_), channel_id=1, source_target_pairs={{0,1},{1,0},{2,3},{3,2},{4,5},{5,4},{6,7},{7,6},{8,9},{9,8},{10,11... | collective-permute-start | bytes 417800 | tf_op jit(solution)/shard_map/ppermute | solution.py:326
  10.6 27.6 %collective-permute-start.1 = (bf16[272,256]{1,0:T(8,128)(2,1)S(1)}, bf16[272,256]{1,0:T(8,128)(2,1)S(1)}, u32[]{:S(2)}, u32[]{:S(2)}) collective-permute-start(bf16[272,256]{1,0:T(8,128)(2,1)S(1)} %get-tuple-element.21.rows_ref.refs_0_), channel_id=1, source_target_pairs={{0,2},{1,3},{2,0},{3,1},{4,6},{5,7},{6,4},{7,5},{8,10},{9,11},{10,... | collective-permute-start | bytes 417800 | tf_op jit(solution)/shard_map/ppermute | solution.py:326
  11.5 26.8 %collective-permute-start.2 = (bf16[272,256]{1,0:T(8,128)(2,1)S(1)}, bf16[272,256]{1,0:T(8,128)(2,1)S(1)}, u32[]{:S(2)}, u32[]{:S(2)}) collective-permute-start(bf16[272,256]{1,0:T(8,128)(2,1)S(1)} %get-tuple-element.21.rows_ref.refs_0_), channel_id=1, source_target_pairs={{0,3},{1,2},{2,1},{3,0},{4,7},{5,6},{6,5},{7,4},{8,11},{9,10},{10,... | collective-permute-start | bytes 417800 | tf_op jit(solution)/shard_map/ppermute | solution.py:326
  12.5 5.6 %collective-permute-start.7 = (bf16[8,2304]{1,0:T(8,128)(2,1)S(1)}, bf16[8,2304]{1,0:T(8,128)(2,1)S(1)}, u32[]{:S(2)}, u32[]{:S(2)}) collective-permute-start(bf16[8,2304]{1,0:T(8,128)(2,1)S(1)} %get-tuple-element.30), channel_id=1, source_target_pairs={{0,8},{1,9},{2,10},{3,11},{4,12},{5,13},{6,14},{7,15},{8,0},{9,1},... | collective-permute-start | bytes 110600 | tf_op jit(solution)/shard_map/ppermute | solution.py:326
  15.1 5.8 %collective-permute-start.8 = (bf16[8,2304]{1,0:T(8,128)(2,1)S(1)}, bf16[8,2304]{1,0:T(8,128)(2,1)S(1)}, u32[]{:S(2)}, u32[]{:S(2)}) collective-permute-start(bf16[8,2304]{1,0:T(8,128)(2,1)S(1)} %get-tuple-element.31), channel_id=1, source_target_pairs={{0,12},{1,13},{2,14},{3,15},{4,8},{5,9},{6,10},{7,11},{8,4},{9,5},... | collective-permute-start | bytes 110600 | tf_op jit(solution)/shard_map/ppermute | solution.py:326
  25.2 4.0 %collective-permute-start.9 = (f32[32,256]{1,0:T(8,128)S(1)}, f32[32,256]{1,0:T(8,128)S(1)}, u32[]{:S(2)}, u32[]{:S(2)}) collective-permute-start(f32[32,256]{1,0:T(8,128)S(1)} %get-tuple-element.34.refs_0_), channel_id=1, source_target_pairs={{0,4},{1,5},{2,6},{3,7},{4,0},{5,1},{6,2},{7,3},{8,12},{9,13},{10,... | collective-permute-start | bytes 98312 | tf_op jit(solution)/shard_map/ppermute | solution.py:326
  25.3 5.4 %collective-permute-start.10 = (f32[32,256]{1,0:T(8,128)S(1)}, f32[32,256]{1,0:T(8,128)S(1)}, u32[]{:S(2)}, u32[]{:S(2)}) collective-permute-start(f32[32,256]{1,0:T(8,128)S(1)} %get-tuple-element.34.refs_0_), channel_id=1, source_target_pairs={{0,8},{1,9},{2,10},{3,11},{4,12},{5,13},{6,14},{7,15},{8,0},{9,1},... | collective-permute-start | bytes 98312 | tf_op jit(solution)/shard_map/ppermute | solution.py:326
  29.2 5.7 %collective-permute-start.11 = (f32[32,256]{1,0:T(8,128)S(1)}, f32[32,256]{1,0:T(8,128)S(1)}, u32[]{:S(2)}, u32[]{:S(2)}) collective-permute-start(f32[32,256]{1,0:T(8,128)S(1)} %get-tuple-element.34.refs_0_), channel_id=1, source_target_pairs={{0,12},{1,13},{2,14},{3,15},{4,8},{5,9},{6,10},{7,11},{8,4},{9,5},... | collective-permute-start | bytes 98312 | tf_op jit(solution)/shard_map/ppermute | solution.py:326
  35.0 5.4 %collective-permute-start.12 = (f32[32,256]{1,0:T(8,128)S(1)}, f32[32,256]{1,0:T(8,128)S(1)}, u32[]{:S(2)}, u32[]{:S(2)}) collective-permute-start(f32[32,256]{1,0:T(8,128)S(1)} %get-tuple-element.36), channel_id=1, source_target_pairs={{0,1},{1,0},{2,3},{3,2},{4,5},{5,4},{6,7},{7,6},{8,9},{9,8},{10,11... | collective-permute-start | bytes 98312 | tf_op jit(solution)/shard_map/ppermute | solution.py:326
  35.0 5.3 %collective-permute-start.13 = (f32[32,256]{1,0:T(8,128)S(1)}, f32[32,256]{1,0:T(8,128)S(1)}, u32[]{:S(2)}, u32[]{:S(2)}) collective-permute-start(f32[32,256]{1,0:T(8,128)S(1)} %get-tuple-element.37), channel_id=1, source_target_pairs={{0,2},{1,3},{2,0},{3,1},{4,6},{5,7},{6,4},{7,5},{8,10},{9,11},{10,... | collective-permute-start | bytes 98312 | tf_op jit(solution)/shard_map/ppermute | solution.py:326
  36.0 4.4 %collective-permute-start.14 = (f32[32,256]{1,0:T(8,128)S(1)}, f32[32,256]{1,0:T(8,128)S(1)}, u32[]{:S(2)}, u32[]{:S(2)}) collective-permute-start(f32[32,256]{1,0:T(8,128)S(1)} %get-tuple-element.38), channel_id=1, source_target_pairs={{0,3},{1,2},{2,1},{3,0},{4,7},{5,6},{6,5},{7,4},{8,11},{9,10},{10,... | collective-permute-start | bytes 98312 | tf_op jit(solution)/shard_map/ppermute | solution.py:326

commit v4 on v3

--- a/solution.py
+++ b/solution.py
@@ -57,7 +57,7 @@
 
 
 def factor_kernel(seqs, res, *refs):
-    sources, (rows_ref, fac_ref, y_scr, *buffers, sems) = refs[:4], refs[4:]
+    sources, (rows_ref, left_ref, right_ref, y_scr, *buffers, sems) = refs[:4], refs[4:]
     get_x, get_left, get_right, get_mask = fetch(sources, buffers, sems)
     width = sources[1].shape[0]
     per = LANES // width
@@ -74,31 +74,26 @@
     keep_rep = dot(keep, spread_matrix(res, res * width, lambda c: c // width))
     segment = iota((seqs, LANES), 1) // width
     span = res * width
-    for side in range(2):
+    for side, ref in enumerate((left_ref, right_ref)):
         for group in range(res // per):
             value = None
             for k in range(per):
                 piece = y_scr.at[side][pl.ds(group * per + k, seqs, stride=res), :]
                 value = piece if value is None else jnp.where(segment == k, piece, value)
             lanes = slice(group * LANES, (group + 1) * LANES)
-            fac_ref[:, side * span + group * LANES : side * span + (group + 1) * LANES] = (
-                value * keep_rep[:, lanes]
-            ).astype(BF16)
-    fac_ref[:, 2 * span :] = keep_wide[:, :LANES].astype(BF16)
-
-
-def pick_kernel(count_a, count_b, span, *refs):
+            ref[:, lanes] = (value * keep_rep[:, lanes]).astype(BF16)
+    left_ref[:, span:] = keep_wide[:, :LANES].astype(BF16)
+
+
+def pick_kernel(count_a, count_b, span, right_ref, *refs):
     ins, outs, scr = refs[:count_b], refs[count_b : count_b + count_a], refs[-1]
     row, col = lax.axis_index("aa"), lax.axis_index("ba")
     for k in range(count_b):
         scr[lax.bitwise_xor(col, k)] = ins[k][...]
-    own = ins[0][...]
     for k in range(count_a):
-        theirs = scr[lax.bitwise_xor(row, k)]
-        outs[k][:, :span] = theirs[:, :span]
-        outs[k][:, span : 2 * span] = own[:, span : 2 * span]
-        outs[k][:, 2 * span : 2 * span + LANES] = theirs[:, 2 * span :]
-        outs[k][:, 2 * span + LANES :] = own[:, 2 * span :]
+        outs[k][:, : span + LANES] = scr[lax.bitwise_xor(row, k)]
+        outs[k][:, span + LANES : 2 * span + LANES] = right_ref[...]
+        outs[k][:, 2 * span + LANES :] = ins[0][:, span:]
 
 
 def spread_kernel(count_a, count_b, *refs):
@@ -129,12 +124,12 @@
     per = LANES // width
     msg = jnp.concatenate([m[...].astype(F32) for m in msgs], axis=0)
     left = msg[:, :span].astype(BF16)
-    keep_row = msg[:, 2 * span : 2 * span + res].astype(BF16)
+    keep_row = msg[:, span : span + res].astype(BF16)
     keep_col = msg[:, 2 * span + LANES : 2 * span + LANES + res].astype(BF16)
     seq_total = msg.shape[0]
     copies = max(1, LANES // seq_total)
     many = max(per, 256 // seq_total)
-    right = msg[:, span : 2 * span]
+    right = msg[:, span + LANES : 2 * span + LANES]
     for t in range(rt_scr.shape[0]):
         rt_scr[t] = jnp.concatenate([right[t * LANES : (t + 1) * LANES]] * copies, axis=0).T
     place = iota((res, LANES), 1) // seq_total
@@ -176,22 +171,19 @@
     wide = wrep_ref.shape[1]
     query = iota((res, wide), 1) % res
     pair = get_pair()
+    upd = dot(a_scr[...], wout_ref[...])
+    total = jnp.concatenate(
+        [
+            pair[i].astype(F32) + upd[i * res : (i + 1) * res] * inverse[:, i : i + 1]
+            for i in range(res)
+        ],
+        axis=0,
+    ).astype(BF16)
+    out_ref[...] = total.reshape(out_ref.shape)
+    spread = dot(layer_norm(total.astype(F32)).astype(BF16), wrep_ref[...])
     bias = jnp.zeros((res, wide), F32)
-    chunk = 8
-    for start in range(0, res, chunk):
-        upd = dot(a_scr[start * res : (start + chunk) * res, :], wout_ref[...])
-        total = jnp.concatenate(
-            [
-                pair[start + i].astype(F32)
-                + upd[i * res : (i + 1) * res] * inverse[:, start + i : start + i + 1]
-                for i in range(chunk)
-            ],
-            axis=0,
-        ).astype(BF16)
-        out_ref[start : start + chunk] = total.reshape(chunk, res, total.shape[1])
-        spread = dot(layer_norm(total.astype(F32)).astype(BF16), wrep_ref[...])
-        for i in range(chunk):
-            bias = jnp.where(query == start + i, spread[i * res : (i + 1) * res], bias)
+    for i in range(res):
+        bias = jnp.where(query == i, spread[i * res : (i + 1) * res], bias)
     bias_ref[...] = bias
 
 
@@ -248,29 +240,37 @@
         bias_scr[k * res : (k + 1) * res, :] = bias_refs[k][...]
     lane_head = iota((res, LANES), 1) // head_width
     diag = iota((res, wide), 0) == iota((res, wide), 1) % res
-    for s in range(seqs):
-        top = jnp.concatenate([limit_ref[s]] * (wide // LANES), axis=1)
-        scores = jnp.minimum(score_ref[s] + bias_scr[...], top)
-        raw = jnp.exp(scores - jnp.max(scores, axis=0, keepdims=True))
-        mass = jnp.sum(raw, axis=0, keepdims=True)
-        diag_scr[s * res : (s + 1) * res, :] = jnp.where(diag, 1.0 / mass, 0.0)
-        probs = raw.astype(BF16)
-        for u in range(channels // LANES):
-            lanes = slice(u * LANES, (u + 1) * LANES)
-            rows = slice(u * per * res, (u + 1) * per * res)
-            mixed = dot_tn(probs[:, rows], value_ref[s, :, lanes])
-            picked = mixed[:res]
-            for h in range(1, per):
-                picked = jnp.where(lane_head == h, mixed[h * res : (h + 1) * res], picked)
-            att_scr[s * res : (s + 1) * res, lanes] = picked
     head_pick = (iota((wide, channels), 0) // res == iota((wide, channels), 1) // head_width).astype(F32)
-    inverse = jnp.dot(
-        diag_scr[...], head_pick, preferred_element_type=F32, precision=lax.Precision.HIGHEST
-    )
-    gated = (att_scr[...] * inverse * gate_ref[...]).astype(BF16)
-    middle = get_x().astype(F32) + dot(gated, get_o())
-    hidden = jnp.maximum(dot(layer_norm(middle).astype(BF16), get_up()), 0.0).astype(BF16)
-    out_ref[...] = (middle + dot(hidden, get_down())).astype(BF16)
+    parts = 1
+    step = seqs // parts
+    for part in range(parts):
+        for s in range(part * step, (part + 1) * step):
+            top = jnp.concatenate([limit_ref[s]] * (wide // LANES), axis=1)
+            scores = jnp.minimum(score_ref[s] + bias_scr[...], top)
+            raw = jnp.exp(scores - jnp.max(scores, axis=0, keepdims=True))
+            mass = jnp.sum(raw, axis=0, keepdims=True)
+            diag_scr[s * res : (s + 1) * res, :] = jnp.where(diag, 1.0 / mass, 0.0)
+            probs = raw.astype(BF16)
+            for u in range(channels // LANES):
+                lanes = slice(u * LANES, (u + 1) * LANES)
+                block = slice(u * per * res, (u + 1) * per * res)
+                mixed = dot_tn(probs[:, block], value_ref[s, :, lanes])
+                picked = mixed[:res]
+                for h in range(1, per):
+                    picked = jnp.where(lane_head == h, mixed[h * res : (h + 1) * res], picked)
+                att_scr[s * res : (s + 1) * res, lanes] = picked
+        rows = slice(part * step * res, (part + 1) * step * res)
+        inverse = jnp.dot(
+            diag_scr[rows, :], head_pick, preferred_element_type=F32, precision=lax.Precision.HIGHEST
+        )
+        gated = (att_scr[rows, :] * inverse * gate_ref[rows, :]).astype(BF16)
+        if part == 0:
+            for wait in (get_x, get_o, get_up, get_down):
+                wait()
+            x_buf, (o_buf, up_buf, down_buf) = buffers[3], buffers[:3]
+        middle = x_buf[rows, :].astype(F32) + dot(gated, o_buf[...])
+        hidden = jnp.maximum(dot(layer_norm(middle).astype(BF16), up_buf[...]), 0.0).astype(BF16)
+        out_ref[rows, :] = (middle + dot(hidden, down_buf[...])).astype(BF16)
 
 
 def call(kernel, mib, outs, scratch=(), blocks=0, hbm=()):
@@ -334,25 +334,26 @@
     flat = alignment_state.reshape(seqs * res, channels)
     tail = -(-seqs // 16) * 16
     inputs = [flat, left_weight.T, right_weight.T, alignment_mask]
-    rows, factors = call(
+    rows, lefts, rights = call(
         functools.partial(factor_kernel, seqs, res),
         4,
         (
             shape((seqs * res + tail, channels), BF16),
-            shape((seqs, 2 * span + LANES), BF16),
+            shape((seqs, span + LANES), BF16),
+            shape((seqs, span), BF16),
         ),
         [pltpu.VMEM((2, seqs * res, LANES), F32)],
         0,
         inputs,
     )(*in_hbm(inputs))
 
-    blocks = [factors] + [along_b(factors, k) for k in range(1, count_b)]
+    blocks = [lefts] + [along_b(lefts, k) for k in range(1, count_b)]
     picked = call(
         functools.partial(pick_kernel, count_a, count_b, span),
         4,
         tuple(shape((seqs, 2 * span + 2 * LANES), BF16) for _ in range(count_a)),
-        [pltpu.VMEM((count_b, seqs, 2 * span + LANES), BF16)],
-    )(*blocks)
+        [pltpu.VMEM((count_b, seqs, span + LANES), BF16)],
+    )(rights, *blocks)
     msgs = [picked[0]] + [along_a(picked[k], k) for k in range(1, count_a)]
     all_rows = [rows] + [along_b(rows, k) for k in range(1, count_b)]
 

time: 44.6 us -> 43.8 us (0.982)
  Pallas kernels: 15.1 us -> 14.5 us
where the time goes in v4:
time: 43.8 us; the launch traced here: 43.5 us
  starting transfers between devices  16.4 us (37%)
  Pallas kernels  14.5 us (33%)
  waiting for transfers between devices  11.9 us (27%)
  between operations  0.76 us (2%)
    ppermute x15, starting transfers between devices, permute(): return lax.ppermute(value, ('aa', 'ba'), pairs)  16.4 us
    ppermute x15, waiting for transfers between devices, permute(): return lax.ppermute(value, ('aa', 'ba'), pairs)  11.9 us
    pallas_call x1, Pallas kernels, per_device(): call(functools.partial(pair_kernel, count_a, res, width), 16, (shape(pair...  4.02 us
    pallas_call x1, Pallas kernels, per_device(): call(functools.partial(attention_kernel, seqs, res, heads, count_b), 16,...  3.73 us
    pallas_call x1, Pallas kernels, per_device(): call(functools.partial(factor_kernel, seqs, res), 4, (shape((seqs * res +...  1.8 us
    pallas_call x1, Pallas kernels, per_device(): call(functools.partial(key_kernel, seqs, res, count_b), 8, (shape((seqs,...  1.61 us
    pallas_call x1, Pallas kernels, per_device(): call(functools.partial(order_kernel, res, width), 4, (shape(outer_output_...  1.5 us
    pallas_call x1, Pallas kernels, per_device(): call(functools.partial(query_kernel, seqs, res, heads), 4, (shape((seqs *...  1.36 us
  transfers between devices with their start and end apart: 15, of which 5 were waited for; matrix products, arithmetic and copies ran while one was open for 0% of the time, Pallas kernels for 21%

profile of v4, /device:TPU:0, one launch (start us, length us, event | category | flops | bytes accessed | tf_op | source)
XLA Modules:
  0.0 43.5 jit_solution(8082899175934668689)
XLA Ops:
  0.6 1.8 %shard_map.149 = (bf16[272,256]{1,0:T(8,128)(2,1)S(1)}, bf16[8,1152]{1,0:T(8,128)(2,1)S(1)}, bf16[8,1024]{1,0:T(8,128)(2,1)S(1)}) custom-call(bf16[256,256]{1,0:T(8,128)(2,1)} %bitcast.5, bf16[32,256]{1,0:T(8,128)(2,1)} %bitcast.8, bf16[32,256]{1,0:T(8,128)(2,1)} %bitcast.9, s32[8,32]{1,0:T(8,128)} %refs_3_.1), custom_call_target="tpu_custom_call" | custom-call | tf_op jit(solution)/shard_map/pallas_call | solution.py:337
  2.4 0.6 %collective-permute-start.3 = (bf16[8,1152]{1,0:T(8,128)(2,1)S(1)}, bf16[8,1152]{1,0:T(8,128)(2,1)S(1)}, u32[]{:S(2)}, u32[]{:S(2)}) collective-permute-start(bf16[8,1152]{1,0:T(8,128)(2,1)S(1)} %get-tuple-element.29.refs_0_), channel_id=1, source_target_pairs={{0,1},{1,0},{2,3},{3,2},{4,5},{5,4},{6,7},{7,6},{8,9},{9,8},{10,11... | collective-permute-start | bytes 55304 | tf_op jit(solution)/shard_map/ppermute | solution.py:326
  3.0 2.6 %collective-permute-start.4 = (bf16[8,1152]{1,0:T(8,128)(2,1)S(1)}, bf16[8,1152]{1,0:T(8,128)(2,1)S(1)}, u32[]{:S(2)}, u32[]{:S(2)}) collective-permute-start(bf16[8,1152]{1,0:T(8,128)(2,1)S(1)} %get-tuple-element.29.refs_0_), channel_id=1, source_target_pairs={{0,2},{1,3},{2,0},{3,1},{4,6},{5,7},{6,4},{7,5},{8,10},{9,11},{10,... | collective-permute-start | bytes 55304 | tf_op jit(solution)/shard_map/ppermute | solution.py:326
  5.5 0.0 collective-permute-start.5
  5.6 0.0 collective-permute-done.3.refs_1_
  5.6 1.7 %collective-permute-done.4.refs_2_ = bf16[8,1152]{1,0:T(8,128)(2,1)S(1)} collective-permute-done((bf16[8,1152]{1,0:T(8,128)(2,1)S(1)}, bf16[8,1152]{1,0:T(8,128)(2,1)S(1)}, u32[]{:S(2)}, u32[]{:S(2)}) %collective-permute-start.4) | collective-permute-done | bytes 18464 | tf_op jit(solution)/shard_map/ppermute | solution.py:326
  7.3 1.4 %collective-permute-done.5.refs_3_ = bf16[8,1152]{1,0:T(8,128)(2,1)S(1)} collective-permute-done((bf16[8,1152]{1,0:T(8,128)(2,1)S(1)}, bf16[8,1152]{1,0:T(8,128)(2,1)S(1)}, u32[]{:S(2)}, u32[]{:S(2)}) %collective-permute-start.5) | collective-permute-done | bytes 18464 | tf_op jit(solution)/shard_map/ppermute | solution.py:326
  8.8 1.6 %collective-permute-start.6 = (bf16[8,2304]{1,0:T(8,128)(2,1)S(1)}, bf16[8,2304]{1,0:T(8,128)(2,1)S(1)}, u32[]{:S(2)}, u32[]{:S(2)}) collective-permute-start(bf16[8,2304]{1,0:T(8,128)(2,1)S(1)} %get-tuple-element.31), channel_id=1, source_target_pairs={{0,4},{1,5},{2,6},{3,7},{4,0},{5,1},{6,2},{7,3},{8,12},{9,13},{10,... | collective-permute-start | bytes 110600 | tf_op jit(solution)/shard_map/ppermute | solution.py:326
  10.4 0.0 collective-permute-start
  10.4 0.7 %collective-permute-start.1 = (bf16[272,256]{1,0:T(8,128)(2,1)S(1)}, bf16[272,256]{1,0:T(8,128)(2,1)S(1)}, u32[]{:S(2)}, u32[]{:S(2)}) collective-permute-start(bf16[272,256]{1,0:T(8,128)(2,1)S(1)} %get-tuple-element.22.rows_ref.refs_0_), channel_id=1, source_target_pairs={{0,2},{1,3},{2,0},{3,1},{4,6},{5,7},{6,4},{7,5},{8,10},{9,11},{10,... | collective-permute-start | bytes 417800 | tf_op jit(solution)/shard_map/ppermute | solution.py:326
  11.1 1.1 %collective-permute-start.2 = (bf16[272,256]{1,0:T(8,128)(2,1)S(1)}, bf16[272,256]{1,0:T(8,128)(2,1)S(1)}, u32[]{:S(2)}, u32[]{:S(2)}) collective-permute-start(bf16[272,256]{1,0:T(8,128)(2,1)S(1)} %get-tuple-element.22.rows_ref.refs_0_), channel_id=1, source_target_pairs={{0,3},{1,2},{2,1},{3,0},{4,7},{5,6},{6,5},{7,4},{8,11},{9,10},{10,... | collective-permute-start | bytes 417800 | tf_op jit(solution)/shard_map/ppermute | solution.py:326
  12.3 2.6 %collective-permute-start.7 = (bf16[8,2304]{1,0:T(8,128)(2,1)S(1)}, bf16[8,2304]{1,0:T(8,128)(2,1)S(1)}, u32[]{:S(2)}, u32[]{:S(2)}) collective-permute-start(bf16[8,2304]{1,0:T(8,128)(2,1)S(1)} %get-tuple-element.32), channel_id=1, source_target_pairs={{0,8},{1,9},{2,10},{3,11},{4,12},{5,13},{6,14},{7,15},{8,0},{9,1},... | collective-permute-start | bytes 110600 | tf_op jit(solution)/shard_map/ppermute | solution.py:326
  14.9 0.0 collective-permute-done.6.refs_1_
  14.9 1.5 %collective-permute-start.8 = (bf16[8,2304]{1,0:T(8,128)(2,1)S(1)}, bf16[8,2304]{1,0:T(8,128)(2,1)S(1)}, u32[]{:S(2)}, u32[]{:S(2)}) collective-permute-start(bf16[8,2304]{1,0:T(8,128)(2,1)S(1)} %get-tuple-element.33), channel_id=1, source_target_pairs={{0,12},{1,13},{2,14},{3,15},{4,8},{5,9},{6,10},{7,11},{8,4},{9,5},... | collective-permute-start | bytes 110600 | tf_op jit(solution)/shard_map/ppermute | solution.py:326
  16.4 1.5 %shard_map.154 = (bf16[1024,128]{1,0:T(8,128)(2,1)S(1)}, bf16[128,256]{1,0:T(8,128)(2,1)S(1)}) custom-call(bf16[1024,128]{1,0:T(8,128)(2,1)} %refs_0_.1, bf16[8,128]{1,0:T(8,128)(2,1)} %bitcast.10), custom_call_target="tpu_custom_call" | custom-call | tf_op jit(solution)/shard_map/pallas_call | solution.py:362
  17.9 0.0 collective-permute-done.7.refs_2_
  17.9 2.7 %collective-permute-done.8.refs_3_ = bf16[8,2304]{1,0:T(8,128)(2,1)S(1)} collective-permute-done((bf16[8,2304]{1,0:T(8,128)(2,1)S(1)}, bf16[8,2304]{1,0:T(8,128)(2,1)S(1)}, u32[]{:S(2)}, u32[]{:S(2)}) %collective-permute-start.8) | collective-permute-done | bytes 36896 | tf_op jit(solution)/shard_map/ppermute | solution.py:326
  20.6 4.0 %shard_map.155 = (bf16[32,32,128]{2,1,0:T(8,128)(2,1)}, f32[32,256]{1,0:T(8,128)S(1)}) custom-call(bf16[8,2304]{1,0:T(8,128)(2,1)S(1)} %get-tuple-element.30.refs_0_, bf16[8,2304]{1,0:T(8,128)(2,1)S(1)} %collective-permute-done.6.refs_1_, bf16[8,2304]{1,0:T(8,128)(2,1)S(1)} %collective-permute-done.7.refs_2_, ...), custom_call_target="tpu_custom_call" | custom-call | tf_op jit(solution)/shard_map/pallas_call | solution.py:373
  24.6 0.1 collective-permute-start.9
  24.7 2.1 %collective-permute-start.10 = (f32[32,256]{1,0:T(8,128)S(1)}, f32[32,256]{1,0:T(8,128)S(1)}, u32[]{:S(2)}, u32[]{:S(2)}) collective-permute-start(f32[32,256]{1,0:T(8,128)S(1)} %get-tuple-element.36.refs_0_), channel_id=1, source_target_pairs={{0,8},{1,9},{2,10},{3,11},{4,12},{5,13},{6,14},{7,15},{8,0},{9,1},... | collective-permute-start | bytes 98312 | tf_op jit(solution)/shard_map/ppermute | solution.py:326
  26.8 1.8 %collective-permute-done.9.refs_1_ = f32[32,256]{1,0:T(8,128)S(1)} collective-permute-done((f32[32,256]{1,0:T(8,128)S(1)}, f32[32,256]{1,0:T(8,128)S(1)}, u32[]{:S(2)}, u32[]{:S(2)}) %collective-permute-start.9) | collective-permute-done | bytes 32800 | tf_op jit(solution)/shard_map/ppermute | solution.py:326
  28.6 1.5 %collective-permute-start.11 = (f32[32,256]{1,0:T(8,128)S(1)}, f32[32,256]{1,0:T(8,128)S(1)}, u32[]{:S(2)}, u32[]{:S(2)}) collective-permute-start(f32[32,256]{1,0:T(8,128)S(1)} %get-tuple-element.36.refs_0_), channel_id=1, source_target_pairs={{0,12},{1,13},{2,14},{3,15},{4,8},{5,9},{6,10},{7,11},{8,4},{9,5},... | collective-permute-start | bytes 98312 | tf_op jit(solution)/shard_map/ppermute | solution.py:326
  30.1 0.0 collective-permute-done.10.refs_2_
  30.2 4.2 %collective-permute-done.11.refs_3_ = f32[32,256]{1,0:T(8,128)S(1)} collective-permute-done((f32[32,256]{1,0:T(8,128)S(1)}, f32[32,256]{1,0:T(8,128)S(1)}, u32[]{:S(2)}, u32[]{:S(2)}) %collective-permute-start.11) | collective-permute-done | bytes 32800 | tf_op jit(solution)/shard_map/ppermute | solution.py:326
  34.4 0.1 collective-permute-start.12
  34.4 0.8 %collective-permute-start.13 = (f32[32,256]{1,0:T(8,128)S(1)}, f32[32,256]{1,0:T(8,128)S(1)}, u32[]{:S(2)}, u32[]{:S(2)}) collective-permute-start(f32[32,256]{1,0:T(8,128)S(1)} %get-tuple-element.39), channel_id=1, source_target_pairs={{0,2},{1,3},{2,0},{3,1},{4,6},{5,7},{6,4},{7,5},{8,10},{9,11},{10,... | collective-permute-start | bytes 98312 | tf_op jit(solution)/shard_map/ppermute | solution.py:326
  35.3 0.0 collective-permute-done.refs_1_
  35.3 1.0 %collective-permute-start.14 = (f32[32,256]{1,0:T(8,128)S(1)}, f32[32,256]{1,0:T(8,128)S(1)}, u32[]{:S(2)}, u32[]{:S(2)}) collective-permute-start(f32[32,256]{1,0:T(8,128)S(1)} %get-tuple-element.40), channel_id=1, source_target_pairs={{0,3},{1,2},{2,1},{3,0},{4,7},{5,6},{6,5},{7,4},{8,11},{9,10},{10,... | collective-permute-start | bytes 98312 | tf_op jit(solution)/shard_map/ppermute | solution.py:326
  36.3 1.4 %shard_map.150 = (bf16[256,256]{1,0:T(8,128)(2,1)S(1)}, f32[256,256]{1,0:T(8,128)S(1)}) custom-call(bf16[272,256]{1,0:T(8,128)(2,1)S(1)} %get-tuple-element.22.rows_ref.refs_0_, bf16[256,256]{1,0:T(8,128)(2,1)} %wq_hbm.1, bf16[256,256]{1,0:T(8,128)(2,1)} %wg_hbm.1), custom_call_target="tpu_custom_call" | custom-call | tf_op jit(solution)/shard_map/pallas_call | solution.py:386
  37.7 0.0 collective-permute-done.1.refs_2_
  37.7 0.0 collective-permute-done.2.refs_3_
  37.7 1.6 %shard_map.151 = (bf16[8,128,256]{2,1,0:T(8,128)(2,1)S(1)}, bf16[8,128,256]{2,1,0:T(8,128)(2,1)S(1)}, f32[8,128,128]{2,1,0:T(8,128)S(1)}) custom-call(bf16[272,256]{1,0:T(8,128)(2,1)S(1)} %get-tuple-element.22.rows_ref.refs_0_, bf16[272,256]{1,0:T(8,128)(2,1)S(1)} %collective-permute-done.refs_1_, bf16[272,256]{1,0:T(8,128)(2,1)S(1)} %collective-permute-done.1.refs_2_, ...), custom_call_target="tpu_custom_call" | custom-call | tf_op jit(solution)/shard_map/pallas_call | solution.py:396
  39.3 0.5 %shard_map.152.refs_0_ = f32[8,128,256]{2,1,0:T(8,128)S(1)} custom-call(bf16[256,256]{1,0:T(8,128)(2,1)S(1)} %get-tuple-element.23.query_ref, bf16[8,128,256]{2,1,0:T(8,128)(2,1)S(1)} %get-tuple-element.24.key_ref), custom_call_target="tpu_custom_call" | custom-call | tf_op jit(solution)/shard_map/pallas_call | solution.py:408
  39.8 0.0 collective-permute-done.12.refs_5_
  39.8 0.0 collective-permute-done.13.refs_6_
  39.8 0.0 collective-permute-done.14.refs_7_
  39.8 3.7 %shard_map.157 = bf16[256,256]{1,0:T(8,128)(2,1)} custom-call(f32[8,128,256]{2,1,0:T(8,128)S(1)} %shard_map.152.refs_0_, bf16[8,128,256]{2,1,0:T(8,128)(2,1)S(1)} %get-tuple-element.25.refs_1_, f32[8,128,128]{2,1,0:T(8,128)S(1)} %get-tuple-element.26.refs_2_, f32[256,256]{1,0:T(8,128)S(1)} %get-tuple-element.27.refs_3_, ...), custom_call_target="tpu_custom_call" | custom-call | tf_op jit(solution)/shard_map/pallas_call | solution.py:423
  (2 shorter events, 0.0 us)
Async XLA Ops:
  2.4 3.2 %collective-permute-start.3 = (bf16[8,1152]{1,0:T(8,128)(2,1)S(1)}, bf16[8,1152]{1,0:T(8,128)(2,1)S(1)}, u32[]{:S(2)}, u32[]{:S(2)}) collective-permute-start(bf16[8,1152]{1,0:T(8,128)(2,1)S(1)} %get-tuple-element.29.refs_0_), channel_id=1, source_target_pairs={{0,1},{1,0},{2,3},{3,2},{4,5},{5,4},{6,7},{7,6},{8,9},{9,8},{10,11... | collective-permute-start | bytes 55304 | tf_op jit(solution)/shard_map/ppermute | solution.py:326
  3.0 4.3 %collective-permute-start.4 = (bf16[8,1152]{1,0:T(8,128)(2,1)S(1)}, bf16[8,1152]{1,0:T(8,128)(2,1)S(1)}, u32[]{:S(2)}, u32[]{:S(2)}) collective-permute-start(bf16[8,1152]{1,0:T(8,128)(2,1)S(1)} %get-tuple-element.29.refs_0_), channel_id=1, source_target_pairs={{0,2},{1,3},{2,0},{3,1},{4,6},{5,7},{6,4},{7,5},{8,10},{9,11},{10,... | collective-permute-start | bytes 55304 | tf_op jit(solution)/shard_map/ppermute | solution.py:326
  5.5 3.2 %collective-permute-start.5 = (bf16[8,1152]{1,0:T(8,128)(2,1)S(1)}, bf16[8,1152]{1,0:T(8,128)(2,1)S(1)}, u32[]{:S(2)}, u32[]{:S(2)}) collective-permute-start(bf16[8,1152]{1,0:T(8,128)(2,1)S(1)} %get-tuple-element.29.refs_0_), channel_id=1, source_target_pairs={{0,3},{1,2},{2,1},{3,0},{4,7},{5,6},{6,5},{7,4},{8,11},{9,10},{10,... | collective-permute-start | bytes 55304 | tf_op jit(solution)/shard_map/ppermute | solution.py:326
  8.8 6.1 %collective-permute-start.6 = (bf16[8,2304]{1,0:T(8,128)(2,1)S(1)}, bf16[8,2304]{1,0:T(8,128)(2,1)S(1)}, u32[]{:S(2)}, u32[]{:S(2)}) collective-permute-start(bf16[8,2304]{1,0:T(8,128)(2,1)S(1)} %get-tuple-element.31), channel_id=1, source_target_pairs={{0,4},{1,5},{2,6},{3,7},{4,0},{5,1},{6,2},{7,3},{8,12},{9,13},{10,... | collective-permute-start | bytes 110600 | tf_op jit(solution)/shard_map/ppermute | solution.py:326
  10.4 24.9 %collective-permute-start = (bf16[272,256]{1,0:T(8,128)(2,1)S(1)}, bf16[272,256]{1,0:T(8,128)(2,1)S(1)}, u32[]{:S(2)}, u32[]{:S(2)}) collective-permute-start(bf16[272,256]{1,0:T(8,128)(2,1)S(1)} %get-tuple-element.22.rows_ref.refs_0_), channel_id=1, source_target_pairs={{0,1},{1,0},{2,3},{3,2},{4,5},{5,4},{6,7},{7,6},{8,9},{9,8},{10,11... | collective-permute-start | bytes 417800 | tf_op jit(solution)/shard_map/ppermute | solution.py:326
  10.4 27.3 %collective-permute-start.1 = (bf16[272,256]{1,0:T(8,128)(2,1)S(1)}, bf16[272,256]{1,0:T(8,128)(2,1)S(1)}, u32[]{:S(2)}, u32[]{:S(2)}) collective-permute-start(bf16[272,256]{1,0:T(8,128)(2,1)S(1)} %get-tuple-element.22.rows_ref.refs_0_), channel_id=1, source_target_pairs={{0,2},{1,3},{2,0},{3,1},{4,6},{5,7},{6,4},{7,5},{8,10},{9,11},{10,... | collective-permute-start | bytes 417800 | tf_op jit(solution)/shard_map/ppermute | solution.py:326
  11.1 26.5 %collective-permute-start.2 = (bf16[272,256]{1,0:T(8,128)(2,1)S(1)}, bf16[272,256]{1,0:T(8,128)(2,1)S(1)}, u32[]{:S(2)}, u32[]{:S(2)}) collective-permute-start(bf16[272,256]{1,0:T(8,128)(2,1)S(1)} %get-tuple-element.22.rows_ref.refs_0_), channel_id=1, source_target_pairs={{0,3},{1,2},{2,1},{3,0},{4,7},{5,6},{6,5},{7,4},{8,11},{9,10},{10,... | collective-permute-start | bytes 417800 | tf_op jit(solution)/shard_map/ppermute | solution.py:326
  12.3 5.6 %collective-permute-start.7 = (bf16[8,2304]{1,0:T(8,128)(2,1)S(1)}, bf16[8,2304]{1,0:T(8,128)(2,1)S(1)}, u32[]{:S(2)}, u32[]{:S(2)}) collective-permute-start(bf16[8,2304]{1,0:T(8,128)(2,1)S(1)} %get-tuple-element.32), channel_id=1, source_target_pairs={{0,8},{1,9},{2,10},{3,11},{4,12},{5,13},{6,14},{7,15},{8,0},{9,1},... | collective-permute-start | bytes 110600 | tf_op jit(solution)/shard_map/ppermute | solution.py:326
  14.9 5.8 %collective-permute-start.8 = (bf16[8,2304]{1,0:T(8,128)(2,1)S(1)}, bf16[8,2304]{1,0:T(8,128)(2,1)S(1)}, u32[]{:S(2)}, u32[]{:S(2)}) collective-permute-start(bf16[8,2304]{1,0:T(8,128)(2,1)S(1)} %get-tuple-element.33), channel_id=1, source_target_pairs={{0,12},{1,13},{2,14},{3,15},{4,8},{5,9},{6,10},{7,11},{8,4},{9,5},... | collective-permute-start | bytes 110600 | tf_op jit(solution)/shard_map/ppermute | solution.py:326
  24.6 4.0 %collective-permute-start.9 = (f32[32,256]{1,0:T(8,128)S(1)}, f32[32,256]{1,0:T(8,128)S(1)}, u32[]{:S(2)}, u32[]{:S(2)}) collective-permute-start(f32[32,256]{1,0:T(8,128)S(1)} %get-tuple-element.36.refs_0_), channel_id=1, source_target_pairs={{0,4},{1,5},{2,6},{3,7},{4,0},{5,1},{6,2},{7,3},{8,12},{9,13},{10,... | collective-permute-start | bytes 98312 | tf_op jit(solution)/shard_map/ppermute | solution.py:326
  24.7 5.4 %collective-permute-start.10 = (f32[32,256]{1,0:T(8,128)S(1)}, f32[32,256]{1,0:T(8,128)S(1)}, u32[]{:S(2)}, u32[]{:S(2)}) collective-permute-start(f32[32,256]{1,0:T(8,128)S(1)} %get-tuple-element.36.refs_0_), channel_id=1, source_target_pairs={{0,8},{1,9},{2,10},{3,11},{4,12},{5,13},{6,14},{7,15},{8,0},{9,1},... | collective-permute-start | bytes 98312 | tf_op jit(solution)/shard_map/ppermute | solution.py:326
  28.6 5.7 %collective-permute-start.11 = (f32[32,256]{1,0:T(8,128)S(1)}, f32[32,256]{1,0:T(8,128)S(1)}, u32[]{:S(2)}, u32[]{:S(2)}) collective-permute-start(f32[32,256]{1,0:T(8,128)S(1)} %get-tuple-element.36.refs_0_), channel_id=1, source_target_pairs={{0,12},{1,13},{2,14},{3,15},{4,8},{5,9},{6,10},{7,11},{8,4},{9,5},... | collective-permute-start | bytes 98312 | tf_op jit(solution)/shard_map/ppermute | solution.py:326
  34.4 5.4 %collective-permute-start.12 = (f32[32,256]{1,0:T(8,128)S(1)}, f32[32,256]{1,0:T(8,128)S(1)}, u32[]{:S(2)}, u32[]{:S(2)}) collective-permute-start(f32[32,256]{1,0:T(8,128)S(1)} %get-tuple-element.38), channel_id=1, source_target_pairs={{0,1},{1,0},{2,3},{3,2},{4,5},{5,4},{6,7},{7,6},{8,9},{9,8},{10,11... | collective-permute-start | bytes 98312 | tf_op jit(solution)/shard_map/ppermute | solution.py:326
  34.4 5.3 %collective-permute-start.13 = (f32[32,256]{1,0:T(8,128)S(1)}, f32[32,256]{1,0:T(8,128)S(1)}, u32[]{:S(2)}, u32[]{:S(2)}) collective-permute-start(f32[32,256]{1,0:T(8,128)S(1)} %get-tuple-element.39), channel_id=1, source_target_pairs={{0,2},{1,3},{2,0},{3,1},{4,6},{5,7},{6,4},{7,5},{8,10},{9,11},{10,... | collective-permute-start | bytes 98312 | tf_op jit(solution)/shard_map/ppermute | solution.py:326
  35.3 4.5 %collective-permute-start.14 = (f32[32,256]{1,0:T(8,128)S(1)}, f32[32,256]{1,0:T(8,128)S(1)}, u32[]{:S(2)}, u32[]{:S(2)}) collective-permute-start(f32[32,256]{1,0:T(8,128)S(1)} %get-tuple-element.40), channel_id=1, source_target_pairs={{0,3},{1,2},{2,1},{3,0},{4,7},{5,6},{6,5},{7,4},{8,11},{9,10},{10,... | collective-permute-start | bytes 98312 | tf_op jit(solution)/shard_map/ppermute | solution.py:326

commit v5 on v4

--- a/solution.py
+++ b/solution.py
@@ -213,7 +213,12 @@
             limit_ref[s, k * res : (k + 1) * res, :] = keep[:, s * LANES : (s + 1) * LANES]
 
 
-def score_kernel(seqs, res, heads, query_ref, key_ref, score_ref):
+def score_kernel(seqs, res, heads, query_ref, key_ref, *refs):
+    count = (len(refs) - 2) // 2
+    sources, score_ref, kept, sems = refs[:count], refs[count], refs[count + 1 : -1], refs[-1]
+    copies = [pltpu.make_async_copy(x, y, sems.at[n]) for n, (x, y) in enumerate(zip(sources, kept))]
+    for copy in copies:
+        copy.start()
     channels = query_ref.shape[1]
     wide = heads * res
     same_head = iota((wide, channels), 0) // res == iota((wide, channels), 1) // (channels // heads)
@@ -224,14 +229,14 @@
             jnp.zeros((), BF16),
         )
         score_ref[s] = dot_nt(key_ref[s], query_wide)
+    for copy in copies:
+        copy.wait()
 
 
 def attention_kernel(seqs, res, heads, count_b, *refs):
     score_ref, value_ref, limit_ref, gate_ref = refs[:4]
     bias_refs, refs = refs[4 : 4 + count_b], refs[4 + count_b :]
-    sources, out_ref, refs = refs[:4], refs[4], refs[5:]
-    bias_scr, att_scr, diag_scr, *buffers, sems = refs
-    get_o, get_up, get_down, get_x = fetch(sources, buffers, sems)
+    wo_ref, up_ref, down_ref, x_ref, out_ref, bias_scr, att_scr, diag_scr = refs
     channels = out_ref.shape[1]
     head_width = channels // heads
     wide = heads * res
@@ -240,37 +245,31 @@
         bias_scr[k * res : (k + 1) * res, :] = bias_refs[k][...]
     lane_head = iota((res, LANES), 1) // head_width
     diag = iota((res, wide), 0) == iota((res, wide), 1) % res
-    head_pick = (iota((wide, channels), 0) // res == iota((wide, channels), 1) // head_width).astype(F32)
-    parts = 1
-    step = seqs // parts
-    for part in range(parts):
-        for s in range(part * step, (part + 1) * step):
-            top = jnp.concatenate([limit_ref[s]] * (wide // LANES), axis=1)
-            scores = jnp.minimum(score_ref[s] + bias_scr[...], top)
-            raw = jnp.exp(scores - jnp.max(scores, axis=0, keepdims=True))
-            mass = jnp.sum(raw, axis=0, keepdims=True)
-            diag_scr[s * res : (s + 1) * res, :] = jnp.where(diag, 1.0 / mass, 0.0)
-            probs = raw.astype(BF16)
-            for u in range(channels // LANES):
-                lanes = slice(u * LANES, (u + 1) * LANES)
-                block = slice(u * per * res, (u + 1) * per * res)
-                mixed = dot_tn(probs[:, block], value_ref[s, :, lanes])
-                picked = mixed[:res]
-                for h in range(1, per):
-                    picked = jnp.where(lane_head == h, mixed[h * res : (h + 1) * res], picked)
-                att_scr[s * res : (s + 1) * res, lanes] = picked
-        rows = slice(part * step * res, (part + 1) * step * res)
-        inverse = jnp.dot(
-            diag_scr[rows, :], head_pick, preferred_element_type=F32, precision=lax.Precision.HIGHEST
-        )
-        gated = (att_scr[rows, :] * inverse * gate_ref[rows, :]).astype(BF16)
-        if part == 0:
-            for wait in (get_x, get_o, get_up, get_down):
-                wait()
-            x_buf, (o_buf, up_buf, down_buf) = buffers[3], buffers[:3]
-        middle = x_buf[rows, :].astype(F32) + dot(gated, o_buf[...])
-        hidden = jnp.maximum(dot(layer_norm(middle).astype(BF16), up_buf[...]), 0.0).astype(BF16)
-        out_ref[rows, :] = (middle + dot(hidden, down_buf[...])).astype(BF16)
+    head_pick = (iota((wide, channels), 0) // res == iota((wide, channels), 1) // head_width).astype(F32).astype(BF16)
+    for s in range(seqs):
+        top = jnp.concatenate([limit_ref[s]] * (wide // LANES), axis=1)
+        scores = jnp.minimum(score_ref[s] + bias_scr[...], top)
+        raw = jnp.exp(scores - jnp.max(scores, axis=0, keepdims=True))
+        mass = jnp.sum(raw, axis=0, keepdims=True)
+        diag_scr[s * res : (s + 1) * res, :] = jnp.where(diag, 1.0 / mass, 0.0)
+        probs = raw.astype(BF16)
+        for u in range(channels // LANES):
+            lanes = slice(u * LANES, (u + 1) * LANES)
+            block = slice(u * per * res, (u + 1) * per * res)
+            mixed = dot_tn(probs[:, block], value_ref[s, :, lanes])
+            picked = mixed[:res]
+            for h in range(1, per):
+                picked = jnp.where(lane_head == h, mixed[h * res : (h + 1) * res], picked)
+            att_scr[s * res : (s + 1) * res, lanes] = picked
+    rest, inverse = diag_scr[...], 0.0
+    for _ in range(3):
+        piece = rest.astype(BF16)
+        inverse = inverse + dot(piece, head_pick)
+        rest = rest - piece.astype(F32)
+    gated = (att_scr[...] * inverse * gate_ref[...]).astype(BF16)
+    middle = x_ref[...].astype(F32) + dot(gated, wo_ref[...])
+    hidden = jnp.maximum(dot(layer_norm(middle).astype(BF16), up_ref[...]), 0.0).astype(BF16)
+    out_ref[...] = (middle + dot(hidden, down_ref[...])).astype(BF16)
 
 
 def call(kernel, mib, outs, scratch=(), blocks=0, hbm=()):
@@ -405,11 +404,16 @@
         count_b,
         weights,
     )(*all_rows, *in_hbm(weights))
-    (scores,) = call(
+    weights = [output_weight, up_weight, down_weight, flat]
+    vmem_spec = pl.BlockSpec(memory_space=pltpu.VMEM)
+    scores, *kept = pl.pallas_call(
         functools.partial(score_kernel, seqs, res, heads),
-        8,
-        (shape((seqs, keys, heads * res), F32),),
-    )(query, key)
+        in_specs=[vmem_spec] * 2 + [pl.BlockSpec(memory_space=pltpu.HBM)] * len(weights),
+        out_shape=(shape((seqs, keys, heads * res), F32),)
+        + tuple(shape(w.shape, w.dtype) for w in weights),
+        scratch_shapes=[pltpu.SemaphoreType.DMA((len(weights),))],
+        compiler_params=pltpu.CompilerParams(vmem_limit_bytes=8 * MIB),
+    )(query, key, *in_hbm(weights))
 
     tiles = [bias] + [along_a(bias, k) for k in range(1, count_a)]
     biases = call(
@@ -419,7 +423,6 @@
         [pltpu.VMEM((count_a,) + bias.shape, F32)],
     )(*tiles)
     biases = [biases[0]] + [along_b(biases[k], k) for k in range(1, count_b)]
-    weights = [output_weight, up_weight, down_weight, flat]
     (out,) = call(
         functools.partial(attention_kernel, seqs, res, heads, count_b),
         16,
@@ -429,9 +432,7 @@
             pltpu.VMEM((seqs * res, channels), F32),
             pltpu.VMEM((seqs * res, heads * res), F32),
         ],
-        4 + count_b,
-        weights,
-    )(scores, value, limit, gate, *biases, *in_hbm(weights))
+    )(scores, value, limit, gate, *biases, *kept)
     return (out.reshape(seqs, res, channels), pair_output)
 
 

time: 43.8 us -> 43.3 us (0.989)
  Pallas kernels: 14.5 us -> 14 us
    pallas_call x1, Pallas kernels: 3.73 us -> 2.11 us  [per_device(): call(functools.partial(attention_kernel, seqs, res, heads, count_b), 16,...]
    pallas_call x1, Pallas kernels: 0.46 us -> 1.58 us  [per_device(): pl.pallas_call(functools.partial(score_kernel, seqs, res, heads), in_spec...]
  transfers between devices with their start and end apart: 15 -> 15, of which waited for: 5 -> 5; matrix products, arithmetic and copies ran while one was open for 0% -> 0% of each run, Pallas kernels for 21% -> 23%
where the time goes in v5:
time: 43.3 us; the launch traced here: 43 us
  starting transfers between devices  16.4 us (38%)
  Pallas kernels  14 us (32%)
  waiting for transfers between devices  11.9 us (27%)
  between operations  0.76 us (2%)
    ppermute x15, starting transfers between devices, permute(): return lax.ppermute(value, ('aa', 'ba'), pairs)  16.4 us
    ppermute x15, waiting for transfers between devices, permute(): return lax.ppermute(value, ('aa', 'ba'), pairs)  11.9 us
    pallas_call x1, Pallas kernels, per_device(): call(functools.partial(pair_kernel, count_a, res, width), 16, (shape(pair...  4.02 us
    pallas_call x1, Pallas kernels, per_device(): call(functools.partial(attention_kernel, seqs, res, heads, count_b), 16,...  2.11 us
    pallas_call x1, Pallas kernels, per_device(): call(functools.partial(factor_kernel, seqs, res), 4, (shape((seqs * res +...  1.8 us
    pallas_call x1, Pallas kernels, per_device(): call(functools.partial(key_kernel, seqs, res, count_b), 8, (shape((seqs,...  1.61 us
    pallas_call x1, Pallas kernels, per_device(): pl.pallas_call(functools.partial(score_kernel, seqs, res, heads), in_spec...  1.58 us
    pallas_call x1, Pallas kernels, per_device(): call(functools.partial(order_kernel, res, width), 4, (shape(outer_output_...  1.5 us
  transfers between devices with their start and end apart: 15, of which 5 were waited for; matrix products, arithmetic and copies ran while one was open for 0% of the time, Pallas kernels for 23%

profile of v5, /device:TPU:0, one launch (start us, length us, event | category | flops | bytes accessed | tf_op | source)
XLA Modules:
  0.0 43.0 jit_solution(6181060421517597807)
XLA Ops:
  0.6 1.8 %shard_map.149 = (bf16[272,256]{1,0:T(8,128)(2,1)S(1)}, bf16[8,1152]{1,0:T(8,128)(2,1)S(1)}, bf16[8,1024]{1,0:T(8,128)(2,1)S(1)}) custom-call(bf16[256,256]{1,0:T(8,128)(2,1)} %bitcast.5, bf16[32,256]{1,0:T(8,128)(2,1)} %bitcast.8, bf16[32,256]{1,0:T(8,128)(2,1)} %bitcast.9, s32[8,32]{1,0:T(8,128)} %refs_3_.1), custom_call_target="tpu_custom_call" | custom-call | tf_op jit(solution)/shard_map/pallas_call | solution.py:336
  2.4 0.6 %collective-permute-start.3 = (bf16[8,1152]{1,0:T(8,128)(2,1)S(1)}, bf16[8,1152]{1,0:T(8,128)(2,1)S(1)}, u32[]{:S(2)}, u32[]{:S(2)}) collective-permute-start(bf16[8,1152]{1,0:T(8,128)(2,1)S(1)} %get-tuple-element.35.refs_0_), channel_id=1, source_target_pairs={{0,1},{1,0},{2,3},{3,2},{4,5},{5,4},{6,7},{7,6},{8,9},{9,8},{10,11... | collective-permute-start | bytes 55304 | tf_op jit(solution)/shard_map/ppermute | solution.py:325
  3.0 2.6 %collective-permute-start.4 = (bf16[8,1152]{1,0:T(8,128)(2,1)S(1)}, bf16[8,1152]{1,0:T(8,128)(2,1)S(1)}, u32[]{:S(2)}, u32[]{:S(2)}) collective-permute-start(bf16[8,1152]{1,0:T(8,128)(2,1)S(1)} %get-tuple-element.35.refs_0_), channel_id=1, source_target_pairs={{0,2},{1,3},{2,0},{3,1},{4,6},{5,7},{6,4},{7,5},{8,10},{9,11},{10,... | collective-permute-start | bytes 55304 | tf_op jit(solution)/shard_map/ppermute | solution.py:325
  5.5 0.0 collective-permute-start.5
  5.6 0.0 collective-permute-done.3.refs_1_
  5.6 1.7 %collective-permute-done.4.refs_2_ = bf16[8,1152]{1,0:T(8,128)(2,1)S(1)} collective-permute-done((bf16[8,1152]{1,0:T(8,128)(2,1)S(1)}, bf16[8,1152]{1,0:T(8,128)(2,1)S(1)}, u32[]{:S(2)}, u32[]{:S(2)}) %collective-permute-start.4) | collective-permute-done | bytes 18464 | tf_op jit(solution)/shard_map/ppermute | solution.py:325
  7.3 1.4 %collective-permute-done.5.refs_3_ = bf16[8,1152]{1,0:T(8,128)(2,1)S(1)} collective-permute-done((bf16[8,1152]{1,0:T(8,128)(2,1)S(1)}, bf16[8,1152]{1,0:T(8,128)(2,1)S(1)}, u32[]{:S(2)}, u32[]{:S(2)}) %collective-permute-start.5) | collective-permute-done | bytes 18464 | tf_op jit(solution)/shard_map/ppermute | solution.py:325
  8.8 1.6 %collective-permute-start.6 = (bf16[8,2304]{1,0:T(8,128)(2,1)S(1)}, bf16[8,2304]{1,0:T(8,128)(2,1)S(1)}, u32[]{:S(2)}, u32[]{:S(2)}) collective-permute-start(bf16[8,2304]{1,0:T(8,128)(2,1)S(1)} %get-tuple-element.37), channel_id=1, source_target_pairs={{0,4},{1,5},{2,6},{3,7},{4,0},{5,1},{6,2},{7,3},{8,12},{9,13},{10,... | collective-permute-start | bytes 110600 | tf_op jit(solution)/shard_map/ppermute | solution.py:325
  10.4 0.0 collective-permute-start
  10.4 0.7 %collective-permute-start.1 = (bf16[272,256]{1,0:T(8,128)(2,1)S(1)}, bf16[272,256]{1,0:T(8,128)(2,1)S(1)}, u32[]{:S(2)}, u32[]{:S(2)}) collective-permute-start(bf16[272,256]{1,0:T(8,128)(2,1)S(1)} %get-tuple-element.27.rows_ref.refs_0_), channel_id=1, source_target_pairs={{0,2},{1,3},{2,0},{3,1},{4,6},{5,7},{6,4},{7,5},{8,10},{9,11},{10,... | collective-permute-start | bytes 417800 | tf_op jit(solution)/shard_map/ppermute | solution.py:325
  11.1 1.1 %collective-permute-start.2 = (bf16[272,256]{1,0:T(8,128)(2,1)S(1)}, bf16[272,256]{1,0:T(8,128)(2,1)S(1)}, u32[]{:S(2)}, u32[]{:S(2)}) collective-permute-start(bf16[272,256]{1,0:T(8,128)(2,1)S(1)} %get-tuple-element.27.rows_ref.refs_0_), channel_id=1, source_target_pairs={{0,3},{1,2},{2,1},{3,0},{4,7},{5,6},{6,5},{7,4},{8,11},{9,10},{10,... | collective-permute-start | bytes 417800 | tf_op jit(solution)/shard_map/ppermute | solution.py:325
  12.3 2.6 %collective-permute-start.7 = (bf16[8,2304]{1,0:T(8,128)(2,1)S(1)}, bf16[8,2304]{1,0:T(8,128)(2,1)S(1)}, u32[]{:S(2)}, u32[]{:S(2)}) collective-permute-start(bf16[8,2304]{1,0:T(8,128)(2,1)S(1)} %get-tuple-element.38), channel_id=1, source_target_pairs={{0,8},{1,9},{2,10},{3,11},{4,12},{5,13},{6,14},{7,15},{8,0},{9,1},... | collective-permute-start | bytes 110600 | tf_op jit(solution)/shard_map/ppermute | solution.py:325
  14.9 0.0 collective-permute-done.6.refs_1_
  14.9 1.5 %collective-permute-start.8 = (bf16[8,2304]{1,0:T(8,128)(2,1)S(1)}, bf16[8,2304]{1,0:T(8,128)(2,1)S(1)}, u32[]{:S(2)}, u32[]{:S(2)}) collective-permute-start(bf16[8,2304]{1,0:T(8,128)(2,1)S(1)} %get-tuple-element.39), channel_id=1, source_target_pairs={{0,12},{1,13},{2,14},{3,15},{4,8},{5,9},{6,10},{7,11},{8,4},{9,5},... | collective-permute-start | bytes 110600 | tf_op jit(solution)/shard_map/ppermute | solution.py:325
  16.4 1.5 %shard_map.154 = (bf16[1024,128]{1,0:T(8,128)(2,1)S(1)}, bf16[128,256]{1,0:T(8,128)(2,1)S(1)}) custom-call(bf16[1024,128]{1,0:T(8,128)(2,1)} %refs_0_.3, bf16[8,128]{1,0:T(8,128)(2,1)} %bitcast.10), custom_call_target="tpu_custom_call" | custom-call | tf_op jit(solution)/shard_map/pallas_call | solution.py:361
  17.9 0.0 collective-permute-done.7.refs_2_
  17.9 2.7 %collective-permute-done.8.refs_3_ = bf16[8,2304]{1,0:T(8,128)(2,1)S(1)} collective-permute-done((bf16[8,2304]{1,0:T(8,128)(2,1)S(1)}, bf16[8,2304]{1,0:T(8,128)(2,1)S(1)}, u32[]{:S(2)}, u32[]{:S(2)}) %collective-permute-start.8) | collective-permute-done | bytes 36896 | tf_op jit(solution)/shard_map/ppermute | solution.py:325
  20.6 4.0 %shard_map.155 = (bf16[32,32,128]{2,1,0:T(8,128)(2,1)}, f32[32,256]{1,0:T(8,128)S(1)}) custom-call(bf16[8,2304]{1,0:T(8,128)(2,1)S(1)} %get-tuple-element.36.refs_0_, bf16[8,2304]{1,0:T(8,128)(2,1)S(1)} %collective-permute-done.6.refs_1_, bf16[8,2304]{1,0:T(8,128)(2,1)S(1)} %collective-permute-done.7.refs_2_, ...), custom_call_target="tpu_custom_call" | custom-call | tf_op jit(solution)/shard_map/pallas_call | solution.py:372
  24.6 0.1 collective-permute-start.9
  24.7 2.1 %collective-permute-start.10 = (f32[32,256]{1,0:T(8,128)S(1)}, f32[32,256]{1,0:T(8,128)S(1)}, u32[]{:S(2)}, u32[]{:S(2)}) collective-permute-start(f32[32,256]{1,0:T(8,128)S(1)} %get-tuple-element.42.refs_0_), channel_id=1, source_target_pairs={{0,8},{1,9},{2,10},{3,11},{4,12},{5,13},{6,14},{7,15},{8,0},{9,1},... | collective-permute-start | bytes 98312 | tf_op jit(solution)/shard_map/ppermute | solution.py:325
  26.8 1.8 %collective-permute-done.9.refs_1_ = f32[32,256]{1,0:T(8,128)S(1)} collective-permute-done((f32[32,256]{1,0:T(8,128)S(1)}, f32[32,256]{1,0:T(8,128)S(1)}, u32[]{:S(2)}, u32[]{:S(2)}) %collective-permute-start.9) | collective-permute-done | bytes 32800 | tf_op jit(solution)/shard_map/ppermute | solution.py:325
  28.6 1.5 %collective-permute-start.11 = (f32[32,256]{1,0:T(8,128)S(1)}, f32[32,256]{1,0:T(8,128)S(1)}, u32[]{:S(2)}, u32[]{:S(2)}) collective-permute-start(f32[32,256]{1,0:T(8,128)S(1)} %get-tuple-element.42.refs_0_), channel_id=1, source_target_pairs={{0,12},{1,13},{2,14},{3,15},{4,8},{5,9},{6,10},{7,11},{8,4},{9,5},... | collective-permute-start | bytes 98312 | tf_op jit(solution)/shard_map/ppermute | solution.py:325
  30.1 0.0 collective-permute-done.10.refs_2_
  30.2 4.2 %collective-permute-done.11.refs_3_ = f32[32,256]{1,0:T(8,128)S(1)} collective-permute-done((f32[32,256]{1,0:T(8,128)S(1)}, f32[32,256]{1,0:T(8,128)S(1)}, u32[]{:S(2)}, u32[]{:S(2)}) %collective-permute-start.11) | collective-permute-done | bytes 32800 | tf_op jit(solution)/shard_map/ppermute | solution.py:325
  34.4 0.1 collective-permute-start.12
  34.4 0.8 %collective-permute-start.13 = (f32[32,256]{1,0:T(8,128)S(1)}, f32[32,256]{1,0:T(8,128)S(1)}, u32[]{:S(2)}, u32[]{:S(2)}) collective-permute-start(f32[32,256]{1,0:T(8,128)S(1)} %get-tuple-element.45), channel_id=1, source_target_pairs={{0,2},{1,3},{2,0},{3,1},{4,6},{5,7},{6,4},{7,5},{8,10},{9,11},{10,... | collective-permute-start | bytes 98312 | tf_op jit(solution)/shard_map/ppermute | solution.py:325
  35.3 0.0 collective-permute-done.refs_1_
  35.3 1.0 %collective-permute-start.14 = (f32[32,256]{1,0:T(8,128)S(1)}, f32[32,256]{1,0:T(8,128)S(1)}, u32[]{:S(2)}, u32[]{:S(2)}) collective-permute-start(f32[32,256]{1,0:T(8,128)S(1)} %get-tuple-element.46), channel_id=1, source_target_pairs={{0,3},{1,2},{2,1},{3,0},{4,7},{5,6},{6,5},{7,4},{8,11},{9,10},{10,... | collective-permute-start | bytes 98312 | tf_op jit(solution)/shard_map/ppermute | solution.py:325
  36.3 1.4 %shard_map.150 = (bf16[256,256]{1,0:T(8,128)(2,1)S(1)}, f32[256,256]{1,0:T(8,128)S(1)}) custom-call(bf16[272,256]{1,0:T(8,128)(2,1)S(1)} %get-tuple-element.27.rows_ref.refs_0_, bf16[256,256]{1,0:T(8,128)(2,1)} %wq_hbm.1, bf16[256,256]{1,0:T(8,128)(2,1)} %wg_hbm.1), custom_call_target="tpu_custom_call" | custom-call | tf_op jit(solution)/shard_map/pallas_call | solution.py:385
  37.7 0.0 collective-permute-done.1.refs_2_
  37.7 0.0 collective-permute-done.2.refs_3_
  37.7 1.6 %shard_map.151 = (bf16[8,128,256]{2,1,0:T(8,128)(2,1)S(1)}, bf16[8,128,256]{2,1,0:T(8,128)(2,1)S(1)}, f32[8,128,128]{2,1,0:T(8,128)S(1)}) custom-call(bf16[272,256]{1,0:T(8,128)(2,1)S(1)} %get-tuple-element.27.rows_ref.refs_0_, bf16[272,256]{1,0:T(8,128)(2,1)S(1)} %collective-permute-done.refs_1_, bf16[272,256]{1,0:T(8,128)(2,1)S(1)} %collective-permute-done.1.refs_2_, ...), custom_call_target="tpu_custom_call" | custom-call | tf_op jit(solution)/shard_map/pallas_call | solution.py:395
  39.3 1.6 %shard_map.152 = (f32[8,128,256]{2,1,0:T(8,128)S(1)}, bf16[256,256]{1,0:T(8,128)(2,1)S(1)}, bf16[256,1024]{1,0:T(8,128)(2,1)S(1)}, bf16[1024,256]{1,0:T(8,128)(2,1)S(1)}, bf16[256,256]{1,0:T(8,128)(2,1)S(1)}) custom-call(bf16[256,256]{1,0:T(8,128)(2,1)S(1)} %get-tuple-element.28.query_ref, bf16[8,128,256]{2,1,0:T(8,128)(2,1)S(1)} %get-tuple-element.29.key_ref, ...), custom_call_target="tpu_custom_call" | custom-call | tf_op jit(solution)/shard_map/pallas_call | solution.py:409
  40.9 0.0 collective-permute-done.12.refs_5_
  40.9 0.0 collective-permute-done.13.refs_6_
  40.9 0.0 collective-permute-done.14.refs_7_
  40.9 2.1 %shard_map.157 = bf16[256,256]{1,0:T(8,128)(2,1)} custom-call(f32[8,128,256]{2,1,0:T(8,128)S(1)} %get-tuple-element.30.refs_0_, bf16[8,128,256]{2,1,0:T(8,128)(2,1)S(1)} %get-tuple-element.31.refs_1_, f32[8,128,128]{2,1,0:T(8,128)S(1)} %get-tuple-element.32.refs_2_, f32[256,256]{1,0:T(8,128)S(1)} %get-tuple-element.33.refs_3_, ...), custom_call_target="tpu_custom_call" | custom-call | tf_op jit(solution)/shard_map/pallas_call | solution.py:426
  (2 shorter events, 0.0 us)
Async XLA Ops:
  2.4 3.2 %collective-permute-start.3 = (bf16[8,1152]{1,0:T(8,128)(2,1)S(1)}, bf16[8,1152]{1,0:T(8,128)(2,1)S(1)}, u32[]{:S(2)}, u32[]{:S(2)}) collective-permute-start(bf16[8,1152]{1,0:T(8,128)(2,1)S(1)} %get-tuple-element.35.refs_0_), channel_id=1, source_target_pairs={{0,1},{1,0},{2,3},{3,2},{4,5},{5,4},{6,7},{7,6},{8,9},{9,8},{10,11... | collective-permute-start | bytes 55304 | tf_op jit(solution)/shard_map/ppermute | solution.py:325
  3.0 4.3 %collective-permute-start.4 = (bf16[8,1152]{1,0:T(8,128)(2,1)S(1)}, bf16[8,1152]{1,0:T(8,128)(2,1)S(1)}, u32[]{:S(2)}, u32[]{:S(2)}) collective-permute-start(bf16[8,1152]{1,0:T(8,128)(2,1)S(1)} %get-tuple-element.35.refs_0_), channel_id=1, source_target_pairs={{0,2},{1,3},{2,0},{3,1},{4,6},{5,7},{6,4},{7,5},{8,10},{9,11},{10,... | collective-permute-start | bytes 55304 | tf_op jit(solution)/shard_map/ppermute | solution.py:325
  5.5 3.2 %collective-permute-start.5 = (bf16[8,1152]{1,0:T(8,128)(2,1)S(1)}, bf16[8,1152]{1,0:T(8,128)(2,1)S(1)}, u32[]{:S(2)}, u32[]{:S(2)}) collective-permute-start(bf16[8,1152]{1,0:T(8,128)(2,1)S(1)} %get-tuple-element.35.refs_0_), channel_id=1, source_target_pairs={{0,3},{1,2},{2,1},{3,0},{4,7},{5,6},{6,5},{7,4},{8,11},{9,10},{10,... | collective-permute-start | bytes 55304 | tf_op jit(solution)/shard_map/ppermute | solution.py:325
  8.8 6.1 %collective-permute-start.6 = (bf16[8,2304]{1,0:T(8,128)(2,1)S(1)}, bf16[8,2304]{1,0:T(8,128)(2,1)S(1)}, u32[]{:S(2)}, u32[]{:S(2)}) collective-permute-start(bf16[8,2304]{1,0:T(8,128)(2,1)S(1)} %get-tuple-element.37), channel_id=1, source_target_pairs={{0,4},{1,5},{2,6},{3,7},{4,0},{5,1},{6,2},{7,3},{8,12},{9,13},{10,... | collective-permute-start | bytes 110600 | tf_op jit(solution)/shard_map/ppermute | solution.py:325
  10.4 24.9 %collective-permute-start = (bf16[272,256]{1,0:T(8,128)(2,1)S(1)}, bf16[272,256]{1,0:T(8,128)(2,1)S(1)}, u32[]{:S(2)}, u32[]{:S(2)}) collective-permute-start(bf16[272,256]{1,0:T(8,128)(2,1)S(1)} %get-tuple-element.27.rows_ref.refs_0_), channel_id=1, source_target_pairs={{0,1},{1,0},{2,3},{3,2},{4,5},{5,4},{6,7},{7,6},{8,9},{9,8},{10,11... | collective-permute-start | bytes 417800 | tf_op jit(solution)/shard_map/ppermute | solution.py:325
  10.4 27.3 %collective-permute-start.1 = (bf16[272,256]{1,0:T(8,128)(2,1)S(1)}, bf16[272,256]{1,0:T(8,128)(2,1)S(1)}, u32[]{:S(2)}, u32[]{:S(2)}) collective-permute-start(bf16[272,256]{1,0:T(8,128)(2,1)S(1)} %get-tuple-element.27.rows_ref.refs_0_), channel_id=1, source_target_pairs={{0,2},{1,3},{2,0},{3,1},{4,6},{5,7},{6,4},{7,5},{8,10},{9,11},{10,... | collective-permute-start | bytes 417800 | tf_op jit(solution)/shard_map/ppermute | solution.py:325
  11.1 26.5 %collective-permute-start.2 = (bf16[272,256]{1,0:T(8,128)(2,1)S(1)}, bf16[272,256]{1,0:T(8,128)(2,1)S(1)}, u32[]{:S(2)}, u32[]{:S(2)}) collective-permute-start(bf16[272,256]{1,0:T(8,128)(2,1)S(1)} %get-tuple-element.27.rows_ref.refs_0_), channel_id=1, source_target_pairs={{0,3},{1,2},{2,1},{3,0},{4,7},{5,6},{6,5},{7,4},{8,11},{9,10},{10,... | collective-permute-start | bytes 417800 | tf_op jit(solution)/shard_map/ppermute | solution.py:325
  12.3 5.6 %collective-permute-start.7 = (bf16[8,2304]{1,0:T(8,128)(2,1)S(1)}, bf16[8,2304]{1,0:T(8,128)(2,1)S(1)}, u32[]{:S(2)}, u32[]{:S(2)}) collective-permute-start(bf16[8,2304]{1,0:T(8,128)(2,1)S(1)} %get-tuple-element.38), channel_id=1, source_target_pairs={{0,8},{1,9},{2,10},{3,11},{4,12},{5,13},{6,14},{7,15},{8,0},{9,1},... | collective-permute-start | bytes 110600 | tf_op jit(solution)/shard_map/ppermute | solution.py:325
  14.9 5.8 %collective-permute-start.8 = (bf16[8,2304]{1,0:T(8,128)(2,1)S(1)}, bf16[8,2304]{1,0:T(8,128)(2,1)S(1)}, u32[]{:S(2)}, u32[]{:S(2)}) collective-permute-start(bf16[8,2304]{1,0:T(8,128)(2,1)S(1)} %get-tuple-element.39), channel_id=1, source_target_pairs={{0,12},{1,13},{2,14},{3,15},{4,8},{5,9},{6,10},{7,11},{8,4},{9,5},... | collective-permute-start | bytes 110600 | tf_op jit(solution)/shard_map/ppermute | solution.py:325
  24.6 4.0 %collective-permute-start.9 = (f32[32,256]{1,0:T(8,128)S(1)}, f32[32,256]{1,0:T(8,128)S(1)}, u32[]{:S(2)}, u32[]{:S(2)}) collective-permute-start(f32[32,256]{1,0:T(8,128)S(1)} %get-tuple-element.42.refs_0_), channel_id=1, source_target_pairs={{0,4},{1,5},{2,6},{3,7},{4,0},{5,1},{6,2},{7,3},{8,12},{9,13},{10,... | collective-permute-start | bytes 98312 | tf_op jit(solution)/shard_map/ppermute | solution.py:325
  24.7 5.4 %collective-permute-start.10 = (f32[32,256]{1,0:T(8,128)S(1)}, f32[32,256]{1,0:T(8,128)S(1)}, u32[]{:S(2)}, u32[]{:S(2)}) collective-permute-start(f32[32,256]{1,0:T(8,128)S(1)} %get-tuple-element.42.refs_0_), channel_id=1, source_target_pairs={{0,8},{1,9},{2,10},{3,11},{4,12},{5,13},{6,14},{7,15},{8,0},{9,1},... | collective-permute-start | bytes 98312 | tf_op jit(solution)/shard_map/ppermute | solution.py:325
  28.6 5.7 %collective-permute-start.11 = (f32[32,256]{1,0:T(8,128)S(1)}, f32[32,256]{1,0:T(8,128)S(1)}, u32[]{:S(2)}, u32[]{:S(2)}) collective-permute-start(f32[32,256]{1,0:T(8,128)S(1)} %get-tuple-element.42.refs_0_), channel_id=1, source_target_pairs={{0,12},{1,13},{2,14},{3,15},{4,8},{5,9},{6,10},{7,11},{8,4},{9,5},... | collective-permute-start | bytes 98312 | tf_op jit(solution)/shard_map/ppermute | solution.py:325
  34.4 6.5 %collective-permute-start.12 = (f32[32,256]{1,0:T(8,128)S(1)}, f32[32,256]{1,0:T(8,128)S(1)}, u32[]{:S(2)}, u32[]{:S(2)}) collective-permute-start(f32[32,256]{1,0:T(8,128)S(1)} %get-tuple-element.44), channel_id=1, source_target_pairs={{0,1},{1,0},{2,3},{3,2},{4,5},{5,4},{6,7},{7,6},{8,9},{9,8},{10,11... | collective-permute-start | bytes 98312 | tf_op jit(solution)/shard_map/ppermute | solution.py:325
  34.4 6.5 %collective-permute-start.13 = (f32[32,256]{1,0:T(8,128)S(1)}, f32[32,256]{1,0:T(8,128)S(1)}, u32[]{:S(2)}, u32[]{:S(2)}) collective-permute-start(f32[32,256]{1,0:T(8,128)S(1)} %get-tuple-element.45), channel_id=1, source_target_pairs={{0,2},{1,3},{2,0},{3,1},{4,6},{5,7},{6,4},{7,5},{8,10},{9,11},{10,... | collective-permute-start | bytes 98312 | tf_op jit(solution)/shard_map/ppermute | solution.py:325
  35.3 5.6 %collective-permute-start.14 = (f32[32,256]{1,0:T(8,128)S(1)}, f32[32,256]{1,0:T(8,128)S(1)}, u32[]{:S(2)}, u32[]{:S(2)}) collective-permute-start(f32[32,256]{1,0:T(8,128)S(1)} %get-tuple-element.46), channel_id=1, source_target_pairs={{0,3},{1,2},{2,1},{3,0},{4,7},{5,6},{6,5},{7,4},{8,11},{9,10},{10,... | collective-permute-start | bytes 98312 | tf_op jit(solution)/shard_map/ppermute | solution.py:325

commit v6 on v5

--- a/solution.py
+++ b/solution.py
@@ -58,42 +58,56 @@
 
 def factor_kernel(seqs, res, *refs):
     sources, (rows_ref, left_ref, right_ref, y_scr, *buffers, sems) = refs[:4], refs[4:]
-    get_x, get_left, get_right, get_mask = fetch(sources, buffers, sems)
-    width = sources[1].shape[0]
+    get_left, get_right, get_mask, get_x = fetch(sources, buffers, sems)
+    width = sources[0].shape[0]
+    lanes = right_ref.shape[1]
     per = LANES // width
-    normed = layer_norm(get_x().astype(F32)).astype(BF16)
     keep = (get_mask() > 0).astype(F32).astype(BF16)
-    rows_ref[: seqs * res, :] = normed
     tail = rows_ref.shape[0] - seqs * res
-    keep_wide = dot(keep, spread_matrix(res, rows_ref.shape[1], lambda c: c))
+    keep_wide = dot(keep, spread_matrix(res, rows_ref.shape[1], lambda c: c % LANES))
     rows_ref[seqs * res :, :] = jnp.concatenate(
         [keep_wide, jnp.zeros((tail - seqs, rows_ref.shape[1]), F32)], axis=0
     ).astype(BF16)
-    y_scr[0] = dot_nt(normed, jnp.concatenate([get_left()] * per, axis=0))
-    y_scr[1] = dot_nt(normed, jnp.concatenate([get_right()] * per, axis=0))
     keep_rep = dot(keep, spread_matrix(res, res * width, lambda c: c // width))
+    keep_turned = dot_tn(keep, spread_matrix(seqs, lanes, lambda c: c % seqs))
+    w_left = jnp.concatenate([get_left()] * per, axis=0)
+    repeat = (iota((lanes, width), 0) // seqs == iota((lanes, width), 1)).astype(F32).astype(BF16)
+    w_right = dot(repeat, get_right()).astype(BF16)
+    normed = layer_norm(get_x().astype(F32)).astype(BF16)
+    rows_ref[: seqs * res, :] = normed
+    y_scr[...] = dot_nt(normed, w_left)
+    made = dot_nt(normed, w_right)
+    own = iota((res, lanes), 1) % seqs
+    right = made[:res]
+    for s in range(1, seqs):
+        right = jnp.where(own == s, made[s * res : (s + 1) * res], right)
+    right_ref[...] = (right * keep_turned).astype(BF16)
     segment = iota((seqs, LANES), 1) // width
     span = res * width
-    for side, ref in enumerate((left_ref, right_ref)):
-        for group in range(res // per):
+    for part in range(lanes // LANES):
+        pieces = []
+        for group in range(part, span // LANES, lanes // LANES):
             value = None
             for k in range(per):
-                piece = y_scr.at[side][pl.ds(group * per + k, seqs, stride=res), :]
+                piece = y_scr[pl.ds(group * per + k, seqs, stride=res), :]
                 value = piece if value is None else jnp.where(segment == k, piece, value)
-            lanes = slice(group * LANES, (group + 1) * LANES)
-            ref[:, lanes] = (value * keep_rep[:, lanes]).astype(BF16)
-    left_ref[:, span:] = keep_wide[:, :LANES].astype(BF16)
-
-
-def pick_kernel(count_a, count_b, span, right_ref, *refs):
+            pieces.append(value * keep_rep[:, group * LANES : (group + 1) * LANES])
+        pieces.append(keep_wide[:, :LANES])
+        left_ref[:, part * LANES : (part + 1) * LANES] = jnp.concatenate(pieces, axis=0).astype(BF16)
+
+
+def pick_kernel(count_a, count_b, seqs, right_ref, *refs):
     ins, outs, scr = refs[:count_b], refs[count_b : count_b + count_a], refs[-1]
     row, col = lax.axis_index("aa"), lax.axis_index("ba")
     for k in range(count_b):
         scr[lax.bitwise_xor(col, k)] = ins[k][...]
+    res, first = right_ref.shape[0], ins[0].shape[0] - seqs
     for k in range(count_a):
-        outs[k][:, : span + LANES] = scr[lax.bitwise_xor(row, k)]
-        outs[k][:, span + LANES : 2 * span + LANES] = right_ref[...]
-        outs[k][:, 2 * span + LANES :] = ins[0][:, span:]
+        theirs = scr[lax.bitwise_xor(row, k)]
+        outs[k][:first, :] = theirs[:first]
+        outs[k][first : first + res, :] = right_ref[...]
+        outs[k][first + res :, :LANES] = theirs[first:, :LANES]
+        outs[k][first + res :, LANES:] = ins[0][first:, LANES:]
 
 
 def spread_kernel(count_a, count_b, *refs):
@@ -118,51 +132,59 @@
 
 def pair_kernel(count_a, res, width, *refs):
     msgs = refs[:count_a]
-    wout_ref, wrep_ref, pair_hbm, out_ref, bias_ref, rt_scr, a_scr, pair_buf, sems = refs[count_a:]
+    wout_ref, wrep_ref, pair_hbm, out_hbm, bias_ref, a_scr, out_buf, pair_buf, sems = refs[count_a:]
     (get_pair,) = fetch([pair_hbm], [pair_buf], sems)
     span = res * width
     per = LANES // width
-    msg = jnp.concatenate([m[...].astype(F32) for m in msgs], axis=0)
-    left = msg[:, :span].astype(BF16)
-    keep_row = msg[:, span : span + res].astype(BF16)
-    keep_col = msg[:, 2 * span + LANES : 2 * span + LANES + res].astype(BF16)
-    seq_total = msg.shape[0]
-    copies = max(1, LANES // seq_total)
-    many = max(per, 256 // seq_total)
-    right = msg[:, span + LANES : 2 * span + LANES]
-    for t in range(rt_scr.shape[0]):
-        rt_scr[t] = jnp.concatenate([right[t * LANES : (t + 1) * LANES]] * copies, axis=0).T
-    place = iota((res, LANES), 1) // seq_total
+    lanes = msgs[0].shape[1]
+    seqs = lanes // width
+    first = span // lanes * seqs
+    many = LANES // (2 * seqs)
+    keeps = jnp.concatenate([m[first + res :, :].astype(F32) for m in msgs], axis=0).astype(BF16)
+    keep_row, keep_col = keeps[:, :res], keeps[:, LANES : LANES + res]
+    low = iota((res, LANES), 1) < many * seqs
     streams = []
-    for first in range(0, width, many):
+    for start in range(0, width, many):
+        at = start * seqs // LANES * LANES
         tiles = []
-        for d in range(first, first + many, copies):
-            for t in range(rt_scr.shape[0]):
-                tile = rt_scr.at[t][pl.ds(d, res, stride=width), :]
-                for k in range(1, copies):
-                    other = rt_scr.at[t][pl.ds(d + k, res, stride=width), :]
-                    tile = jnp.where(place == k, other, tile)
-                tiles.append(tile.astype(BF16))
+        for n in range(0, count_a, 2):
+            one, two = (m[first : first + res, at : at + LANES] for m in msgs[n : n + 2])
+            if start * seqs == at:
+                tiles.append(jnp.where(low, one, pltpu.roll(two, LANES // 2, 1)))
+            else:
+                tiles.append(jnp.where(low, pltpu.roll(one, LANES // 2, 1), two))
         streams.append(jnp.concatenate(tiles, axis=1))
     streams = jnp.concatenate(streams, axis=0)
-    segment = iota((seq_total, LANES), 1) // width
-    zero = jnp.zeros((seq_total, LANES), BF16)
+    half = iota((2 * seqs, LANES), 0) // seqs
+    segment = iota((2 * seqs, LANES), 1) // width
+    here = [(segment == d) & (half == d % 2) for d in range(per)]
+    zero = jnp.zeros((2 * seqs, LANES), BF16)
+    lefts = [m[:first, :].astype(F32) for m in msgs]
     for i in range(res):
         group, k = i // per, i % per
-        only = jnp.where(segment == k, left[:, group * LANES : (group + 1) * LANES], zero)
-        moved = [
-            only if d == k else pltpu.roll(only, ((d - k) % per) * width, 1) for d in range(per)
-        ]
-        diagonal = jnp.concatenate(
-            [
-                jnp.concatenate(
-                    [moved[d % per] if u == d // per else zero for u in range(many // per)], axis=1
+        if k == 0:
+            p, at = group * LANES // lanes, group * LANES % lanes
+            turned = []
+            for left in lefts:
+                tile = left[p * seqs : (p + 1) * seqs, at : at + LANES]
+                tile = jnp.concatenate([tile, tile], axis=0).astype(BF16)
+                turned.append([tile] + [pltpu.roll(tile, r * width, 1) for r in range(1, per)])
+        rows = []
+        for turn in turned:
+            pairs = [
+                jnp.where(
+                    here[d], turn[(d - k) % per], jnp.where(here[d + 1], turn[(d + 1 - k) % per], zero)
                 )
-                for d in range(many)
-            ],
-            axis=0,
-        )
-        prod = dot(streams, diagonal).astype(BF16)
+                for d in range(0, per, 2)
+            ]
+            for d in range(0, many, 2):
+                rows.append(
+                    jnp.concatenate(
+                        [pairs[d % per // 2] if u == d // per else zero for u in range(many // per)],
+                        axis=1,
+                    )
+                )
+        prod = dot(streams, jnp.concatenate(rows, axis=0)).astype(BF16)
         for n in range(width // many):
             a_scr[i * res : (i + 1) * res, n * many * width : (n + 1) * many * width] = prod[
                 n * res : (n + 1) * res
@@ -179,12 +201,15 @@
         ],
         axis=0,
     ).astype(BF16)
-    out_ref[...] = total.reshape(out_ref.shape)
+    out_buf[...] = total.reshape(out_buf.shape)
+    out_copy = pltpu.make_async_copy(out_buf, out_hbm, sems.at[1])
+    out_copy.start()
     spread = dot(layer_norm(total.astype(F32)).astype(BF16), wrep_ref[...])
     bias = jnp.zeros((res, wide), F32)
     for i in range(res):
         bias = jnp.where(query == i, spread[i * res : (i + 1) * res], bias)
     bias_ref[...] = bias
+    out_copy.wait()
 
 
 def query_kernel(seqs, res, heads, rows_ref, wq_hbm, wg_hbm, query_ref, gate_ref, *scratch):
@@ -272,13 +297,12 @@
     out_ref[...] = (middle + dot(hidden, down_ref[...])).astype(BF16)
 
 
-def call(kernel, mib, outs, scratch=(), blocks=0, hbm=()):
-    specs = {}
+def call(kernel, mib, outs, scratch=(), blocks=0, hbm=(), more_sems=0, **specs):
     if hbm:
         vmem_spec = pl.BlockSpec(memory_space=pltpu.VMEM)
         specs["in_specs"] = [vmem_spec] * blocks + [pl.BlockSpec(memory_space=pltpu.HBM)] * len(hbm)
         scratch = list(scratch) + [pltpu.VMEM(h.shape, h.dtype) for h in hbm]
-        scratch.append(pltpu.SemaphoreType.DMA((len(hbm),)))
+        scratch.append(pltpu.SemaphoreType.DMA((len(hbm) + more_sems,)))
     return pl.pallas_call(
         kernel,
         out_shape=outs,
@@ -314,6 +338,7 @@
     width = left_weight.shape[1]
     heads = pair_bias_weight.shape[1]
     span = res * width
+    wide = width * seqs
     shape = jax.ShapeDtypeStruct
 
     def permute(value, target):
@@ -332,31 +357,30 @@
 
     flat = alignment_state.reshape(seqs * res, channels)
     tail = -(-seqs // 16) * 16
-    inputs = [flat, left_weight.T, right_weight.T, alignment_mask]
+    inputs = [left_weight.T, right_weight.T, alignment_mask, flat]
     rows, lefts, rights = call(
         functools.partial(factor_kernel, seqs, res),
         4,
         (
             shape((seqs * res + tail, channels), BF16),
-            shape((seqs, span + LANES), BF16),
-            shape((seqs, span), BF16),
+            shape((seqs * (span // wide + 1), wide), BF16),
+            shape((res, wide), BF16),
         ),
-        [pltpu.VMEM((2, seqs * res, LANES), F32)],
+        [pltpu.VMEM((seqs * res, LANES), F32)],
         0,
         inputs,
     )(*in_hbm(inputs))
 
     blocks = [lefts] + [along_b(lefts, k) for k in range(1, count_b)]
     picked = call(
-        functools.partial(pick_kernel, count_a, count_b, span),
+        functools.partial(pick_kernel, count_a, count_b, seqs),
         4,
-        tuple(shape((seqs, 2 * span + 2 * LANES), BF16) for _ in range(count_a)),
-        [pltpu.VMEM((count_b, seqs, span + LANES), BF16)],
+        tuple(shape((lefts.shape[0] + res, wide), BF16) for _ in range(count_a)),
+        [pltpu.VMEM((count_b,) + lefts.shape, BF16)],
     )(rights, *blocks)
     msgs = [picked[0]] + [along_a(picked[k], k) for k in range(1, count_a)]
     all_rows = [rows] + [along_b(rows, k) for k in range(1, count_b)]
 
-    seq_total = seqs * count_a
     weights = [outer_output_weight, pair_bias_weight.T]
     w_out, w_rep = call(
         functools.partial(order_kernel, res, width),
@@ -374,11 +398,16 @@
         16,
         (shape(pair_state.shape, BF16), shape((res, heads * res), F32)),
         [
-            pltpu.VMEM((pl.cdiv(seq_total, LANES), span, LANES), F32),
             pltpu.VMEM((res * res, width * width), BF16),
+            pltpu.VMEM(pair_state.shape, BF16),
         ],
         count_a + 2,
         [pair_state],
+        1,
+        out_specs=(
+            pl.BlockSpec(memory_space=pltpu.HBM),
+            pl.BlockSpec(memory_space=pltpu.VMEM),
+        ),
     )(*msgs, w_out, w_rep, *in_hbm([pair_state]))
 
     weights = [query_weight, gate_weight]

time: 43.3 us -> 42.7 us (0.986)
  Pallas kernels: 14 us -> 13.5 us
where the time goes in v6:
time: 42.7 us; the launch traced here: 42.5 us
  starting transfers between devices  16.4 us (38%)
  Pallas kernels  13.5 us (32%)
  waiting for transfers between devices  11.9 us (28%)
  between operations  0.76 us (2%)
    ppermute x15, starting transfers between devices, permute(): return lax.ppermute(value, ('aa', 'ba'), pairs)  16.4 us
    ppermute x15, waiting for transfers between devices, permute(): return lax.ppermute(value, ('aa', 'ba'), pairs)  11.9 us
    pallas_call x1, Pallas kernels, per_device(): call(functools.partial(pair_kernel, count_a, res, width), 16, (shape(pair...  3.65 us
    pallas_call x1, Pallas kernels, per_device(): call(functools.partial(attention_kernel, seqs, res, heads, count_b), 16,...  2.11 us
    pallas_call x1, Pallas kernels, per_device(): call(functools.partial(key_kernel, seqs, res, count_b), 8, (shape((seqs,...  1.61 us
    pallas_call x1, Pallas kernels, per_device(): call(functools.partial(factor_kernel, seqs, res), 4, (shape((seqs * res +...  1.6 us
    pallas_call x1, Pallas kernels, per_device(): pl.pallas_call(functools.partial(score_kernel, seqs, res, heads), in_spec...  1.58 us
    pallas_call x1, Pallas kernels, per_device(): call(functools.partial(order_kernel, res, width), 4, (shape(outer_output_...  1.5 us
  transfers between devices with their start and end apart: 15, of which 5 were waited for; matrix products, arithmetic and copies ran while one was open for 0% of the time, Pallas kernels for 23%

profile of v6, /device:TPU:0, one launch (start us, length us, event | category | flops | bytes accessed | tf_op | source)
XLA Modules:
  0.0 42.5 jit_solution(15151908073955749042)
XLA Ops:
  0.6 1.6 %shard_map.149 = (bf16[272,256]{1,0:T(8,128)(2,1)S(1)}, bf16[40,256]{1,0:T(8,128)(2,1)S(1)}, bf16[32,256]{1,0:T(8,128)(2,1)S(1)}) custom-call(bf16[32,256]{1,0:T(8,128)(2,1)} %bitcast.8, bf16[32,256]{1,0:T(8,128)(2,1)} %bitcast.9, s32[8,32]{1,0:T(8,128)} %refs_2_.2, bf16[256,256]{1,0:T(8,128)(2,1)} %bitcast.5), custom_call_target="tpu_custom_call" | custom-call | tf_op jit(solution)/shard_map/pallas_call | solution.py:361
  2.2 0.6 %collective-permute-start.3 = (bf16[40,256]{1,0:T(8,128)(2,1)S(1)}, bf16[40,256]{1,0:T(8,128)(2,1)S(1)}, u32[]{:S(2)}, u32[]{:S(2)}) collective-permute-start(bf16[40,256]{1,0:T(8,128)(2,1)S(1)} %get-tuple-element.35.refs_0_), channel_id=1, source_target_pairs={{0,1},{1,0},{2,3},{3,2},{4,5},{5,4},{6,7},{7,6},{8,9},{9,8},{10,11... | collective-permute-start | bytes 61448 | tf_op jit(solution)/shard_map/ppermute | solution.py:350
  2.8 2.6 %collective-permute-start.4 = (bf16[40,256]{1,0:T(8,128)(2,1)S(1)}, bf16[40,256]{1,0:T(8,128)(2,1)S(1)}, u32[]{:S(2)}, u32[]{:S(2)}) collective-permute-start(bf16[40,256]{1,0:T(8,128)(2,1)S(1)} %get-tuple-element.35.refs_0_), channel_id=1, source_target_pairs={{0,2},{1,3},{2,0},{3,1},{4,6},{5,7},{6,4},{7,5},{8,10},{9,11},{10,... | collective-permute-start | bytes 61448 | tf_op jit(solution)/shard_map/ppermute | solution.py:350
  5.3 0.0 collective-permute-start.5
  5.4 0.0 collective-permute-done.3.refs_1_
  5.4 1.7 %collective-permute-done.4.refs_2_ = bf16[40,256]{1,0:T(8,128)(2,1)S(1)} collective-permute-done((bf16[40,256]{1,0:T(8,128)(2,1)S(1)}, bf16[40,256]{1,0:T(8,128)(2,1)S(1)}, u32[]{:S(2)}, u32[]{:S(2)}) %collective-permute-start.4) | collective-permute-done | bytes 20512 | tf_op jit(solution)/shard_map/ppermute | solution.py:350
  7.1 1.4 %collective-permute-done.5.refs_3_ = bf16[40,256]{1,0:T(8,128)(2,1)S(1)} collective-permute-done((bf16[40,256]{1,0:T(8,128)(2,1)S(1)}, bf16[40,256]{1,0:T(8,128)(2,1)S(1)}, u32[]{:S(2)}, u32[]{:S(2)}) %collective-permute-start.5) | collective-permute-done | bytes 20512 | tf_op jit(solution)/shard_map/ppermute | solution.py:350
  8.6 1.6 %collective-permute-start.6 = (bf16[72,256]{1,0:T(8,128)(2,1)S(1)}, bf16[72,256]{1,0:T(8,128)(2,1)S(1)}, u32[]{:S(2)}, u32[]{:S(2)}) collective-permute-start(bf16[72,256]{1,0:T(8,128)(2,1)S(1)} %get-tuple-element.37), channel_id=1, source_target_pairs={{0,4},{1,5},{2,6},{3,7},{4,0},{5,1},{6,2},{7,3},{8,12},{9,13},{10,... | collective-permute-start | bytes 110600 | tf_op jit(solution)/shard_map/ppermute | solution.py:350
  10.2 0.0 collective-permute-start
  10.2 0.8 %collective-permute-start.1 = (bf16[272,256]{1,0:T(8,128)(2,1)S(1)}, bf16[272,256]{1,0:T(8,128)(2,1)S(1)}, u32[]{:S(2)}, u32[]{:S(2)}) collective-permute-start(bf16[272,256]{1,0:T(8,128)(2,1)S(1)} %get-tuple-element.27.rows_ref.refs_0_), channel_id=1, source_target_pairs={{0,2},{1,3},{2,0},{3,1},{4,6},{5,7},{6,4},{7,5},{8,10},{9,11},{10,... | collective-permute-start | bytes 417800 | tf_op jit(solution)/shard_map/ppermute | solution.py:350
  11.0 1.1 %collective-permute-start.2 = (bf16[272,256]{1,0:T(8,128)(2,1)S(1)}, bf16[272,256]{1,0:T(8,128)(2,1)S(1)}, u32[]{:S(2)}, u32[]{:S(2)}) collective-permute-start(bf16[272,256]{1,0:T(8,128)(2,1)S(1)} %get-tuple-element.27.rows_ref.refs_0_), channel_id=1, source_target_pairs={{0,3},{1,2},{2,1},{3,0},{4,7},{5,6},{6,5},{7,4},{8,11},{9,10},{10,... | collective-permute-start | bytes 417800 | tf_op jit(solution)/shard_map/ppermute | solution.py:350
  12.1 2.6 %collective-permute-start.7 = (bf16[72,256]{1,0:T(8,128)(2,1)S(1)}, bf16[72,256]{1,0:T(8,128)(2,1)S(1)}, u32[]{:S(2)}, u32[]{:S(2)}) collective-permute-start(bf16[72,256]{1,0:T(8,128)(2,1)S(1)} %get-tuple-element.38), channel_id=1, source_target_pairs={{0,8},{1,9},{2,10},{3,11},{4,12},{5,13},{6,14},{7,15},{8,0},{9,1},... | collective-permute-start | bytes 110600 | tf_op jit(solution)/shard_map/ppermute | solution.py:350
  14.7 0.0 collective-permute-done.6.refs_1_
  14.7 1.5 %collective-permute-start.8 = (bf16[72,256]{1,0:T(8,128)(2,1)S(1)}, bf16[72,256]{1,0:T(8,128)(2,1)S(1)}, u32[]{:S(2)}, u32[]{:S(2)}) collective-permute-start(bf16[72,256]{1,0:T(8,128)(2,1)S(1)} %get-tuple-element.39), channel_id=1, source_target_pairs={{0,12},{1,13},{2,14},{3,15},{4,8},{5,9},{6,10},{7,11},{8,4},{9,5},... | collective-permute-start | bytes 110600 | tf_op jit(solution)/shard_map/ppermute | solution.py:350
  16.2 1.5 %shard_map.154 = (bf16[1024,128]{1,0:T(8,128)(2,1)S(1)}, bf16[128,256]{1,0:T(8,128)(2,1)S(1)}) custom-call(bf16[1024,128]{1,0:T(8,128)(2,1)} %refs_0_.3, bf16[8,128]{1,0:T(8,128)(2,1)} %bitcast.10), custom_call_target="tpu_custom_call" | custom-call | tf_op jit(solution)/shard_map/pallas_call | solution.py:385
  17.7 0.0 collective-permute-done.7.refs_2_
  17.7 2.7 %collective-permute-done.8.refs_3_ = bf16[72,256]{1,0:T(8,128)(2,1)S(1)} collective-permute-done((bf16[72,256]{1,0:T(8,128)(2,1)S(1)}, bf16[72,256]{1,0:T(8,128)(2,1)S(1)}, u32[]{:S(2)}, u32[]{:S(2)}) %collective-permute-start.8) | collective-permute-done | bytes 36896 | tf_op jit(solution)/shard_map/ppermute | solution.py:350
  20.4 3.7 %shard_map.155 = (bf16[32,32,128]{2,1,0:T(8,128)(2,1)}, f32[32,256]{1,0:T(8,128)S(1)}) custom-call(bf16[72,256]{1,0:T(8,128)(2,1)S(1)} %get-tuple-element.36.refs_0_, bf16[72,256]{1,0:T(8,128)(2,1)S(1)} %collective-permute-done.6.refs_1_, bf16[72,256]{1,0:T(8,128)(2,1)S(1)} %collective-permute-done.7.refs_2_, ...), custom_call_target="tpu_custom_call" | custom-call | tf_op jit(solution)/shard_map/pallas_call | solution.py:396
  24.1 0.1 collective-permute-start.9
  24.2 2.1 %collective-permute-start.10 = (f32[32,256]{1,0:T(8,128)S(1)}, f32[32,256]{1,0:T(8,128)S(1)}, u32[]{:S(2)}, u32[]{:S(2)}) collective-permute-start(f32[32,256]{1,0:T(8,128)S(1)} %get-tuple-element.42.refs_0_), channel_id=1, source_target_pairs={{0,8},{1,9},{2,10},{3,11},{4,12},{5,13},{6,14},{7,15},{8,0},{9,1},... | collective-permute-start | bytes 98312 | tf_op jit(solution)/shard_map/ppermute | solution.py:350
  26.3 1.8 %collective-permute-done.9.refs_1_ = f32[32,256]{1,0:T(8,128)S(1)} collective-permute-done((f32[32,256]{1,0:T(8,128)S(1)}, f32[32,256]{1,0:T(8,128)S(1)}, u32[]{:S(2)}, u32[]{:S(2)}) %collective-permute-start.9) | collective-permute-done | bytes 32800 | tf_op jit(solution)/shard_map/ppermute | solution.py:350
  28.1 1.5 %collective-permute-start.11 = (f32[32,256]{1,0:T(8,128)S(1)}, f32[32,256]{1,0:T(8,128)S(1)}, u32[]{:S(2)}, u32[]{:S(2)}) collective-permute-start(f32[32,256]{1,0:T(8,128)S(1)} %get-tuple-element.42.refs_0_), channel_id=1, source_target_pairs={{0,12},{1,13},{2,14},{3,15},{4,8},{5,9},{6,10},{7,11},{8,4},{9,5},... | collective-permute-start | bytes 98312 | tf_op jit(solution)/shard_map/ppermute | solution.py:350
  29.6 0.0 collective-permute-done.10.refs_2_
  29.6 4.2 %collective-permute-done.11.refs_3_ = f32[32,256]{1,0:T(8,128)S(1)} collective-permute-done((f32[32,256]{1,0:T(8,128)S(1)}, f32[32,256]{1,0:T(8,128)S(1)}, u32[]{:S(2)}, u32[]{:S(2)}) %collective-permute-start.11) | collective-permute-done | bytes 32800 | tf_op jit(solution)/shard_map/ppermute | solution.py:350
  33.8 0.1 collective-permute-start.12
  33.9 0.8 %collective-permute-start.13 = (f32[32,256]{1,0:T(8,128)S(1)}, f32[32,256]{1,0:T(8,128)S(1)}, u32[]{:S(2)}, u32[]{:S(2)}) collective-permute-start(f32[32,256]{1,0:T(8,128)S(1)} %get-tuple-element.45), channel_id=1, source_target_pairs={{0,2},{1,3},{2,0},{3,1},{4,6},{5,7},{6,4},{7,5},{8,10},{9,11},{10,... | collective-permute-start | bytes 98312 | tf_op jit(solution)/shard_map/ppermute | solution.py:350
  34.7 0.0 collective-permute-done.refs_1_
  34.7 1.0 %collective-permute-start.14 = (f32[32,256]{1,0:T(8,128)S(1)}, f32[32,256]{1,0:T(8,128)S(1)}, u32[]{:S(2)}, u32[]{:S(2)}) collective-permute-start(f32[32,256]{1,0:T(8,128)S(1)} %get-tuple-element.46), channel_id=1, source_target_pairs={{0,3},{1,2},{2,1},{3,0},{4,7},{5,6},{6,5},{7,4},{8,11},{9,10},{10,... | collective-permute-start | bytes 98312 | tf_op jit(solution)/shard_map/ppermute | solution.py:350
  35.7 1.4 %shard_map.150 = (bf16[256,256]{1,0:T(8,128)(2,1)S(1)}, f32[256,256]{1,0:T(8,128)S(1)}) custom-call(bf16[272,256]{1,0:T(8,128)(2,1)S(1)} %get-tuple-element.27.rows_ref.refs_0_, bf16[256,256]{1,0:T(8,128)(2,1)} %wq_hbm.1, bf16[256,256]{1,0:T(8,128)(2,1)} %wg_hbm.1), custom_call_target="tpu_custom_call" | custom-call | tf_op jit(solution)/shard_map/pallas_call | solution.py:414
  37.1 0.0 collective-permute-done.1.refs_2_
  37.1 0.0 collective-permute-done.2.refs_3_
  37.1 1.6 %shard_map.151 = (bf16[8,128,256]{2,1,0:T(8,128)(2,1)S(1)}, bf16[8,128,256]{2,1,0:T(8,128)(2,1)S(1)}, f32[8,128,128]{2,1,0:T(8,128)S(1)}) custom-call(bf16[272,256]{1,0:T(8,128)(2,1)S(1)} %get-tuple-element.27.rows_ref.refs_0_, bf16[272,256]{1,0:T(8,128)(2,1)S(1)} %collective-permute-done.refs_1_, bf16[272,256]{1,0:T(8,128)(2,1)S(1)} %collective-permute-done.1.refs_2_, ...), custom_call_target="tpu_custom_call" | custom-call | tf_op jit(solution)/shard_map/pallas_call | solution.py:424
  38.7 1.6 %shard_map.152 = (f32[8,128,256]{2,1,0:T(8,128)S(1)}, bf16[256,256]{1,0:T(8,128)(2,1)S(1)}, bf16[256,1024]{1,0:T(8,128)(2,1)S(1)}, bf16[1024,256]{1,0:T(8,128)(2,1)S(1)}, bf16[256,256]{1,0:T(8,128)(2,1)S(1)}) custom-call(bf16[256,256]{1,0:T(8,128)(2,1)S(1)} %get-tuple-element.28.query_ref, bf16[8,128,256]{2,1,0:T(8,128)(2,1)S(1)} %get-tuple-element.29.key_ref, ...), custom_call_target="tpu_custom_call" | custom-call | tf_op jit(solution)/shard_map/pallas_call | solution.py:438
  40.3 0.0 collective-permute-done.12.refs_5_
  40.4 0.0 collective-permute-done.13.refs_6_
  40.4 0.0 collective-permute-done.14.refs_7_
  40.4 2.1 %shard_map.157 = bf16[256,256]{1,0:T(8,128)(2,1)} custom-call(f32[8,128,256]{2,1,0:T(8,128)S(1)} %get-tuple-element.30.refs_0_, bf16[8,128,256]{2,1,0:T(8,128)(2,1)S(1)} %get-tuple-element.31.refs_1_, f32[8,128,128]{2,1,0:T(8,128)S(1)} %get-tuple-element.32.refs_2_, f32[256,256]{1,0:T(8,128)S(1)} %get-tuple-element.33.refs_3_, ...), custom_call_target="tpu_custom_call" | custom-call | tf_op jit(solution)/shard_map/pallas_call | solution.py:455
  (2 shorter events, 0.0 us)
Async XLA Ops:
  2.2 3.2 %collective-permute-start.3 = (bf16[40,256]{1,0:T(8,128)(2,1)S(1)}, bf16[40,256]{1,0:T(8,128)(2,1)S(1)}, u32[]{:S(2)}, u32[]{:S(2)}) collective-permute-start(bf16[40,256]{1,0:T(8,128)(2,1)S(1)} %get-tuple-element.35.refs_0_), channel_id=1, source_target_pairs={{0,1},{1,0},{2,3},{3,2},{4,5},{5,4},{6,7},{7,6},{8,9},{9,8},{10,11... | collective-permute-start | bytes 61448 | tf_op jit(solution)/shard_map/ppermute | solution.py:350
  2.8 4.3 %collective-permute-start.4 = (bf16[40,256]{1,0:T(8,128)(2,1)S(1)}, bf16[40,256]{1,0:T(8,128)(2,1)S(1)}, u32[]{:S(2)}, u32[]{:S(2)}) collective-permute-start(bf16[40,256]{1,0:T(8,128)(2,1)S(1)} %get-tuple-element.35.refs_0_), channel_id=1, source_target_pairs={{0,2},{1,3},{2,0},{3,1},{4,6},{5,7},{6,4},{7,5},{8,10},{9,11},{10,... | collective-permute-start | bytes 61448 | tf_op jit(solution)/shard_map/ppermute | solution.py:350
  5.3 3.2 %collective-permute-start.5 = (bf16[40,256]{1,0:T(8,128)(2,1)S(1)}, bf16[40,256]{1,0:T(8,128)(2,1)S(1)}, u32[]{:S(2)}, u32[]{:S(2)}) collective-permute-start(bf16[40,256]{1,0:T(8,128)(2,1)S(1)} %get-tuple-element.35.refs_0_), channel_id=1, source_target_pairs={{0,3},{1,2},{2,1},{3,0},{4,7},{5,6},{6,5},{7,4},{8,11},{9,10},{10,... | collective-permute-start | bytes 61448 | tf_op jit(solution)/shard_map/ppermute | solution.py:350
  8.6 6.1 %collective-permute-start.6 = (bf16[72,256]{1,0:T(8,128)(2,1)S(1)}, bf16[72,256]{1,0:T(8,128)(2,1)S(1)}, u32[]{:S(2)}, u32[]{:S(2)}) collective-permute-start(bf16[72,256]{1,0:T(8,128)(2,1)S(1)} %get-tuple-element.37), channel_id=1, source_target_pairs={{0,4},{1,5},{2,6},{3,7},{4,0},{5,1},{6,2},{7,3},{8,12},{9,13},{10,... | collective-permute-start | bytes 110600 | tf_op jit(solution)/shard_map/ppermute | solution.py:350
  10.2 24.5 %collective-permute-start = (bf16[272,256]{1,0:T(8,128)(2,1)S(1)}, bf16[272,256]{1,0:T(8,128)(2,1)S(1)}, u32[]{:S(2)}, u32[]{:S(2)}) collective-permute-start(bf16[272,256]{1,0:T(8,128)(2,1)S(1)} %get-tuple-element.27.rows_ref.refs_0_), channel_id=1, source_target_pairs={{0,1},{1,0},{2,3},{3,2},{4,5},{5,4},{6,7},{7,6},{8,9},{9,8},{10,11... | collective-permute-start | bytes 417800 | tf_op jit(solution)/shard_map/ppermute | solution.py:350
  10.2 26.9 %collective-permute-start.1 = (bf16[272,256]{1,0:T(8,128)(2,1)S(1)}, bf16[272,256]{1,0:T(8,128)(2,1)S(1)}, u32[]{:S(2)}, u32[]{:S(2)}) collective-permute-start(bf16[272,256]{1,0:T(8,128)(2,1)S(1)} %get-tuple-element.27.rows_ref.refs_0_), channel_id=1, source_target_pairs={{0,2},{1,3},{2,0},{3,1},{4,6},{5,7},{6,4},{7,5},{8,10},{9,11},{10,... | collective-permute-start | bytes 417800 | tf_op jit(solution)/shard_map/ppermute | solution.py:350
  11.0 26.1 %collective-permute-start.2 = (bf16[272,256]{1,0:T(8,128)(2,1)S(1)}, bf16[272,256]{1,0:T(8,128)(2,1)S(1)}, u32[]{:S(2)}, u32[]{:S(2)}) collective-permute-start(bf16[272,256]{1,0:T(8,128)(2,1)S(1)} %get-tuple-element.27.rows_ref.refs_0_), channel_id=1, source_target_pairs={{0,3},{1,2},{2,1},{3,0},{4,7},{5,6},{6,5},{7,4},{8,11},{9,10},{10,... | collective-permute-start | bytes 417800 | tf_op jit(solution)/shard_map/ppermute | solution.py:350
  12.1 5.6 %collective-permute-start.7 = (bf16[72,256]{1,0:T(8,128)(2,1)S(1)}, bf16[72,256]{1,0:T(8,128)(2,1)S(1)}, u32[]{:S(2)}, u32[]{:S(2)}) collective-permute-start(bf16[72,256]{1,0:T(8,128)(2,1)S(1)} %get-tuple-element.38), channel_id=1, source_target_pairs={{0,8},{1,9},{2,10},{3,11},{4,12},{5,13},{6,14},{7,15},{8,0},{9,1},... | collective-permute-start | bytes 110600 | tf_op jit(solution)/shard_map/ppermute | solution.py:350
  14.7 5.8 %collective-permute-start.8 = (bf16[72,256]{1,0:T(8,128)(2,1)S(1)}, bf16[72,256]{1,0:T(8,128)(2,1)S(1)}, u32[]{:S(2)}, u32[]{:S(2)}) collective-permute-start(bf16[72,256]{1,0:T(8,128)(2,1)S(1)} %get-tuple-element.39), channel_id=1, source_target_pairs={{0,12},{1,13},{2,14},{3,15},{4,8},{5,9},{6,10},{7,11},{8,4},{9,5},... | collective-permute-start | bytes 110600 | tf_op jit(solution)/shard_map/ppermute | solution.py:350
  24.1 4.0 %collective-permute-start.9 = (f32[32,256]{1,0:T(8,128)S(1)}, f32[32,256]{1,0:T(8,128)S(1)}, u32[]{:S(2)}, u32[]{:S(2)}) collective-permute-start(f32[32,256]{1,0:T(8,128)S(1)} %get-tuple-element.42.refs_0_), channel_id=1, source_target_pairs={{0,4},{1,5},{2,6},{3,7},{4,0},{5,1},{6,2},{7,3},{8,12},{9,13},{10,... | collective-permute-start | bytes 98312 | tf_op jit(solution)/shard_map/ppermute | solution.py:350
  24.2 5.4 %collective-permute-start.10 = (f32[32,256]{1,0:T(8,128)S(1)}, f32[32,256]{1,0:T(8,128)S(1)}, u32[]{:S(2)}, u32[]{:S(2)}) collective-permute-start(f32[32,256]{1,0:T(8,128)S(1)} %get-tuple-element.42.refs_0_), channel_id=1, source_target_pairs={{0,8},{1,9},{2,10},{3,11},{4,12},{5,13},{6,14},{7,15},{8,0},{9,1},... | collective-permute-start | bytes 98312 | tf_op jit(solution)/shard_map/ppermute | solution.py:350
  28.1 5.7 %collective-permute-start.11 = (f32[32,256]{1,0:T(8,128)S(1)}, f32[32,256]{1,0:T(8,128)S(1)}, u32[]{:S(2)}, u32[]{:S(2)}) collective-permute-start(f32[32,256]{1,0:T(8,128)S(1)} %get-tuple-element.42.refs_0_), channel_id=1, source_target_pairs={{0,12},{1,13},{2,14},{3,15},{4,8},{5,9},{6,10},{7,11},{8,4},{9,5},... | collective-permute-start | bytes 98312 | tf_op jit(solution)/shard_map/ppermute | solution.py:350
  33.8 6.5 %collective-permute-start.12 = (f32[32,256]{1,0:T(8,128)S(1)}, f32[32,256]{1,0:T(8,128)S(1)}, u32[]{:S(2)}, u32[]{:S(2)}) collective-permute-start(f32[32,256]{1,0:T(8,128)S(1)} %get-tuple-element.44), channel_id=1, source_target_pairs={{0,1},{1,0},{2,3},{3,2},{4,5},{5,4},{6,7},{7,6},{8,9},{9,8},{10,11... | collective-permute-start | bytes 98312 | tf_op jit(solution)/shard_map/ppermute | solution.py:350
  33.9 6.5 %collective-permute-start.13 = (f32[32,256]{1,0:T(8,128)S(1)}, f32[32,256]{1,0:T(8,128)S(1)}, u32[]{:S(2)}, u32[]{:S(2)}) collective-permute-start(f32[32,256]{1,0:T(8,128)S(1)} %get-tuple-element.45), channel_id=1, source_target_pairs={{0,2},{1,3},{2,0},{3,1},{4,6},{5,7},{6,4},{7,5},{8,10},{9,11},{10,... | collective-permute-start | bytes 98312 | tf_op jit(solution)/shard_map/ppermute | solution.py:350
  34.7 5.6 %collective-permute-start.14 = (f32[32,256]{1,0:T(8,128)S(1)}, f32[32,256]{1,0:T(8,128)S(1)}, u32[]{:S(2)}, u32[]{:S(2)}) collective-permute-start(f32[32,256]{1,0:T(8,128)S(1)} %get-tuple-element.46), channel_id=1, source_target_pairs={{0,3},{1,2},{2,1},{3,0},{4,7},{5,6},{6,5},{7,4},{8,11},{9,10},{10,... | collective-permute-start | bytes 98312 | tf_op jit(solution)/shard_map/ppermute | solution.py:350

commit v7 on v6

--- a/solution.py
+++ b/solution.py
@@ -54,6 +54,18 @@
         return get
 
     return [ready(n) for n in range(len(copies))]
+
+
+def carry(sources, kept, sems, first):
+    copies = [pltpu.make_async_copy(s, k, sems.at[first + n]) for n, (s, k) in enumerate(zip(sources, kept))]
+    for copy in copies:
+        copy.start()
+
+    def done():
+        for copy in copies:
+            copy.wait()
+
+    return done
 
 
 def factor_kernel(seqs, res, *refs):
@@ -120,20 +132,27 @@
 
 
 def order_kernel(res, width, *refs):
-    sources, (wout_ref, wrep_ref, wf_scr, *buffers, sems) = refs[:2], refs[2:]
+    sources, later, (wout_ref, wrep_ref), kept = refs[:2], refs[2:4], refs[4:6], refs[6:8]
+    wf_scr, *buffers, sems = refs[8:]
     get_wout, get_wbias = fetch(sources, buffers, sems)
+    done = carry(later, kept, sems, 2)
     heads = sources[1].shape[0]
     wf_scr[...] = get_wout().astype(F32)
     for d in range(width):
         wout_ref[d * width : (d + 1) * width, :] = wf_scr[pl.ds(d, width, stride=width), :].astype(BF16)
     repeat = spread_matrix(heads, heads * res, lambda c: c // res)
     wrep_ref[...] = dot_tn(get_wbias(), repeat).astype(BF16)
+    done()
 
 
 def pair_kernel(count_a, res, width, *refs):
     msgs = refs[:count_a]
-    wout_ref, wrep_ref, pair_hbm, out_hbm, bias_ref, a_scr, out_buf, pair_buf, sems = refs[count_a:]
+    wout_ref, wrep_ref, pair_hbm, *refs = refs[count_a:]
+    count = (len(refs) - 6) // 2
+    later, (out_hbm, bias_ref), kept = refs[:count], refs[count : count + 2], refs[count + 2 : -4]
+    a_scr, out_buf, pair_buf, sems = refs[-4:]
     (get_pair,) = fetch([pair_hbm], [pair_buf], sems)
+    done = carry(later, kept, sems, 2)
     span = res * width
     per = LANES // width
     lanes = msgs[0].shape[1]
@@ -210,23 +229,21 @@
         bias = jnp.where(query == i, spread[i * res : (i + 1) * res], bias)
     bias_ref[...] = bias
     out_copy.wait()
-
-
-def query_kernel(seqs, res, heads, rows_ref, wq_hbm, wg_hbm, query_ref, gate_ref, *scratch):
-    get_q, get_g = fetch([wq_hbm, wg_hbm], scratch[:2], scratch[2])
+    done()
+
+
+def query_kernel(seqs, res, heads, rows_ref, wq_ref, wg_ref, query_ref, gate_ref):
     own = rows_ref[: seqs * res, :]
     head_width = query_ref.shape[1] // heads
-    query_ref[...] = (dot(own, get_q()) * (head_width ** (-0.5))).astype(BF16)
-    gate_ref[...] = jax.nn.sigmoid(dot(own, get_g()))
+    query_ref[...] = (dot(own, wq_ref[...]) * (head_width ** (-0.5))).astype(BF16)
+    gate_ref[...] = jax.nn.sigmoid(dot(own, wg_ref[...]))
 
 
 def key_kernel(seqs, res, count_b, *refs):
-    rows_refs, refs = refs[:count_b], refs[count_b:]
-    wk_hbm, wv_hbm, key_ref, value_ref, limit_ref, wk_buf, wv_buf, sems = refs
-    get_k, get_v = fetch([wk_hbm, wv_hbm], [wk_buf, wv_buf], sems)
+    rows_refs, (wk_ref, wv_ref, key_ref, value_ref, limit_ref) = refs[:count_b], refs[count_b:]
     spread = spread_matrix(seqs, seqs * LANES, lambda c: c // LANES)
-    for get, ref in ((get_k, key_ref), (get_v, value_ref)):
-        weight = get()
+    for weight_ref, ref in ((wk_ref, key_ref), (wv_ref, value_ref)):
+        weight = weight_ref[...]
         for k in range(count_b):
             made = dot(rows_refs[k][: seqs * res, :], weight).astype(BF16)
             for s in range(seqs):
@@ -238,12 +255,7 @@
             limit_ref[s, k * res : (k + 1) * res, :] = keep[:, s * LANES : (s + 1) * LANES]
 
 
-def score_kernel(seqs, res, heads, query_ref, key_ref, *refs):
-    count = (len(refs) - 2) // 2
-    sources, score_ref, kept, sems = refs[:count], refs[count], refs[count + 1 : -1], refs[-1]
-    copies = [pltpu.make_async_copy(x, y, sems.at[n]) for n, (x, y) in enumerate(zip(sources, kept))]
-    for copy in copies:
-        copy.start()
+def score_kernel(seqs, res, heads, query_ref, key_ref, score_ref):
     channels = query_ref.shape[1]
     wide = heads * res
     same_head = iota((wide, channels), 0) // res == iota((wide, channels), 1) // (channels // heads)
@@ -254,8 +266,6 @@
             jnp.zeros((), BF16),
         )
         score_ref[s] = dot_nt(key_ref[s], query_wide)
-    for copy in copies:
-        copy.wait()
 
 
 def attention_kernel(seqs, res, heads, count_b, *refs):
@@ -297,12 +307,13 @@
     out_ref[...] = (middle + dot(hidden, down_ref[...])).astype(BF16)
 
 
-def call(kernel, mib, outs, scratch=(), blocks=0, hbm=(), more_sems=0, **specs):
+def call(kernel, mib, outs, scratch=(), blocks=0, hbm=(), later=(), more_sems=0, **specs):
     if hbm:
-        vmem_spec = pl.BlockSpec(memory_space=pltpu.VMEM)
-        specs["in_specs"] = [vmem_spec] * blocks + [pl.BlockSpec(memory_space=pltpu.HBM)] * len(hbm)
+        vmem_spec, hbm_spec = (pl.BlockSpec(memory_space=m) for m in (pltpu.VMEM, pltpu.HBM))
+        outs = tuple(outs) + tuple(jax.ShapeDtypeStruct(x.shape, x.dtype) for x in later)
+        specs["in_specs"] = [vmem_spec] * blocks + [hbm_spec] * (len(hbm) + len(later))
         scratch = list(scratch) + [pltpu.VMEM(h.shape, h.dtype) for h in hbm]
-        scratch.append(pltpu.SemaphoreType.DMA((len(hbm) + more_sems,)))
+        scratch.append(pltpu.SemaphoreType.DMA((len(hbm) + len(later) + more_sems,)))
     return pl.pallas_call(
         kernel,
         out_shape=outs,
@@ -382,7 +393,8 @@
     all_rows = [rows] + [along_b(rows, k) for k in range(1, count_b)]
 
     weights = [outer_output_weight, pair_bias_weight.T]
-    w_out, w_rep = call(
+    later = [query_weight, gate_weight]
+    w_out, w_rep, *w_query = call(
         functools.partial(order_kernel, res, width),
         4,
         (
@@ -392,8 +404,11 @@
         [pltpu.VMEM(outer_output_weight.shape, F32)],
         0,
         weights,
-    )(*in_hbm(weights))
-    pair_output, bias = call(
+        later,
+    )(*in_hbm(weights + later))
+    later = [key_weight, value_weight, output_weight, up_weight, down_weight, flat]
+    vmem_spec, hbm_spec = (pl.BlockSpec(memory_space=m) for m in (pltpu.VMEM, pltpu.HBM))
+    pair_output, bias, w_key, w_value, *kept = call(
         functools.partial(pair_kernel, count_a, res, width),
         16,
         (shape(pair_state.shape, BF16), shape((res, heads * res), F32)),
@@ -403,24 +418,17 @@
         ],
         count_a + 2,
         [pair_state],
+        later,
         1,
-        out_specs=(
-            pl.BlockSpec(memory_space=pltpu.HBM),
-            pl.BlockSpec(memory_space=pltpu.VMEM),
-        ),
-    )(*msgs, w_out, w_rep, *in_hbm([pair_state]))
-
-    weights = [query_weight, gate_weight]
+        out_specs=(hbm_spec,) + (vmem_spec,) * (1 + len(later)),
+    )(*msgs, w_out, w_rep, *in_hbm([pair_state] + later))
+
     query, gate = call(
         functools.partial(query_kernel, seqs, res, heads),
         4,
         (shape((seqs * res, channels), BF16), shape((seqs * res, channels), F32)),
-        [],
-        1,
-        weights,
-    )(rows, *in_hbm(weights))
+    )(rows, *w_query)
     keys = res * count_b
-    weights = [key_weight, value_weight]
     key, value, limit = call(
         functools.partial(key_kernel, seqs, res, count_b),
         8,
@@ -429,20 +437,12 @@
             shape((seqs, keys, channels), BF16),
             shape((seqs, keys, LANES), F32),
         ),
-        [],
-        count_b,
-        weights,
-    )(*all_rows, *in_hbm(weights))
-    weights = [output_weight, up_weight, down_weight, flat]
-    vmem_spec = pl.BlockSpec(memory_space=pltpu.VMEM)
-    scores, *kept = pl.pallas_call(
+    )(*all_rows, w_key, w_value)
+    (scores,) = call(
         functools.partial(score_kernel, seqs, res, heads),
-        in_specs=[vmem_spec] * 2 + [pl.BlockSpec(memory_space=pltpu.HBM)] * len(weights),
-        out_shape=(shape((seqs, keys, heads * res), F32),)
-        + tuple(shape(w.shape, w.dtype) for w in weights),
-        scratch_shapes=[pltpu.SemaphoreType.DMA((len(weights),))],
-        compiler_params=pltpu.CompilerParams(vmem_limit_bytes=8 * MIB),
-    )(query, key, *in_hbm(weights))
+        8,
+        (shape((seqs, keys, heads * res), F32),),
+    )(query, key)
 
     tiles = [bias] + [along_a(bias, k) for k in range(1, count_a)]
     biases = call(

time: 42.7 us -> 40.7 us (0.953)
  Pallas kernels: 13.5 us -> 10.2 us
  waiting for transfers between devices: 11.9 us -> 13.3 us
    ppermute x15, waiting for transfers between devices: 11.9 us -> 13.3 us  [permute(): return lax.ppermute(value, ('aa', 'ba'), pairs)]
    pallas_call x1, Pallas kernels: 1.36 us -> 0.23 us  [per_device(): call(functools.partial(query_kernel, seqs, res, heads), 4, (shape((seqs *...]
    pallas_call x1, Pallas kernels: 1.58 us -> 0.46 us  [per_device(): call(functools.partial(score_kernel, seqs, res, heads), 8, (shape((seqs,...]
    pallas_call x1, Pallas kernels: 1.61 us -> 0.51 us  [per_device(): call(functools.partial(key_kernel, seqs, res, count_b), 8, (shape((seqs,...]
  transfers between devices with their start and end apart: 15 -> 15, of which waited for: 5 -> 7; matrix products, arithmetic and copies ran while one was open for 0% -> 0% of each run, Pallas kernels for 23% -> 16%
where the time goes in v7:
time: 40.7 us; the launch traced here: 40.6 us
  starting transfers between devices  16.4 us (40%)
  waiting for transfers between devices  13.3 us (33%)
  Pallas kernels  10.2 us (25%)
  between operations  0.74 us (2%)
    ppermute x15, starting transfers between devices, permute(): return lax.ppermute(value, ('aa', 'ba'), pairs)  16.4 us
    ppermute x15, waiting for transfers between devices, permute(): return lax.ppermute(value, ('aa', 'ba'), pairs)  13.3 us
    pallas_call x1, Pallas kernels, per_device(): call(functools.partial(pair_kernel, count_a, res, width), 16, (shape(pair...  3.72 us
    pallas_call x1, Pallas kernels, per_device(): call(functools.partial(attention_kernel, seqs, res, heads, count_b), 16,...  2.09 us
    pallas_call x1, Pallas kernels, per_device(): call(functools.partial(factor_kernel, seqs, res), 4, (shape((seqs * res +...  1.6 us
    pallas_call x1, Pallas kernels, per_device(): call(functools.partial(order_kernel, res, width), 4, (shape(outer_output_...  1.52 us
  transfers between devices with their start and end apart: 15, of which 7 were waited for; matrix products, arithmetic and copies ran while one was open for 0% of the time, Pallas kernels for 16%

profile of v7, /device:TPU:0, one launch (start us, length us, event | category | flops | bytes accessed | tf_op | source)
XLA Modules:
  0.0 40.6 jit_solution(7524186914170599295)
XLA Ops:
  0.6 1.6 %shard_map.149 = (bf16[272,256]{1,0:T(8,128)(2,1)S(1)}, bf16[40,256]{1,0:T(8,128)(2,1)S(1)}, bf16[32,256]{1,0:T(8,128)(2,1)S(1)}) custom-call(bf16[32,256]{1,0:T(8,128)(2,1)} %bitcast.8, bf16[32,256]{1,0:T(8,128)(2,1)} %bitcast.9, s32[8,32]{1,0:T(8,128)} %refs_2_.2, bf16[256,256]{1,0:T(8,128)(2,1)} %bitcast.5), custom_call_target="tpu_custom_call" | custom-call | tf_op jit(solution)/shard_map/pallas_call | solution.py:372
  2.2 0.6 %collective-permute-start.3 = (bf16[40,256]{1,0:T(8,128)(2,1)S(1)}, bf16[40,256]{1,0:T(8,128)(2,1)S(1)}, u32[]{:S(2)}, u32[]{:S(2)}) collective-permute-start(bf16[40,256]{1,0:T(8,128)(2,1)S(1)} %get-tuple-element.35.refs_0_), channel_id=1, source_target_pairs={{0,1},{1,0},{2,3},{3,2},{4,5},{5,4},{6,7},{7,6},{8,9},{9,8},{10,11... | collective-permute-start | bytes 61448 | tf_op jit(solution)/shard_map/ppermute | solution.py:361
  2.8 2.6 %collective-permute-start.4 = (bf16[40,256]{1,0:T(8,128)(2,1)S(1)}, bf16[40,256]{1,0:T(8,128)(2,1)S(1)}, u32[]{:S(2)}, u32[]{:S(2)}) collective-permute-start(bf16[40,256]{1,0:T(8,128)(2,1)S(1)} %get-tuple-element.35.refs_0_), channel_id=1, source_target_pairs={{0,2},{1,3},{2,0},{3,1},{4,6},{5,7},{6,4},{7,5},{8,10},{9,11},{10,... | collective-permute-start | bytes 61448 | tf_op jit(solution)/shard_map/ppermute | solution.py:361
  5.3 0.0 collective-permute-start.5
  5.4 0.0 collective-permute-done.3.refs_1_
  5.4 1.7 %collective-permute-done.4.refs_2_ = bf16[40,256]{1,0:T(8,128)(2,1)S(1)} collective-permute-done((bf16[40,256]{1,0:T(8,128)(2,1)S(1)}, bf16[40,256]{1,0:T(8,128)(2,1)S(1)}, u32[]{:S(2)}, u32[]{:S(2)}) %collective-permute-start.4) | collective-permute-done | bytes 20512 | tf_op jit(solution)/shard_map/ppermute | solution.py:361
  7.1 1.4 %collective-permute-done.5.refs_3_ = bf16[40,256]{1,0:T(8,128)(2,1)S(1)} collective-permute-done((bf16[40,256]{1,0:T(8,128)(2,1)S(1)}, bf16[40,256]{1,0:T(8,128)(2,1)S(1)}, u32[]{:S(2)}, u32[]{:S(2)}) %collective-permute-start.5) | collective-permute-done | bytes 20512 | tf_op jit(solution)/shard_map/ppermute | solution.py:361
  8.6 1.6 %collective-permute-start.6 = (bf16[72,256]{1,0:T(8,128)(2,1)S(1)}, bf16[72,256]{1,0:T(8,128)(2,1)S(1)}, u32[]{:S(2)}, u32[]{:S(2)}) collective-permute-start(bf16[72,256]{1,0:T(8,128)(2,1)S(1)} %get-tuple-element.37), channel_id=1, source_target_pairs={{0,4},{1,5},{2,6},{3,7},{4,0},{5,1},{6,2},{7,3},{8,12},{9,13},{10,... | collective-permute-start | bytes 110600 | tf_op jit(solution)/shard_map/ppermute | solution.py:361
  10.2 0.0 collective-permute-start
  10.2 0.8 %collective-permute-start.1 = (bf16[272,256]{1,0:T(8,128)(2,1)S(1)}, bf16[272,256]{1,0:T(8,128)(2,1)S(1)}, u32[]{:S(2)}, u32[]{:S(2)}) collective-permute-start(bf16[272,256]{1,0:T(8,128)(2,1)S(1)} %get-tuple-element.30.rows_ref.refs_0_), channel_id=1, source_target_pairs={{0,2},{1,3},{2,0},{3,1},{4,6},{5,7},{6,4},{7,5},{8,10},{9,11},{10,... | collective-permute-start | bytes 417800 | tf_op jit(solution)/shard_map/ppermute | solution.py:361
  11.0 1.1 %collective-permute-start.2 = (bf16[272,256]{1,0:T(8,128)(2,1)S(1)}, bf16[272,256]{1,0:T(8,128)(2,1)S(1)}, u32[]{:S(2)}, u32[]{:S(2)}) collective-permute-start(bf16[272,256]{1,0:T(8,128)(2,1)S(1)} %get-tuple-element.30.rows_ref.refs_0_), channel_id=1, source_target_pairs={{0,3},{1,2},{2,1},{3,0},{4,7},{5,6},{6,5},{7,4},{8,11},{9,10},{10,... | collective-permute-start | bytes 417800 | tf_op jit(solution)/shard_map/ppermute | solution.py:361
  12.1 2.6 %collective-permute-start.7 = (bf16[72,256]{1,0:T(8,128)(2,1)S(1)}, bf16[72,256]{1,0:T(8,128)(2,1)S(1)}, u32[]{:S(2)}, u32[]{:S(2)}) collective-permute-start(bf16[72,256]{1,0:T(8,128)(2,1)S(1)} %get-tuple-element.38), channel_id=1, source_target_pairs={{0,8},{1,9},{2,10},{3,11},{4,12},{5,13},{6,14},{7,15},{8,0},{9,1},... | collective-permute-start | bytes 110600 | tf_op jit(solution)/shard_map/ppermute | solution.py:361
  14.7 0.0 collective-permute-done.6.refs_1_
  14.7 1.5 %collective-permute-start.8 = (bf16[72,256]{1,0:T(8,128)(2,1)S(1)}, bf16[72,256]{1,0:T(8,128)(2,1)S(1)}, u32[]{:S(2)}, u32[]{:S(2)}) collective-permute-start(bf16[72,256]{1,0:T(8,128)(2,1)S(1)} %get-tuple-element.39), channel_id=1, source_target_pairs={{0,12},{1,13},{2,14},{3,15},{4,8},{5,9},{6,10},{7,11},{8,4},{9,5},... | collective-permute-start | bytes 110600 | tf_op jit(solution)/shard_map/ppermute | solution.py:361
  16.2 1.5 %shard_map.150 = (bf16[1024,128]{1,0:T(8,128)(2,1)S(1)}, bf16[128,256]{1,0:T(8,128)(2,1)S(1)}, bf16[256,256]{1,0:T(8,128)(2,1)S(1)}, bf16[256,256]{1,0:T(8,128)(2,1)S(1)}) custom-call(bf16[1024,128]{1,0:T(8,128)(2,1)} %refs_0_.1, bf16[8,128]{1,0:T(8,128)(2,1)} %bitcast.10, bf16[256,256]{1,0:T(8,128)(2,1)} %refs_2_.3, bf16[256,256]{1,0:T(8,128)(2,1)} %refs_3_.1), custom_call_target="tpu_custom_call" | custom-call | tf_op jit(solution)/shard_map/pallas_call | solution.py:397
  17.7 0.0 collective-permute-done.7.refs_2_
  17.7 2.7 %collective-permute-done.8.refs_3_ = bf16[72,256]{1,0:T(8,128)(2,1)S(1)} collective-permute-done((bf16[72,256]{1,0:T(8,128)(2,1)S(1)}, bf16[72,256]{1,0:T(8,128)(2,1)S(1)}, u32[]{:S(2)}, u32[]{:S(2)}) %collective-permute-start.8) | collective-permute-done | bytes 36896 | tf_op jit(solution)/shard_map/ppermute | solution.py:361
  20.4 3.7 %shard_map.153 = (bf16[32,32,128]{2,1,0:T(8,128)(2,1)}, f32[32,256]{1,0:T(8,128)S(1)}, bf16[256,256]{1,0:T(8,128)(2,1)S(1)}, bf16[256,256]{1,0:T(8,128)(2,1)S(1)...) custom-call(bf16[72,256]{1,0:T(8,128)(2,1)S(1)} %get-tuple-element.3, ...), custom_call_target="tpu_custom_call" | custom-call | tf_op jit(solution)/shard_map/pallas_call | solution.py:411
  24.2 0.1 collective-permute-start.9
  24.2 2.1 %collective-permute-start.10 = (f32[32,256]{1,0:T(8,128)S(1)}, f32[32,256]{1,0:T(8,128)S(1)}, u32[]{:S(2)}, u32[]{:S(2)}) collective-permute-start(f32[32,256]{1,0:T(8,128)S(1)} %get-tuple-element.48.refs_0_), channel_id=1, source_target_pairs={{0,8},{1,9},{2,10},{3,11},{4,12},{5,13},{6,14},{7,15},{8,0},{9,1},... | collective-permute-start | bytes 98312 | tf_op jit(solution)/shard_map/ppermute | solution.py:361
  26.3 1.8 %collective-permute-done.9.refs_1_ = f32[32,256]{1,0:T(8,128)S(1)} collective-permute-done((f32[32,256]{1,0:T(8,128)S(1)}, f32[32,256]{1,0:T(8,128)S(1)}, u32[]{:S(2)}, u32[]{:S(2)}) %collective-permute-start.9) | collective-permute-done | bytes 32800 | tf_op jit(solution)/shard_map/ppermute | solution.py:361
  28.1 1.5 %collective-permute-start.11 = (f32[32,256]{1,0:T(8,128)S(1)}, f32[32,256]{1,0:T(8,128)S(1)}, u32[]{:S(2)}, u32[]{:S(2)}) collective-permute-start(f32[32,256]{1,0:T(8,128)S(1)} %get-tuple-element.48.refs_0_), channel_id=1, source_target_pairs={{0,12},{1,13},{2,14},{3,15},{4,8},{5,9},{6,10},{7,11},{8,4},{9,5},... | collective-permute-start | bytes 98312 | tf_op jit(solution)/shard_map/ppermute | solution.py:361
  29.7 0.0 collective-permute-done.10.refs_2_
  29.7 4.2 %collective-permute-done.11.refs_3_ = f32[32,256]{1,0:T(8,128)S(1)} collective-permute-done((f32[32,256]{1,0:T(8,128)S(1)}, f32[32,256]{1,0:T(8,128)S(1)}, u32[]{:S(2)}, u32[]{:S(2)}) %collective-permute-start.11) | collective-permute-done | bytes 32800 | tf_op jit(solution)/shard_map/ppermute | solution.py:361
  33.9 0.1 collective-permute-start.12
  34.0 0.8 %collective-permute-start.13 = (f32[32,256]{1,0:T(8,128)S(1)}, f32[32,256]{1,0:T(8,128)S(1)}, u32[]{:S(2)}, u32[]{:S(2)}) collective-permute-start(f32[32,256]{1,0:T(8,128)S(1)} %get-tuple-element.51), channel_id=1, source_target_pairs={{0,2},{1,3},{2,0},{3,1},{4,6},{5,7},{6,4},{7,5},{8,10},{9,11},{10,... | collective-permute-start | bytes 98312 | tf_op jit(solution)/shard_map/ppermute | solution.py:361
  34.8 0.0 collective-permute-done.refs_1_
  34.8 1.0 %collective-permute-start.14 = (f32[32,256]{1,0:T(8,128)S(1)}, f32[32,256]{1,0:T(8,128)S(1)}, u32[]{:S(2)}, u32[]{:S(2)}) collective-permute-start(f32[32,256]{1,0:T(8,128)S(1)} %get-tuple-element.52), channel_id=1, source_target_pairs={{0,3},{1,2},{2,1},{3,0},{4,7},{5,6},{6,5},{7,4},{8,11},{9,10},{10,... | collective-permute-start | bytes 98312 | tf_op jit(solution)/shard_map/ppermute | solution.py:361
  35.8 0.2 shard_map.151
  36.1 0.0 collective-permute-done.1.refs_2_
  36.1 0.0 collective-permute-done.2.refs_3_
  36.1 0.5 %shard_map.154 = (bf16[8,128,256]{2,1,0:T(8,128)(2,1)S(1)}, bf16[8,128,256]{2,1,0:T(8,128)(2,1)S(1)}, f32[8,128,128]{2,1,0:T(8,128)S(1)}) custom-call(bf16[272,256]{1,0:T(8,128)(2,1)S(1)} %get-tuple-element.30.rows_ref.refs_0_, bf16[272,256]{1,0:T(8,128)(2,1)S(1)} %collective-permute-done.refs_1_, bf16[272,256]{1,0:T(8,128)(2,1)S(1)} %collective-permute-done.1.refs_2_, ...), custom_call_target="tpu_custom_call" | custom-call | tf_op jit(solution)/shard_map/pallas_call | solution.py:432
  36.6 0.5 %shard_map.155.refs_0_ = f32[8,128,256]{2,1,0:T(8,128)S(1)} custom-call(bf16[256,256]{1,0:T(8,128)(2,1)S(1)} %get-tuple-element.33.query_ref, bf16[8,128,256]{2,1,0:T(8,128)(2,1)S(1)} %get-tuple-element.44.key_ref), custom_call_target="tpu_custom_call" | custom-call | tf_op jit(solution)/shard_map/pallas_call | solution.py:441
  37.1 0.0 collective-permute-done.12.refs_5_
  37.1 1.0 %collective-permute-done.13.refs_6_ = f32[32,256]{1,0:T(8,128)S(1)} collective-permute-done((f32[32,256]{1,0:T(8,128)S(1)}, f32[32,256]{1,0:T(8,128)S(1)}, u32[]{:S(2)}, u32[]{:S(2)}) %collective-permute-start.13) | collective-permute-done | bytes 32800 | tf_op jit(solution)/shard_map/ppermute | solution.py:361
  38.1 0.4 collective-permute-done.14.refs_7_
  38.5 2.1 %shard_map.157 = bf16[256,256]{1,0:T(8,128)(2,1)} custom-call(f32[8,128,256]{2,1,0:T(8,128)S(1)} %shard_map.155.refs_0_, bf16[8,128,256]{2,1,0:T(8,128)(2,1)S(1)} %get-tuple-element.45.refs_1_, f32[8,128,128]{2,1,0:T(8,128)S(1)} %get-tuple-element.46.refs_2_, f32[256,256]{1,0:T(8,128)S(1)} %get-tuple-element.47.refs_3_, ...), custom_call_target="tpu_custom_call" | custom-call | tf_op jit(solution)/shard_map/pallas_call | solution.py:455
  (2 shorter events, 0.0 us)
Async XLA Ops:
  2.2 3.2 %collective-permute-start.3 = (bf16[40,256]{1,0:T(8,128)(2,1)S(1)}, bf16[40,256]{1,0:T(8,128)(2,1)S(1)}, u32[]{:S(2)}, u32[]{:S(2)}) collective-permute-start(bf16[40,256]{1,0:T(8,128)(2,1)S(1)} %get-tuple-element.35.refs_0_), channel_id=1, source_target_pairs={{0,1},{1,0},{2,3},{3,2},{4,5},{5,4},{6,7},{7,6},{8,9},{9,8},{10,11... | collective-permute-start | bytes 61448 | tf_op jit(solution)/shard_map/ppermute | solution.py:361
  2.8 4.3 %collective-permute-start.4 = (bf16[40,256]{1,0:T(8,128)(2,1)S(1)}, bf16[40,256]{1,0:T(8,128)(2,1)S(1)}, u32[]{:S(2)}, u32[]{:S(2)}) collective-permute-start(bf16[40,256]{1,0:T(8,128)(2,1)S(1)} %get-tuple-element.35.refs_0_), channel_id=1, source_target_pairs={{0,2},{1,3},{2,0},{3,1},{4,6},{5,7},{6,4},{7,5},{8,10},{9,11},{10,... | collective-permute-start | bytes 61448 | tf_op jit(solution)/shard_map/ppermute | solution.py:361
  5.3 3.2 %collective-permute-start.5 = (bf16[40,256]{1,0:T(8,128)(2,1)S(1)}, bf16[40,256]{1,0:T(8,128)(2,1)S(1)}, u32[]{:S(2)}, u32[]{:S(2)}) collective-permute-start(bf16[40,256]{1,0:T(8,128)(2,1)S(1)} %get-tuple-element.35.refs_0_), channel_id=1, source_target_pairs={{0,3},{1,2},{2,1},{3,0},{4,7},{5,6},{6,5},{7,4},{8,11},{9,10},{10,... | collective-permute-start | bytes 61448 | tf_op jit(solution)/shard_map/ppermute | solution.py:361
  8.6 6.1 %collective-permute-start.6 = (bf16[72,256]{1,0:T(8,128)(2,1)S(1)}, bf16[72,256]{1,0:T(8,128)(2,1)S(1)}, u32[]{:S(2)}, u32[]{:S(2)}) collective-permute-start(bf16[72,256]{1,0:T(8,128)(2,1)S(1)} %get-tuple-element.37), channel_id=1, source_target_pairs={{0,4},{1,5},{2,6},{3,7},{4,0},{5,1},{6,2},{7,3},{8,12},{9,13},{10,... | collective-permute-start | bytes 110600 | tf_op jit(solution)/shard_map/ppermute | solution.py:361
  10.2 24.6 %collective-permute-start = (bf16[272,256]{1,0:T(8,128)(2,1)S(1)}, bf16[272,256]{1,0:T(8,128)(2,1)S(1)}, u32[]{:S(2)}, u32[]{:S(2)}) collective-permute-start(bf16[272,256]{1,0:T(8,128)(2,1)S(1)} %get-tuple-element.30.rows_ref.refs_0_), channel_id=1, source_target_pairs={{0,1},{1,0},{2,3},{3,2},{4,5},{5,4},{6,7},{7,6},{8,9},{9,8},{10,11... | collective-permute-start | bytes 417800 | tf_op jit(solution)/shard_map/ppermute | solution.py:361
  10.2 25.8 %collective-permute-start.1 = (bf16[272,256]{1,0:T(8,128)(2,1)S(1)}, bf16[272,256]{1,0:T(8,128)(2,1)S(1)}, u32[]{:S(2)}, u32[]{:S(2)}) collective-permute-start(bf16[272,256]{1,0:T(8,128)(2,1)S(1)} %get-tuple-element.30.rows_ref.refs_0_), channel_id=1, source_target_pairs={{0,2},{1,3},{2,0},{3,1},{4,6},{5,7},{6,4},{7,5},{8,10},{9,11},{10,... | collective-permute-start | bytes 417800 | tf_op jit(solution)/shard_map/ppermute | solution.py:361
  11.0 25.1 %collective-permute-start.2 = (bf16[272,256]{1,0:T(8,128)(2,1)S(1)}, bf16[272,256]{1,0:T(8,128)(2,1)S(1)}, u32[]{:S(2)}, u32[]{:S(2)}) collective-permute-start(bf16[272,256]{1,0:T(8,128)(2,1)S(1)} %get-tuple-element.30.rows_ref.refs_0_), channel_id=1, source_target_pairs={{0,3},{1,2},{2,1},{3,0},{4,7},{5,6},{6,5},{7,4},{8,11},{9,10},{10,... | collective-permute-start | bytes 417800 | tf_op jit(solution)/shard_map/ppermute | solution.py:361
  12.1 5.6 %collective-permute-start.7 = (bf16[72,256]{1,0:T(8,128)(2,1)S(1)}, bf16[72,256]{1,0:T(8,128)(2,1)S(1)}, u32[]{:S(2)}, u32[]{:S(2)}) collective-permute-start(bf16[72,256]{1,0:T(8,128)(2,1)S(1)} %get-tuple-element.38), channel_id=1, source_target_pairs={{0,8},{1,9},{2,10},{3,11},{4,12},{5,13},{6,14},{7,15},{8,0},{9,1},... | collective-permute-start | bytes 110600 | tf_op jit(solution)/shard_map/ppermute | solution.py:361
  14.7 5.8 %collective-permute-start.8 = (bf16[72,256]{1,0:T(8,128)(2,1)S(1)}, bf16[72,256]{1,0:T(8,128)(2,1)S(1)}, u32[]{:S(2)}, u32[]{:S(2)}) collective-permute-start(bf16[72,256]{1,0:T(8,128)(2,1)S(1)} %get-tuple-element.39), channel_id=1, source_target_pairs={{0,12},{1,13},{2,14},{3,15},{4,8},{5,9},{6,10},{7,11},{8,4},{9,5},... | collective-permute-start | bytes 110600 | tf_op jit(solution)/shard_map/ppermute | solution.py:361
  24.2 4.0 %collective-permute-start.9 = (f32[32,256]{1,0:T(8,128)S(1)}, f32[32,256]{1,0:T(8,128)S(1)}, u32[]{:S(2)}, u32[]{:S(2)}) collective-permute-start(f32[32,256]{1,0:T(8,128)S(1)} %get-tuple-element.48.refs_0_), channel_id=1, source_target_pairs={{0,4},{1,5},{2,6},{3,7},{4,0},{5,1},{6,2},{7,3},{8,12},{9,13},{10,... | collective-permute-start | bytes 98312 | tf_op jit(solution)/shard_map/ppermute | solution.py:361
  24.2 5.4 %collective-permute-start.10 = (f32[32,256]{1,0:T(8,128)S(1)}, f32[32,256]{1,0:T(8,128)S(1)}, u32[]{:S(2)}, u32[]{:S(2)}) collective-permute-start(f32[32,256]{1,0:T(8,128)S(1)} %get-tuple-element.48.refs_0_), channel_id=1, source_target_pairs={{0,8},{1,9},{2,10},{3,11},{4,12},{5,13},{6,14},{7,15},{8,0},{9,1},... | collective-permute-start | bytes 98312 | tf_op jit(solution)/shard_map/ppermute | solution.py:361
  28.1 5.7 %collective-permute-start.11 = (f32[32,256]{1,0:T(8,128)S(1)}, f32[32,256]{1,0:T(8,128)S(1)}, u32[]{:S(2)}, u32[]{:S(2)}) collective-permute-start(f32[32,256]{1,0:T(8,128)S(1)} %get-tuple-element.48.refs_0_), channel_id=1, source_target_pairs={{0,12},{1,13},{2,14},{3,15},{4,8},{5,9},{6,10},{7,11},{8,4},{9,5},... | collective-permute-start | bytes 98312 | tf_op jit(solution)/shard_map/ppermute | solution.py:361
  33.9 3.2 %collective-permute-start.12 = (f32[32,256]{1,0:T(8,128)S(1)}, f32[32,256]{1,0:T(8,128)S(1)}, u32[]{:S(2)}, u32[]{:S(2)}) collective-permute-start(f32[32,256]{1,0:T(8,128)S(1)} %get-tuple-element.50), channel_id=1, source_target_pairs={{0,1},{1,0},{2,3},{3,2},{4,5},{5,4},{6,7},{7,6},{8,9},{9,8},{10,11... | collective-permute-start | bytes 98312 | tf_op jit(solution)/shard_map/ppermute | solution.py:361
  34.0 4.1 %collective-permute-start.13 = (f32[32,256]{1,0:T(8,128)S(1)}, f32[32,256]{1,0:T(8,128)S(1)}, u32[]{:S(2)}, u32[]{:S(2)}) collective-permute-start(f32[32,256]{1,0:T(8,128)S(1)} %get-tuple-element.51), channel_id=1, source_target_pairs={{0,2},{1,3},{2,0},{3,1},{4,6},{5,7},{6,4},{7,5},{8,10},{9,11},{10,... | collective-permute-start | bytes 98312 | tf_op jit(solution)/shard_map/ppermute | solution.py:361
  34.8 3.7 %collective-permute-start.14 = (f32[32,256]{1,0:T(8,128)S(1)}, f32[32,256]{1,0:T(8,128)S(1)}, u32[]{:S(2)}, u32[]{:S(2)}) collective-permute-start(f32[32,256]{1,0:T(8,128)S(1)} %get-tuple-element.52), channel_id=1, source_target_pairs={{0,3},{1,2},{2,1},{3,0},{4,7},{5,6},{6,5},{7,4},{8,11},{9,10},{10,... | collective-permute-start | bytes 98312 | tf_op jit(solution)/shard_map/ppermute | solution.py:361

commit v8 on v7

--- a/solution.py
+++ b/solution.py
@@ -13,10 +13,19 @@
 LANES = 128
 EPS = 1e-05
 MIB = 1024 * 1024
+MASKED = -1e30
 
 
 def layer_norm(values):
     center = values - jnp.mean(values, axis=-1, keepdims=True)
+    spread = jnp.mean(center * center, axis=-1, keepdims=True)
+    return center * lax.rsqrt(spread + EPS)
+
+
+def layer_norm_half(values):
+    depth = values.shape[-1]
+    total = dot(values, jnp.ones((depth, depth), BF16))
+    center = values.astype(F32) - total * (1.0 / depth)
     spread = jnp.mean(center * center, axis=-1, keepdims=True)
     return center * lax.rsqrt(spread + EPS)
 
@@ -223,7 +232,7 @@
     out_buf[...] = total.reshape(out_buf.shape)
     out_copy = pltpu.make_async_copy(out_buf, out_hbm, sems.at[1])
     out_copy.start()
-    spread = dot(layer_norm(total.astype(F32)).astype(BF16), wrep_ref[...])
+    spread = dot(layer_norm_half(total).astype(BF16), wrep_ref[...])
     bias = jnp.zeros((res, wide), F32)
     for i in range(res):
         bias = jnp.where(query == i, spread[i * res : (i + 1) * res], bias)
@@ -240,7 +249,7 @@
 
 
 def key_kernel(seqs, res, count_b, *refs):
-    rows_refs, (wk_ref, wv_ref, key_ref, value_ref, limit_ref) = refs[:count_b], refs[count_b:]
+    rows_refs, (wk_ref, wv_ref, key_ref, value_ref, keep_ref) = refs[:count_b], refs[count_b:]
     spread = spread_matrix(seqs, seqs * LANES, lambda c: c // LANES)
     for weight_ref, ref in ((wk_ref, key_ref), (wv_ref, value_ref)):
         weight = weight_ref[...]
@@ -250,12 +259,11 @@
                 ref[s, k * res : (k + 1) * res, :] = made[s * res : (s + 1) * res]
     for k in range(count_b):
         keep = dot_tn(rows_refs[k][seqs * res : seqs * res + seqs, :res], spread)
-        keep = jnp.where(keep > 0, 3e38, -1000000000.0)
         for s in range(seqs):
-            limit_ref[s, k * res : (k + 1) * res, :] = keep[:, s * LANES : (s + 1) * LANES]
-
-
-def score_kernel(seqs, res, heads, query_ref, key_ref, score_ref):
+            keep_ref[s, k * res : (k + 1) * res, :] = keep[:, s * LANES : (s + 1) * LANES]
+
+
+def score_kernel(seqs, res, heads, query_ref, key_ref, keep_ref, score_ref):
     channels = query_ref.shape[1]
     wide = heads * res
     same_head = iota((wide, channels), 0) // res == iota((wide, channels), 1) // (channels // heads)
@@ -265,25 +273,24 @@
             jnp.concatenate([query_ref[s * res : (s + 1) * res, :]] * heads, axis=0),
             jnp.zeros((), BF16),
         )
-        score_ref[s] = dot_nt(key_ref[s], query_wide)
+        keep = jnp.concatenate([keep_ref[s]] * (wide // LANES), axis=1)
+        score_ref[s] = jnp.where(keep > 0, dot_nt(key_ref[s], query_wide), MASKED)
 
 
 def attention_kernel(seqs, res, heads, count_b, *refs):
-    score_ref, value_ref, limit_ref, gate_ref = refs[:4]
-    bias_refs, refs = refs[4 : 4 + count_b], refs[4 + count_b :]
-    wo_ref, up_ref, down_ref, x_ref, out_ref, bias_scr, att_scr, diag_scr = refs
+    score_ref, value_ref, gate_ref = refs[:3]
+    bias_refs, refs = refs[3 : 3 + count_b], refs[3 + count_b :]
+    wo_ref, up_ref, down_ref, x_ref, out_ref, att_scr, diag_scr = refs
     channels = out_ref.shape[1]
     head_width = channels // heads
     wide = heads * res
     per = LANES // head_width
-    for k in range(count_b):
-        bias_scr[k * res : (k + 1) * res, :] = bias_refs[k][...]
+    bias = jnp.concatenate([b[...] for b in bias_refs], axis=0)
     lane_head = iota((res, LANES), 1) // head_width
     diag = iota((res, wide), 0) == iota((res, wide), 1) % res
     head_pick = (iota((wide, channels), 0) // res == iota((wide, channels), 1) // head_width).astype(F32).astype(BF16)
     for s in range(seqs):
-        top = jnp.concatenate([limit_ref[s]] * (wide // LANES), axis=1)
-        scores = jnp.minimum(score_ref[s] + bias_scr[...], top)
+        scores = score_ref[s] + bias
         raw = jnp.exp(scores - jnp.max(scores, axis=0, keepdims=True))
         mass = jnp.sum(raw, axis=0, keepdims=True)
         diag_scr[s * res : (s + 1) * res, :] = jnp.where(diag, 1.0 / mass, 0.0)
@@ -429,7 +436,7 @@
         (shape((seqs * res, channels), BF16), shape((seqs * res, channels), F32)),
     )(rows, *w_query)
     keys = res * count_b
-    key, value, limit = call(
+    key, value, keeps = call(
         functools.partial(key_kernel, seqs, res, count_b),
         8,
         (
@@ -442,7 +449,7 @@
         functools.partial(score_kernel, seqs, res, heads),
         8,
         (shape((seqs, keys, heads * res), F32),),
-    )(query, key)
+    )(query, key, keeps)
 
     tiles = [bias] + [along_a(bias, k) for k in range(1, count_a)]
     biases = call(
@@ -457,11 +464,10 @@
         16,
         (shape((seqs * res, channels), BF16),),
         [
-            pltpu.VMEM((keys, heads * res), F32),
             pltpu.VMEM((seqs * res, channels), F32),
             pltpu.VMEM((seqs * res, heads * res), F32),
         ],
-    )(scores, value, limit, gate, *biases, *kept)
+    )(scores, value, gate, *biases, *kept)
     return (out.reshape(seqs, res, channels), pair_output)
 
 

time: 40.7 us -> 40.3 us (level)
  Pallas kernels: 10.2 us -> 9.71 us
    pallas_call x1, Pallas kernels: 3.72 us -> 3.31 us  [per_device(): call(functools.partial(pair_kernel, count_a, res, width), 16, (shape(pair...]
  transfers between devices with their start and end apart: 15 -> 15, of which waited for: 7 -> 7; matrix products, arithmetic and copies ran while one was open for 0% -> 0% of each run, Pallas kernels for 16% -> 15%
where the time goes in v8:
time: 40.3 us; the launch traced here: 40.1 us
  starting transfers between devices  16.4 us (41%)
  waiting for transfers between devices  13.3 us (33%)
  Pallas kernels  9.71 us (24%)
  between operations  0.74 us (2%)
    ppermute x15, starting transfers between devices, permute(): return lax.ppermute(value, ('aa', 'ba'), pairs)  16.4 us
    ppermute x15, waiting for transfers between devices, permute(): return lax.ppermute(value, ('aa', 'ba'), pairs)  13.3 us
    pallas_call x1, Pallas kernels, per_device(): call(functools.partial(pair_kernel, count_a, res, width), 16, (shape(pair...  3.31 us
    pallas_call x1, Pallas kernels, per_device(): call(functools.partial(attention_kernel, seqs, res, heads, count_b), 16,...  2.03 us
    pallas_call x1, Pallas kernels, per_device(): call(functools.partial(factor_kernel, seqs, res), 4, (shape((seqs * res +...  1.6 us
    pallas_call x1, Pallas kernels, per_device(): call(functools.partial(order_kernel, res, width), 4, (shape(outer_output_...  1.52 us
  transfers between devices with their start and end apart: 15, of which 7 were waited for; matrix products, arithmetic and copies ran while one was open for 0% of the time, Pallas kernels for 15%

profile of v8, /device:TPU:0, one launch (start us, length us, event | category | flops | bytes accessed | tf_op | source)
XLA Modules:
  0.0 40.1 jit_solution(12929366849947523087)
XLA Ops:
  0.6 1.6 %shard_map.149 = (bf16[272,256]{1,0:T(8,128)(2,1)S(1)}, bf16[40,256]{1,0:T(8,128)(2,1)S(1)}, bf16[32,256]{1,0:T(8,128)(2,1)S(1)}) custom-call(bf16[32,256]{1,0:T(8,128)(2,1)} %bitcast.8, bf16[32,256]{1,0:T(8,128)(2,1)} %bitcast.9, s32[8,32]{1,0:T(8,128)} %refs_2_.2, bf16[256,256]{1,0:T(8,128)(2,1)} %bitcast.5), custom_call_target="tpu_custom_call" | custom-call | tf_op jit(solution)/shard_map/pallas_call | solution.py:379
  2.2 0.6 %collective-permute-start.3 = (bf16[40,256]{1,0:T(8,128)(2,1)S(1)}, bf16[40,256]{1,0:T(8,128)(2,1)S(1)}, u32[]{:S(2)}, u32[]{:S(2)}) collective-permute-start(bf16[40,256]{1,0:T(8,128)(2,1)S(1)} %get-tuple-element.35.refs_0_), channel_id=1, source_target_pairs={{0,1},{1,0},{2,3},{3,2},{4,5},{5,4},{6,7},{7,6},{8,9},{9,8},{10,11... | collective-permute-start | bytes 61448 | tf_op jit(solution)/shard_map/ppermute | solution.py:368
  2.8 2.6 %collective-permute-start.4 = (bf16[40,256]{1,0:T(8,128)(2,1)S(1)}, bf16[40,256]{1,0:T(8,128)(2,1)S(1)}, u32[]{:S(2)}, u32[]{:S(2)}) collective-permute-start(bf16[40,256]{1,0:T(8,128)(2,1)S(1)} %get-tuple-element.35.refs_0_), channel_id=1, source_target_pairs={{0,2},{1,3},{2,0},{3,1},{4,6},{5,7},{6,4},{7,5},{8,10},{9,11},{10,... | collective-permute-start | bytes 61448 | tf_op jit(solution)/shard_map/ppermute | solution.py:368
  5.3 0.0 collective-permute-start.5
  5.4 0.0 collective-permute-done.3.refs_1_
  5.4 1.7 %collective-permute-done.4.refs_2_ = bf16[40,256]{1,0:T(8,128)(2,1)S(1)} collective-permute-done((bf16[40,256]{1,0:T(8,128)(2,1)S(1)}, bf16[40,256]{1,0:T(8,128)(2,1)S(1)}, u32[]{:S(2)}, u32[]{:S(2)}) %collective-permute-start.4) | collective-permute-done | bytes 20512 | tf_op jit(solution)/shard_map/ppermute | solution.py:368
  7.1 1.4 %collective-permute-done.5.refs_3_ = bf16[40,256]{1,0:T(8,128)(2,1)S(1)} collective-permute-done((bf16[40,256]{1,0:T(8,128)(2,1)S(1)}, bf16[40,256]{1,0:T(8,128)(2,1)S(1)}, u32[]{:S(2)}, u32[]{:S(2)}) %collective-permute-start.5) | collective-permute-done | bytes 20512 | tf_op jit(solution)/shard_map/ppermute | solution.py:368
  8.6 1.6 %collective-permute-start.6 = (bf16[72,256]{1,0:T(8,128)(2,1)S(1)}, bf16[72,256]{1,0:T(8,128)(2,1)S(1)}, u32[]{:S(2)}, u32[]{:S(2)}) collective-permute-start(bf16[72,256]{1,0:T(8,128)(2,1)S(1)} %get-tuple-element.37), channel_id=1, source_target_pairs={{0,4},{1,5},{2,6},{3,7},{4,0},{5,1},{6,2},{7,3},{8,12},{9,13},{10,... | collective-permute-start | bytes 110600 | tf_op jit(solution)/shard_map/ppermute | solution.py:368
  10.2 0.0 collective-permute-start
  10.2 0.8 %collective-permute-start.1 = (bf16[272,256]{1,0:T(8,128)(2,1)S(1)}, bf16[272,256]{1,0:T(8,128)(2,1)S(1)}, u32[]{:S(2)}, u32[]{:S(2)}) collective-permute-start(bf16[272,256]{1,0:T(8,128)(2,1)S(1)} %get-tuple-element.30.rows_ref.refs_0_), channel_id=1, source_target_pairs={{0,2},{1,3},{2,0},{3,1},{4,6},{5,7},{6,4},{7,5},{8,10},{9,11},{10,... | collective-permute-start | bytes 417800 | tf_op jit(solution)/shard_map/ppermute | solution.py:368
  11.0 1.1 %collective-permute-start.2 = (bf16[272,256]{1,0:T(8,128)(2,1)S(1)}, bf16[272,256]{1,0:T(8,128)(2,1)S(1)}, u32[]{:S(2)}, u32[]{:S(2)}) collective-permute-start(bf16[272,256]{1,0:T(8,128)(2,1)S(1)} %get-tuple-element.30.rows_ref.refs_0_), channel_id=1, source_target_pairs={{0,3},{1,2},{2,1},{3,0},{4,7},{5,6},{6,5},{7,4},{8,11},{9,10},{10,... | collective-permute-start | bytes 417800 | tf_op jit(solution)/shard_map/ppermute | solution.py:368
  12.1 2.6 %collective-permute-start.7 = (bf16[72,256]{1,0:T(8,128)(2,1)S(1)}, bf16[72,256]{1,0:T(8,128)(2,1)S(1)}, u32[]{:S(2)}, u32[]{:S(2)}) collective-permute-start(bf16[72,256]{1,0:T(8,128)(2,1)S(1)} %get-tuple-element.38), channel_id=1, source_target_pairs={{0,8},{1,9},{2,10},{3,11},{4,12},{5,13},{6,14},{7,15},{8,0},{9,1},... | collective-permute-start | bytes 110600 | tf_op jit(solution)/shard_map/ppermute | solution.py:368
  14.7 0.0 collective-permute-done.6.refs_1_
  14.7 1.5 %collective-permute-start.8 = (bf16[72,256]{1,0:T(8,128)(2,1)S(1)}, bf16[72,256]{1,0:T(8,128)(2,1)S(1)}, u32[]{:S(2)}, u32[]{:S(2)}) collective-permute-start(bf16[72,256]{1,0:T(8,128)(2,1)S(1)} %get-tuple-element.39), channel_id=1, source_target_pairs={{0,12},{1,13},{2,14},{3,15},{4,8},{5,9},{6,10},{7,11},{8,4},{9,5},... | collective-permute-start | bytes 110600 | tf_op jit(solution)/shard_map/ppermute | solution.py:368
  16.2 1.5 %shard_map.150 = (bf16[1024,128]{1,0:T(8,128)(2,1)S(1)}, bf16[128,256]{1,0:T(8,128)(2,1)S(1)}, bf16[256,256]{1,0:T(8,128)(2,1)S(1)}, bf16[256,256]{1,0:T(8,128)(2,1)S(1)}) custom-call(bf16[1024,128]{1,0:T(8,128)(2,1)} %refs_0_.1, bf16[8,128]{1,0:T(8,128)(2,1)} %bitcast.10, bf16[256,256]{1,0:T(8,128)(2,1)} %refs_2_.3, bf16[256,256]{1,0:T(8,128)(2,1)} %refs_3_.1), custom_call_target="tpu_custom_call" | custom-call | tf_op jit(solution)/shard_map/pallas_call | solution.py:404
  17.7 0.0 collective-permute-done.7.refs_2_
  17.7 2.7 %collective-permute-done.8.refs_3_ = bf16[72,256]{1,0:T(8,128)(2,1)S(1)} collective-permute-done((bf16[72,256]{1,0:T(8,128)(2,1)S(1)}, bf16[72,256]{1,0:T(8,128)(2,1)S(1)}, u32[]{:S(2)}, u32[]{:S(2)}) %collective-permute-start.8) | collective-permute-done | bytes 36896 | tf_op jit(solution)/shard_map/ppermute | solution.py:368
  20.4 3.3 %shard_map.153 = (bf16[32,32,128]{2,1,0:T(8,128)(2,1)}, f32[32,256]{1,0:T(8,128)S(1)}, bf16[256,256]{1,0:T(8,128)(2,1)S(1)}, bf16[256,256]{1,0:T(8,128)(2,1)S(1)...) custom-call(bf16[72,256]{1,0:T(8,128)(2,1)S(1)} %get-tuple-element.3, ...), custom_call_target="tpu_custom_call" | custom-call | tf_op jit(solution)/shard_map/pallas_call | solution.py:418
  23.7 0.1 collective-permute-start.9
  23.8 2.1 %collective-permute-start.10 = (f32[32,256]{1,0:T(8,128)S(1)}, f32[32,256]{1,0:T(8,128)S(1)}, u32[]{:S(2)}, u32[]{:S(2)}) collective-permute-start(f32[32,256]{1,0:T(8,128)S(1)} %get-tuple-element.48.refs_0_), channel_id=1, source_target_pairs={{0,8},{1,9},{2,10},{3,11},{4,12},{5,13},{6,14},{7,15},{8,0},{9,1},... | collective-permute-start | bytes 98312 | tf_op jit(solution)/shard_map/ppermute | solution.py:368
  25.9 1.8 %collective-permute-done.9.refs_1_ = f32[32,256]{1,0:T(8,128)S(1)} collective-permute-done((f32[32,256]{1,0:T(8,128)S(1)}, f32[32,256]{1,0:T(8,128)S(1)}, u32[]{:S(2)}, u32[]{:S(2)}) %collective-permute-start.9) | collective-permute-done | bytes 32800 | tf_op jit(solution)/shard_map/ppermute | solution.py:368
  27.7 1.5 %collective-permute-start.11 = (f32[32,256]{1,0:T(8,128)S(1)}, f32[32,256]{1,0:T(8,128)S(1)}, u32[]{:S(2)}, u32[]{:S(2)}) collective-permute-start(f32[32,256]{1,0:T(8,128)S(1)} %get-tuple-element.48.refs_0_), channel_id=1, source_target_pairs={{0,12},{1,13},{2,14},{3,15},{4,8},{5,9},{6,10},{7,11},{8,4},{9,5},... | collective-permute-start | bytes 98312 | tf_op jit(solution)/shard_map/ppermute | solution.py:368
  29.3 0.0 collective-permute-done.10.refs_2_
  29.3 4.2 %collective-permute-done.11.refs_3_ = f32[32,256]{1,0:T(8,128)S(1)} collective-permute-done((f32[32,256]{1,0:T(8,128)S(1)}, f32[32,256]{1,0:T(8,128)S(1)}, u32[]{:S(2)}, u32[]{:S(2)}) %collective-permute-start.11) | collective-permute-done | bytes 32800 | tf_op jit(solution)/shard_map/ppermute | solution.py:368
  33.5 0.1 collective-permute-start.12
  33.5 0.8 %collective-permute-start.13 = (f32[32,256]{1,0:T(8,128)S(1)}, f32[32,256]{1,0:T(8,128)S(1)}, u32[]{:S(2)}, u32[]{:S(2)}) collective-permute-start(f32[32,256]{1,0:T(8,128)S(1)} %get-tuple-element.51), channel_id=1, source_target_pairs={{0,2},{1,3},{2,0},{3,1},{4,6},{5,7},{6,4},{7,5},{8,10},{9,11},{10,... | collective-permute-start | bytes 98312 | tf_op jit(solution)/shard_map/ppermute | solution.py:368
  34.4 0.0 collective-permute-done.refs_1_
  34.4 1.0 %collective-permute-start.14 = (f32[32,256]{1,0:T(8,128)S(1)}, f32[32,256]{1,0:T(8,128)S(1)}, u32[]{:S(2)}, u32[]{:S(2)}) collective-permute-start(f32[32,256]{1,0:T(8,128)S(1)} %get-tuple-element.52), channel_id=1, source_target_pairs={{0,3},{1,2},{2,1},{3,0},{4,7},{5,6},{6,5},{7,4},{8,11},{9,10},{10,... | collective-permute-start | bytes 98312 | tf_op jit(solution)/shard_map/ppermute | solution.py:368
  35.4 0.2 shard_map.151
  35.6 0.0 collective-permute-done.1.refs_2_
  35.7 0.0 collective-permute-done.2.refs_3_
  35.7 0.5 %shard_map.154 = (bf16[8,128,256]{2,1,0:T(8,128)(2,1)S(1)}, bf16[8,128,256]{2,1,0:T(8,128)(2,1)S(1)}, f32[8,128,128]{2,1,0:T(8,128)S(1)}) custom-call(bf16[272,256]{1,0:T(8,128)(2,1)S(1)} %get-tuple-element.30.rows_ref.refs_0_, bf16[272,256]{1,0:T(8,128)(2,1)S(1)} %collective-permute-done.refs_1_, bf16[272,256]{1,0:T(8,128)(2,1)S(1)} %collective-permute-done.1.refs_2_, ...), custom_call_target="tpu_custom_call" | custom-call | tf_op jit(solution)/shard_map/pallas_call | solution.py:439
  36.2 0.5 %shard_map.155.refs_0_ = f32[8,128,256]{2,1,0:T(8,128)S(1)} custom-call(bf16[256,256]{1,0:T(8,128)(2,1)S(1)} %get-tuple-element.33.query_ref, bf16[8,128,256]{2,1,0:T(8,128)(2,1)S(1)} %get-tuple-element.44.key_ref, f32[8,128,128]{2,1,0:T(8,128)S(1)} %get-tuple-element.45.keep_ref), custom_call_target="tpu_custom_call" | custom-call | tf_op jit(solution)/shard_map/pallas_call | solution.py:448
  36.7 0.0 collective-permute-done.12.refs_4_
  36.7 1.0 %collective-permute-done.13.refs_5_ = f32[32,256]{1,0:T(8,128)S(1)} collective-permute-done((f32[32,256]{1,0:T(8,128)S(1)}, f32[32,256]{1,0:T(8,128)S(1)}, u32[]{:S(2)}, u32[]{:S(2)}) %collective-permute-start.13) | collective-permute-done | bytes 32800 | tf_op jit(solution)/shard_map/ppermute | solution.py:368
  37.7 0.4 collective-permute-done.14.refs_6_
  38.1 2.0 %shard_map.157 = bf16[256,256]{1,0:T(8,128)(2,1)} custom-call(f32[8,128,256]{2,1,0:T(8,128)S(1)} %shard_map.155.refs_0_, bf16[8,128,256]{2,1,0:T(8,128)(2,1)S(1)} %get-tuple-element.46.refs_1_, f32[256,256]{1,0:T(8,128)S(1)} %get-tuple-element.47.refs_2_, f32[32,256]{1,0:T(8,128)S(1)} %get-tuple-element.49.refs_3_, ...), custom_call_target="tpu_custom_call" | custom-call | tf_op jit(solution)/shard_map/pallas_call | solution.py:462
  (2 shorter events, 0.0 us)
Async XLA Ops:
  2.2 3.2 %collective-permute-start.3 = (bf16[40,256]{1,0:T(8,128)(2,1)S(1)}, bf16[40,256]{1,0:T(8,128)(2,1)S(1)}, u32[]{:S(2)}, u32[]{:S(2)}) collective-permute-start(bf16[40,256]{1,0:T(8,128)(2,1)S(1)} %get-tuple-element.35.refs_0_), channel_id=1, source_target_pairs={{0,1},{1,0},{2,3},{3,2},{4,5},{5,4},{6,7},{7,6},{8,9},{9,8},{10,11... | collective-permute-start | bytes 61448 | tf_op jit(solution)/shard_map/ppermute | solution.py:368
  2.8 4.3 %collective-permute-start.4 = (bf16[40,256]{1,0:T(8,128)(2,1)S(1)}, bf16[40,256]{1,0:T(8,128)(2,1)S(1)}, u32[]{:S(2)}, u32[]{:S(2)}) collective-permute-start(bf16[40,256]{1,0:T(8,128)(2,1)S(1)} %get-tuple-element.35.refs_0_), channel_id=1, source_target_pairs={{0,2},{1,3},{2,0},{3,1},{4,6},{5,7},{6,4},{7,5},{8,10},{9,11},{10,... | collective-permute-start | bytes 61448 | tf_op jit(solution)/shard_map/ppermute | solution.py:368
  5.3 3.2 %collective-permute-start.5 = (bf16[40,256]{1,0:T(8,128)(2,1)S(1)}, bf16[40,256]{1,0:T(8,128)(2,1)S(1)}, u32[]{:S(2)}, u32[]{:S(2)}) collective-permute-start(bf16[40,256]{1,0:T(8,128)(2,1)S(1)} %get-tuple-element.35.refs_0_), channel_id=1, source_target_pairs={{0,3},{1,2},{2,1},{3,0},{4,7},{5,6},{6,5},{7,4},{8,11},{9,10},{10,... | collective-permute-start | bytes 61448 | tf_op jit(solution)/shard_map/ppermute | solution.py:368
  8.6 6.1 %collective-permute-start.6 = (bf16[72,256]{1,0:T(8,128)(2,1)S(1)}, bf16[72,256]{1,0:T(8,128)(2,1)S(1)}, u32[]{:S(2)}, u32[]{:S(2)}) collective-permute-start(bf16[72,256]{1,0:T(8,128)(2,1)S(1)} %get-tuple-element.37), channel_id=1, source_target_pairs={{0,4},{1,5},{2,6},{3,7},{4,0},{5,1},{6,2},{7,3},{8,12},{9,13},{10,... | collective-permute-start | bytes 110600 | tf_op jit(solution)/shard_map/ppermute | solution.py:368
  10.2 24.1 %collective-permute-start = (bf16[272,256]{1,0:T(8,128)(2,1)S(1)}, bf16[272,256]{1,0:T(8,128)(2,1)S(1)}, u32[]{:S(2)}, u32[]{:S(2)}) collective-permute-start(bf16[272,256]{1,0:T(8,128)(2,1)S(1)} %get-tuple-element.30.rows_ref.refs_0_), channel_id=1, source_target_pairs={{0,1},{1,0},{2,3},{3,2},{4,5},{5,4},{6,7},{7,6},{8,9},{9,8},{10,11... | collective-permute-start | bytes 417800 | tf_op jit(solution)/shard_map/ppermute | solution.py:368
  10.2 25.4 %collective-permute-start.1 = (bf16[272,256]{1,0:T(8,128)(2,1)S(1)}, bf16[272,256]{1,0:T(8,128)(2,1)S(1)}, u32[]{:S(2)}, u32[]{:S(2)}) collective-permute-start(bf16[272,256]{1,0:T(8,128)(2,1)S(1)} %get-tuple-element.30.rows_ref.refs_0_), channel_id=1, source_target_pairs={{0,2},{1,3},{2,0},{3,1},{4,6},{5,7},{6,4},{7,5},{8,10},{9,11},{10,... | collective-permute-start | bytes 417800 | tf_op jit(solution)/shard_map/ppermute | solution.py:368
  11.0 24.7 %collective-permute-start.2 = (bf16[272,256]{1,0:T(8,128)(2,1)S(1)}, bf16[272,256]{1,0:T(8,128)(2,1)S(1)}, u32[]{:S(2)}, u32[]{:S(2)}) collective-permute-start(bf16[272,256]{1,0:T(8,128)(2,1)S(1)} %get-tuple-element.30.rows_ref.refs_0_), channel_id=1, source_target_pairs={{0,3},{1,2},{2,1},{3,0},{4,7},{5,6},{6,5},{7,4},{8,11},{9,10},{10,... | collective-permute-start | bytes 417800 | tf_op jit(solution)/shard_map/ppermute | solution.py:368
  12.1 5.6 %collective-permute-start.7 = (bf16[72,256]{1,0:T(8,128)(2,1)S(1)}, bf16[72,256]{1,0:T(8,128)(2,1)S(1)}, u32[]{:S(2)}, u32[]{:S(2)}) collective-permute-start(bf16[72,256]{1,0:T(8,128)(2,1)S(1)} %get-tuple-element.38), channel_id=1, source_target_pairs={{0,8},{1,9},{2,10},{3,11},{4,12},{5,13},{6,14},{7,15},{8,0},{9,1},... | collective-permute-start | bytes 110600 | tf_op jit(solution)/shard_map/ppermute | solution.py:368
  14.7 5.8 %collective-permute-start.8 = (bf16[72,256]{1,0:T(8,128)(2,1)S(1)}, bf16[72,256]{1,0:T(8,128)(2,1)S(1)}, u32[]{:S(2)}, u32[]{:S(2)}) collective-permute-start(bf16[72,256]{1,0:T(8,128)(2,1)S(1)} %get-tuple-element.39), channel_id=1, source_target_pairs={{0,12},{1,13},{2,14},{3,15},{4,8},{5,9},{6,10},{7,11},{8,4},{9,5},... | collective-permute-start | bytes 110600 | tf_op jit(solution)/shard_map/ppermute | solution.py:368
  23.7 4.0 %collective-permute-start.9 = (f32[32,256]{1,0:T(8,128)S(1)}, f32[32,256]{1,0:T(8,128)S(1)}, u32[]{:S(2)}, u32[]{:S(2)}) collective-permute-start(f32[32,256]{1,0:T(8,128)S(1)} %get-tuple-element.48.refs_0_), channel_id=1, source_target_pairs={{0,4},{1,5},{2,6},{3,7},{4,0},{5,1},{6,2},{7,3},{8,12},{9,13},{10,... | collective-permute-start | bytes 98312 | tf_op jit(solution)/shard_map/ppermute | solution.py:368
  23.8 5.4 %collective-permute-start.10 = (f32[32,256]{1,0:T(8,128)S(1)}, f32[32,256]{1,0:T(8,128)S(1)}, u32[]{:S(2)}, u32[]{:S(2)}) collective-permute-start(f32[32,256]{1,0:T(8,128)S(1)} %get-tuple-element.48.refs_0_), channel_id=1, source_target_pairs={{0,8},{1,9},{2,10},{3,11},{4,12},{5,13},{6,14},{7,15},{8,0},{9,1},... | collective-permute-start | bytes 98312 | tf_op jit(solution)/shard_map/ppermute | solution.py:368
  27.7 5.7 %collective-permute-start.11 = (f32[32,256]{1,0:T(8,128)S(1)}, f32[32,256]{1,0:T(8,128)S(1)}, u32[]{:S(2)}, u32[]{:S(2)}) collective-permute-start(f32[32,256]{1,0:T(8,128)S(1)} %get-tuple-element.48.refs_0_), channel_id=1, source_target_pairs={{0,12},{1,13},{2,14},{3,15},{4,8},{5,9},{6,10},{7,11},{8,4},{9,5},... | collective-permute-start | bytes 98312 | tf_op jit(solution)/shard_map/ppermute | solution.py:368
  33.5 3.2 %collective-permute-start.12 = (f32[32,256]{1,0:T(8,128)S(1)}, f32[32,256]{1,0:T(8,128)S(1)}, u32[]{:S(2)}, u32[]{:S(2)}) collective-permute-start(f32[32,256]{1,0:T(8,128)S(1)} %get-tuple-element.50), channel_id=1, source_target_pairs={{0,1},{1,0},{2,3},{3,2},{4,5},{5,4},{6,7},{7,6},{8,9},{9,8},{10,11... | collective-permute-start | bytes 98312 | tf_op jit(solution)/shard_map/ppermute | solution.py:368
  33.5 4.1 %collective-permute-start.13 = (f32[32,256]{1,0:T(8,128)S(1)}, f32[32,256]{1,0:T(8,128)S(1)}, u32[]{:S(2)}, u32[]{:S(2)}) collective-permute-start(f32[32,256]{1,0:T(8,128)S(1)} %get-tuple-element.51), channel_id=1, source_target_pairs={{0,2},{1,3},{2,0},{3,1},{4,6},{5,7},{6,4},{7,5},{8,10},{9,11},{10,... | collective-permute-start | bytes 98312 | tf_op jit(solution)/shard_map/ppermute | solution.py:368
  34.4 3.7 %collective-permute-start.14 = (f32[32,256]{1,0:T(8,128)S(1)}, f32[32,256]{1,0:T(8,128)S(1)}, u32[]{:S(2)}, u32[]{:S(2)}) collective-permute-start(f32[32,256]{1,0:T(8,128)S(1)} %get-tuple-element.52), channel_id=1, source_target_pairs={{0,3},{1,2},{2,1},{3,0},{4,7},{5,6},{6,5},{7,4},{8,11},{9,10},{10,... | collective-permute-start | bytes 98312 | tf_op jit(solution)/shard_map/ppermute | solution.py:368

commit v9 on v8

--- a/solution.py
+++ b/solution.py
@@ -221,21 +221,28 @@
     wide = wrep_ref.shape[1]
     query = iota((res, wide), 1) % res
     pair = get_pair()
-    upd = dot(a_scr[...], wout_ref[...])
-    total = jnp.concatenate(
-        [
-            pair[i].astype(F32) + upd[i * res : (i + 1) * res] * inverse[:, i : i + 1]
-            for i in range(res)
-        ],
-        axis=0,
-    ).astype(BF16)
-    out_buf[...] = total.reshape(out_buf.shape)
+    bias = jnp.zeros((res, wide), F32)
+    chunk = 16 if res % 16 == 0 else res
+    totals = []
+    for start in range(0, res, chunk):
+        upd = dot(a_scr[start * res : (start + chunk) * res, :], wout_ref[...])
+        totals.append(
+            jnp.concatenate(
+                [
+                    pair[start + i].astype(F32)
+                    + upd[i * res : (i + 1) * res] * inverse[:, start + i : start + i + 1]
+                    for i in range(chunk)
+                ],
+                axis=0,
+            ).astype(BF16)
+        )
+        out_buf[start : start + chunk] = totals[-1].reshape(chunk, res, upd.shape[1])
     out_copy = pltpu.make_async_copy(out_buf, out_hbm, sems.at[1])
     out_copy.start()
-    spread = dot(layer_norm_half(total).astype(BF16), wrep_ref[...])
-    bias = jnp.zeros((res, wide), F32)
-    for i in range(res):
-        bias = jnp.where(query == i, spread[i * res : (i + 1) * res], bias)
+    for n, total in enumerate(totals):
+        spread = dot(layer_norm_half(total).astype(BF16), wrep_ref[...])
+        for i in range(chunk):
+            bias = jnp.where(query == n * chunk + i, spread[i * res : (i + 1) * res], bias)
     bias_ref[...] = bias
     out_copy.wait()
     done()

time: 40.3 us -> 40.1 us (level)
  no operation moved by 1% of the time
where the time goes in v9:
time: 40.1 us; the launch traced here: 39.9 us
  starting transfers between devices  16.4 us (41%)
  waiting for transfers between devices  13.3 us (33%)
  Pallas kernels  9.55 us (24%)
  between operations  0.74 us (2%)
    ppermute x15, starting transfers between devices, permute(): return lax.ppermute(value, ('aa', 'ba'), pairs)  16.4 us
    ppermute x15, waiting for transfers between devices, permute(): return lax.ppermute(value, ('aa', 'ba'), pairs)  13.3 us
    pallas_call x1, Pallas kernels, per_device(): call(functools.partial(pair_kernel, count_a, res, width), 16, (shape(pair...  3.15 us
    pallas_call x1, Pallas kernels, per_device(): call(functools.partial(attention_kernel, seqs, res, heads, count_b), 16,...  2.03 us
    pallas_call x1, Pallas kernels, per_device(): call(functools.partial(factor_kernel, seqs, res), 4, (shape((seqs * res +...  1.6 us
    pallas_call x1, Pallas kernels, per_device(): call(functools.partial(order_kernel, res, width), 4, (shape(outer_output_...  1.52 us
  transfers between devices with their start and end apart: 15, of which 7 were waited for; matrix products, arithmetic and copies ran while one was open for 0% of the time, Pallas kernels for 15%

profile of v9, /device:TPU:0, one launch (start us, length us, event | category | flops | bytes accessed | tf_op | source)
XLA Modules:
  0.0 39.9 jit_solution(3158892398395640825)
XLA Ops:
  0.6 1.6 %shard_map.149 = (bf16[272,256]{1,0:T(8,128)(2,1)S(1)}, bf16[40,256]{1,0:T(8,128)(2,1)S(1)}, bf16[32,256]{1,0:T(8,128)(2,1)S(1)}) custom-call(bf16[32,256]{1,0:T(8,128)(2,1)} %bitcast.8, bf16[32,256]{1,0:T(8,128)(2,1)} %bitcast.9, s32[8,32]{1,0:T(8,128)} %refs_2_.2, bf16[256,256]{1,0:T(8,128)(2,1)} %bitcast.5), custom_call_target="tpu_custom_call" | custom-call | tf_op jit(solution)/shard_map/pallas_call | solution.py:386
  2.2 0.6 %collective-permute-start.3 = (bf16[40,256]{1,0:T(8,128)(2,1)S(1)}, bf16[40,256]{1,0:T(8,128)(2,1)S(1)}, u32[]{:S(2)}, u32[]{:S(2)}) collective-permute-start(bf16[40,256]{1,0:T(8,128)(2,1)S(1)} %get-tuple-element.35.refs_0_), channel_id=1, source_target_pairs={{0,1},{1,0},{2,3},{3,2},{4,5},{5,4},{6,7},{7,6},{8,9},{9,8},{10,11... | collective-permute-start | bytes 61448 | tf_op jit(solution)/shard_map/ppermute | solution.py:375
  2.8 2.6 %collective-permute-start.4 = (bf16[40,256]{1,0:T(8,128)(2,1)S(1)}, bf16[40,256]{1,0:T(8,128)(2,1)S(1)}, u32[]{:S(2)}, u32[]{:S(2)}) collective-permute-start(bf16[40,256]{1,0:T(8,128)(2,1)S(1)} %get-tuple-element.35.refs_0_), channel_id=1, source_target_pairs={{0,2},{1,3},{2,0},{3,1},{4,6},{5,7},{6,4},{7,5},{8,10},{9,11},{10,... | collective-permute-start | bytes 61448 | tf_op jit(solution)/shard_map/ppermute | solution.py:375
  5.3 0.0 collective-permute-start.5
  5.4 0.0 collective-permute-done.3.refs_1_
  5.4 1.7 %collective-permute-done.4.refs_2_ = bf16[40,256]{1,0:T(8,128)(2,1)S(1)} collective-permute-done((bf16[40,256]{1,0:T(8,128)(2,1)S(1)}, bf16[40,256]{1,0:T(8,128)(2,1)S(1)}, u32[]{:S(2)}, u32[]{:S(2)}) %collective-permute-start.4) | collective-permute-done | bytes 20512 | tf_op jit(solution)/shard_map/ppermute | solution.py:375
  7.1 1.4 %collective-permute-done.5.refs_3_ = bf16[40,256]{1,0:T(8,128)(2,1)S(1)} collective-permute-done((bf16[40,256]{1,0:T(8,128)(2,1)S(1)}, bf16[40,256]{1,0:T(8,128)(2,1)S(1)}, u32[]{:S(2)}, u32[]{:S(2)}) %collective-permute-start.5) | collective-permute-done | bytes 20512 | tf_op jit(solution)/shard_map/ppermute | solution.py:375
  8.6 1.6 %collective-permute-start.6 = (bf16[72,256]{1,0:T(8,128)(2,1)S(1)}, bf16[72,256]{1,0:T(8,128)(2,1)S(1)}, u32[]{:S(2)}, u32[]{:S(2)}) collective-permute-start(bf16[72,256]{1,0:T(8,128)(2,1)S(1)} %get-tuple-element.37), channel_id=1, source_target_pairs={{0,4},{1,5},{2,6},{3,7},{4,0},{5,1},{6,2},{7,3},{8,12},{9,13},{10,... | collective-permute-start | bytes 110600 | tf_op jit(solution)/shard_map/ppermute | solution.py:375
  10.2 0.0 collective-permute-start
  10.2 0.8 %collective-permute-start.1 = (bf16[272,256]{1,0:T(8,128)(2,1)S(1)}, bf16[272,256]{1,0:T(8,128)(2,1)S(1)}, u32[]{:S(2)}, u32[]{:S(2)}) collective-permute-start(bf16[272,256]{1,0:T(8,128)(2,1)S(1)} %get-tuple-element.30.rows_ref.refs_0_), channel_id=1, source_target_pairs={{0,2},{1,3},{2,0},{3,1},{4,6},{5,7},{6,4},{7,5},{8,10},{9,11},{10,... | collective-permute-start | bytes 417800 | tf_op jit(solution)/shard_map/ppermute | solution.py:375
  11.0 1.1 %collective-permute-start.2 = (bf16[272,256]{1,0:T(8,128)(2,1)S(1)}, bf16[272,256]{1,0:T(8,128)(2,1)S(1)}, u32[]{:S(2)}, u32[]{:S(2)}) collective-permute-start(bf16[272,256]{1,0:T(8,128)(2,1)S(1)} %get-tuple-element.30.rows_ref.refs_0_), channel_id=1, source_target_pairs={{0,3},{1,2},{2,1},{3,0},{4,7},{5,6},{6,5},{7,4},{8,11},{9,10},{10,... | collective-permute-start | bytes 417800 | tf_op jit(solution)/shard_map/ppermute | solution.py:375
  12.1 2.6 %collective-permute-start.7 = (bf16[72,256]{1,0:T(8,128)(2,1)S(1)}, bf16[72,256]{1,0:T(8,128)(2,1)S(1)}, u32[]{:S(2)}, u32[]{:S(2)}) collective-permute-start(bf16[72,256]{1,0:T(8,128)(2,1)S(1)} %get-tuple-element.38), channel_id=1, source_target_pairs={{0,8},{1,9},{2,10},{3,11},{4,12},{5,13},{6,14},{7,15},{8,0},{9,1},... | collective-permute-start | bytes 110600 | tf_op jit(solution)/shard_map/ppermute | solution.py:375
  14.7 0.0 collective-permute-done.6.refs_1_
  14.7 1.5 %collective-permute-start.8 = (bf16[72,256]{1,0:T(8,128)(2,1)S(1)}, bf16[72,256]{1,0:T(8,128)(2,1)S(1)}, u32[]{:S(2)}, u32[]{:S(2)}) collective-permute-start(bf16[72,256]{1,0:T(8,128)(2,1)S(1)} %get-tuple-element.39), channel_id=1, source_target_pairs={{0,12},{1,13},{2,14},{3,15},{4,8},{5,9},{6,10},{7,11},{8,4},{9,5},... | collective-permute-start | bytes 110600 | tf_op jit(solution)/shard_map/ppermute | solution.py:375
  16.2 1.5 %shard_map.150 = (bf16[1024,128]{1,0:T(8,128)(2,1)S(1)}, bf16[128,256]{1,0:T(8,128)(2,1)S(1)}, bf16[256,256]{1,0:T(8,128)(2,1)S(1)}, bf16[256,256]{1,0:T(8,128)(2,1)S(1)}) custom-call(bf16[1024,128]{1,0:T(8,128)(2,1)} %refs_0_.1, bf16[8,128]{1,0:T(8,128)(2,1)} %bitcast.10, bf16[256,256]{1,0:T(8,128)(2,1)} %refs_2_.3, bf16[256,256]{1,0:T(8,128)(2,1)} %refs_3_.1), custom_call_target="tpu_custom_call" | custom-call | tf_op jit(solution)/shard_map/pallas_call | solution.py:411
  17.7 0.0 collective-permute-done.7.refs_2_
  17.7 2.7 %collective-permute-done.8.refs_3_ = bf16[72,256]{1,0:T(8,128)(2,1)S(1)} collective-permute-done((bf16[72,256]{1,0:T(8,128)(2,1)S(1)}, bf16[72,256]{1,0:T(8,128)(2,1)S(1)}, u32[]{:S(2)}, u32[]{:S(2)}) %collective-permute-start.8) | collective-permute-done | bytes 36896 | tf_op jit(solution)/shard_map/ppermute | solution.py:375
  20.4 3.1 %shard_map.153 = (bf16[32,32,128]{2,1,0:T(8,128)(2,1)}, f32[32,256]{1,0:T(8,128)S(1)}, bf16[256,256]{1,0:T(8,128)(2,1)S(1)}, bf16[256,256]{1,0:T(8,128)(2,1)S(1)...) custom-call(bf16[72,256]{1,0:T(8,128)(2,1)S(1)} %get-tuple-element.3, ...), custom_call_target="tpu_custom_call" | custom-call | tf_op jit(solution)/shard_map/pallas_call | solution.py:425
  23.6 0.1 collective-permute-start.9
  23.7 2.1 %collective-permute-start.10 = (f32[32,256]{1,0:T(8,128)S(1)}, f32[32,256]{1,0:T(8,128)S(1)}, u32[]{:S(2)}, u32[]{:S(2)}) collective-permute-start(f32[32,256]{1,0:T(8,128)S(1)} %get-tuple-element.48.refs_0_), channel_id=1, source_target_pairs={{0,8},{1,9},{2,10},{3,11},{4,12},{5,13},{6,14},{7,15},{8,0},{9,1},... | collective-permute-start | bytes 98312 | tf_op jit(solution)/shard_map/ppermute | solution.py:375
  25.7 1.8 %collective-permute-done.9.refs_1_ = f32[32,256]{1,0:T(8,128)S(1)} collective-permute-done((f32[32,256]{1,0:T(8,128)S(1)}, f32[32,256]{1,0:T(8,128)S(1)}, u32[]{:S(2)}, u32[]{:S(2)}) %collective-permute-start.9) | collective-permute-done | bytes 32800 | tf_op jit(solution)/shard_map/ppermute | solution.py:375
  27.6 1.5 %collective-permute-start.11 = (f32[32,256]{1,0:T(8,128)S(1)}, f32[32,256]{1,0:T(8,128)S(1)}, u32[]{:S(2)}, u32[]{:S(2)}) collective-permute-start(f32[32,256]{1,0:T(8,128)S(1)} %get-tuple-element.48.refs_0_), channel_id=1, source_target_pairs={{0,12},{1,13},{2,14},{3,15},{4,8},{5,9},{6,10},{7,11},{8,4},{9,5},... | collective-permute-start | bytes 98312 | tf_op jit(solution)/shard_map/ppermute | solution.py:375
  29.1 0.0 collective-permute-done.10.refs_2_
  29.1 4.2 %collective-permute-done.11.refs_3_ = f32[32,256]{1,0:T(8,128)S(1)} collective-permute-done((f32[32,256]{1,0:T(8,128)S(1)}, f32[32,256]{1,0:T(8,128)S(1)}, u32[]{:S(2)}, u32[]{:S(2)}) %collective-permute-start.11) | collective-permute-done | bytes 32800 | tf_op jit(solution)/shard_map/ppermute | solution.py:375
  33.3 0.1 collective-permute-start.12
  33.4 0.8 %collective-permute-start.13 = (f32[32,256]{1,0:T(8,128)S(1)}, f32[32,256]{1,0:T(8,128)S(1)}, u32[]{:S(2)}, u32[]{:S(2)}) collective-permute-start(f32[32,256]{1,0:T(8,128)S(1)} %get-tuple-element.51), channel_id=1, source_target_pairs={{0,2},{1,3},{2,0},{3,1},{4,6},{5,7},{6,4},{7,5},{8,10},{9,11},{10,... | collective-permute-start | bytes 98312 | tf_op jit(solution)/shard_map/ppermute | solution.py:375
  34.2 0.0 collective-permute-done.refs_1_
  34.2 1.0 %collective-permute-start.14 = (f32[32,256]{1,0:T(8,128)S(1)}, f32[32,256]{1,0:T(8,128)S(1)}, u32[]{:S(2)}, u32[]{:S(2)}) collective-permute-start(f32[32,256]{1,0:T(8,128)S(1)} %get-tuple-element.52), channel_id=1, source_target_pairs={{0,3},{1,2},{2,1},{3,0},{4,7},{5,6},{6,5},{7,4},{8,11},{9,10},{10,... | collective-permute-start | bytes 98312 | tf_op jit(solution)/shard_map/ppermute | solution.py:375
  35.2 0.2 shard_map.151
  35.5 0.0 collective-permute-done.1.refs_2_
  35.5 0.0 collective-permute-done.2.refs_3_
  35.5 0.5 %shard_map.154 = (bf16[8,128,256]{2,1,0:T(8,128)(2,1)S(1)}, bf16[8,128,256]{2,1,0:T(8,128)(2,1)S(1)}, f32[8,128,128]{2,1,0:T(8,128)S(1)}) custom-call(bf16[272,256]{1,0:T(8,128)(2,1)S(1)} %get-tuple-element.30.rows_ref.refs_0_, bf16[272,256]{1,0:T(8,128)(2,1)S(1)} %collective-permute-done.refs_1_, bf16[272,256]{1,0:T(8,128)(2,1)S(1)} %collective-permute-done.1.refs_2_, ...), custom_call_target="tpu_custom_call" | custom-call | tf_op jit(solution)/shard_map/pallas_call | solution.py:446
  36.0 0.5 %shard_map.155.refs_0_ = f32[8,128,256]{2,1,0:T(8,128)S(1)} custom-call(bf16[256,256]{1,0:T(8,128)(2,1)S(1)} %get-tuple-element.33.query_ref, bf16[8,128,256]{2,1,0:T(8,128)(2,1)S(1)} %get-tuple-element.44.key_ref, f32[8,128,128]{2,1,0:T(8,128)S(1)} %get-tuple-element.45.keep_ref), custom_call_target="tpu_custom_call" | custom-call | tf_op jit(solution)/shard_map/pallas_call | solution.py:455
  36.5 0.0 collective-permute-done.12.refs_4_
  36.5 1.0 %collective-permute-done.13.refs_5_ = f32[32,256]{1,0:T(8,128)S(1)} collective-permute-done((f32[32,256]{1,0:T(8,128)S(1)}, f32[32,256]{1,0:T(8,128)S(1)}, u32[]{:S(2)}, u32[]{:S(2)}) %collective-permute-start.13) | collective-permute-done | bytes 32800 | tf_op jit(solution)/shard_map/ppermute | solution.py:375
  37.5 0.4 collective-permute-done.14.refs_6_
  37.9 2.0 %shard_map.157 = bf16[256,256]{1,0:T(8,128)(2,1)} custom-call(f32[8,128,256]{2,1,0:T(8,128)S(1)} %shard_map.155.refs_0_, bf16[8,128,256]{2,1,0:T(8,128)(2,1)S(1)} %get-tuple-element.46.refs_1_, f32[256,256]{1,0:T(8,128)S(1)} %get-tuple-element.47.refs_2_, f32[32,256]{1,0:T(8,128)S(1)} %get-tuple-element.49.refs_3_, ...), custom_call_target="tpu_custom_call" | custom-call | tf_op jit(solution)/shard_map/pallas_call | solution.py:469
  (2 shorter events, 0.0 us)
Async XLA Ops:
  2.2 3.2 %collective-permute-start.3 = (bf16[40,256]{1,0:T(8,128)(2,1)S(1)}, bf16[40,256]{1,0:T(8,128)(2,1)S(1)}, u32[]{:S(2)}, u32[]{:S(2)}) collective-permute-start(bf16[40,256]{1,0:T(8,128)(2,1)S(1)} %get-tuple-element.35.refs_0_), channel_id=1, source_target_pairs={{0,1},{1,0},{2,3},{3,2},{4,5},{5,4},{6,7},{7,6},{8,9},{9,8},{10,11... | collective-permute-start | bytes 61448 | tf_op jit(solution)/shard_map/ppermute | solution.py:375
  2.8 4.3 %collective-permute-start.4 = (bf16[40,256]{1,0:T(8,128)(2,1)S(1)}, bf16[40,256]{1,0:T(8,128)(2,1)S(1)}, u32[]{:S(2)}, u32[]{:S(2)}) collective-permute-start(bf16[40,256]{1,0:T(8,128)(2,1)S(1)} %get-tuple-element.35.refs_0_), channel_id=1, source_target_pairs={{0,2},{1,3},{2,0},{3,1},{4,6},{5,7},{6,4},{7,5},{8,10},{9,11},{10,... | collective-permute-start | bytes 61448 | tf_op jit(solution)/shard_map/ppermute | solution.py:375
  5.3 3.2 %collective-permute-start.5 = (bf16[40,256]{1,0:T(8,128)(2,1)S(1)}, bf16[40,256]{1,0:T(8,128)(2,1)S(1)}, u32[]{:S(2)}, u32[]{:S(2)}) collective-permute-start(bf16[40,256]{1,0:T(8,128)(2,1)S(1)} %get-tuple-element.35.refs_0_), channel_id=1, source_target_pairs={{0,3},{1,2},{2,1},{3,0},{4,7},{5,6},{6,5},{7,4},{8,11},{9,10},{10,... | collective-permute-start | bytes 61448 | tf_op jit(solution)/shard_map/ppermute | solution.py:375
  8.6 6.1 %collective-permute-start.6 = (bf16[72,256]{1,0:T(8,128)(2,1)S(1)}, bf16[72,256]{1,0:T(8,128)(2,1)S(1)}, u32[]{:S(2)}, u32[]{:S(2)}) collective-permute-start(bf16[72,256]{1,0:T(8,128)(2,1)S(1)} %get-tuple-element.37), channel_id=1, source_target_pairs={{0,4},{1,5},{2,6},{3,7},{4,0},{5,1},{6,2},{7,3},{8,12},{9,13},{10,... | collective-permute-start | bytes 110600 | tf_op jit(solution)/shard_map/ppermute | solution.py:375
  10.2 24.0 %collective-permute-start = (bf16[272,256]{1,0:T(8,128)(2,1)S(1)}, bf16[272,256]{1,0:T(8,128)(2,1)S(1)}, u32[]{:S(2)}, u32[]{:S(2)}) collective-permute-start(bf16[272,256]{1,0:T(8,128)(2,1)S(1)} %get-tuple-element.30.rows_ref.refs_0_), channel_id=1, source_target_pairs={{0,1},{1,0},{2,3},{3,2},{4,5},{5,4},{6,7},{7,6},{8,9},{9,8},{10,11... | collective-permute-start | bytes 417800 | tf_op jit(solution)/shard_map/ppermute | solution.py:375
  10.2 25.3 %collective-permute-start.1 = (bf16[272,256]{1,0:T(8,128)(2,1)S(1)}, bf16[272,256]{1,0:T(8,128)(2,1)S(1)}, u32[]{:S(2)}, u32[]{:S(2)}) collective-permute-start(bf16[272,256]{1,0:T(8,128)(2,1)S(1)} %get-tuple-element.30.rows_ref.refs_0_), channel_id=1, source_target_pairs={{0,2},{1,3},{2,0},{3,1},{4,6},{5,7},{6,4},{7,5},{8,10},{9,11},{10,... | collective-permute-start | bytes 417800 | tf_op jit(solution)/shard_map/ppermute | solution.py:375
  11.0 24.5 %collective-permute-start.2 = (bf16[272,256]{1,0:T(8,128)(2,1)S(1)}, bf16[272,256]{1,0:T(8,128)(2,1)S(1)}, u32[]{:S(2)}, u32[]{:S(2)}) collective-permute-start(bf16[272,256]{1,0:T(8,128)(2,1)S(1)} %get-tuple-element.30.rows_ref.refs_0_), channel_id=1, source_target_pairs={{0,3},{1,2},{2,1},{3,0},{4,7},{5,6},{6,5},{7,4},{8,11},{9,10},{10,... | collective-permute-start | bytes 417800 | tf_op jit(solution)/shard_map/ppermute | solution.py:375
  12.1 5.6 %collective-permute-start.7 = (bf16[72,256]{1,0:T(8,128)(2,1)S(1)}, bf16[72,256]{1,0:T(8,128)(2,1)S(1)}, u32[]{:S(2)}, u32[]{:S(2)}) collective-permute-start(bf16[72,256]{1,0:T(8,128)(2,1)S(1)} %get-tuple-element.38), channel_id=1, source_target_pairs={{0,8},{1,9},{2,10},{3,11},{4,12},{5,13},{6,14},{7,15},{8,0},{9,1},... | collective-permute-start | bytes 110600 | tf_op jit(solution)/shard_map/ppermute | solution.py:375
  14.7 5.8 %collective-permute-start.8 = (bf16[72,256]{1,0:T(8,128)(2,1)S(1)}, bf16[72,256]{1,0:T(8,128)(2,1)S(1)}, u32[]{:S(2)}, u32[]{:S(2)}) collective-permute-start(bf16[72,256]{1,0:T(8,128)(2,1)S(1)} %get-tuple-element.39), channel_id=1, source_target_pairs={{0,12},{1,13},{2,14},{3,15},{4,8},{5,9},{6,10},{7,11},{8,4},{9,5},... | collective-permute-start | bytes 110600 | tf_op jit(solution)/shard_map/ppermute | solution.py:375
  23.6 4.0 %collective-permute-start.9 = (f32[32,256]{1,0:T(8,128)S(1)}, f32[32,256]{1,0:T(8,128)S(1)}, u32[]{:S(2)}, u32[]{:S(2)}) collective-permute-start(f32[32,256]{1,0:T(8,128)S(1)} %get-tuple-element.48.refs_0_), channel_id=1, source_target_pairs={{0,4},{1,5},{2,6},{3,7},{4,0},{5,1},{6,2},{7,3},{8,12},{9,13},{10,... | collective-permute-start | bytes 98312 | tf_op jit(solution)/shard_map/ppermute | solution.py:375
  23.7 5.4 %collective-permute-start.10 = (f32[32,256]{1,0:T(8,128)S(1)}, f32[32,256]{1,0:T(8,128)S(1)}, u32[]{:S(2)}, u32[]{:S(2)}) collective-permute-start(f32[32,256]{1,0:T(8,128)S(1)} %get-tuple-element.48.refs_0_), channel_id=1, source_target_pairs={{0,8},{1,9},{2,10},{3,11},{4,12},{5,13},{6,14},{7,15},{8,0},{9,1},... | collective-permute-start | bytes 98312 | tf_op jit(solution)/shard_map/ppermute | solution.py:375
  27.6 5.7 %collective-permute-start.11 = (f32[32,256]{1,0:T(8,128)S(1)}, f32[32,256]{1,0:T(8,128)S(1)}, u32[]{:S(2)}, u32[]{:S(2)}) collective-permute-start(f32[32,256]{1,0:T(8,128)S(1)} %get-tuple-element.48.refs_0_), channel_id=1, source_target_pairs={{0,12},{1,13},{2,14},{3,15},{4,8},{5,9},{6,10},{7,11},{8,4},{9,5},... | collective-permute-start | bytes 98312 | tf_op jit(solution)/shard_map/ppermute | solution.py:375
  33.3 3.2 %collective-permute-start.12 = (f32[32,256]{1,0:T(8,128)S(1)}, f32[32,256]{1,0:T(8,128)S(1)}, u32[]{:S(2)}, u32[]{:S(2)}) collective-permute-start(f32[32,256]{1,0:T(8,128)S(1)} %get-tuple-element.50), channel_id=1, source_target_pairs={{0,1},{1,0},{2,3},{3,2},{4,5},{5,4},{6,7},{7,6},{8,9},{9,8},{10,11... | collective-permute-start | bytes 98312 | tf_op jit(solution)/shard_map/ppermute | solution.py:375
  33.4 4.1 %collective-permute-start.13 = (f32[32,256]{1,0:T(8,128)S(1)}, f32[32,256]{1,0:T(8,128)S(1)}, u32[]{:S(2)}, u32[]{:S(2)}) collective-permute-start(f32[32,256]{1,0:T(8,128)S(1)} %get-tuple-element.51), channel_id=1, source_target_pairs={{0,2},{1,3},{2,0},{3,1},{4,6},{5,7},{6,4},{7,5},{8,10},{9,11},{10,... | collective-permute-start | bytes 98312 | tf_op jit(solution)/shard_map/ppermute | solution.py:375
  34.2 3.7 %collective-permute-start.14 = (f32[32,256]{1,0:T(8,128)S(1)}, f32[32,256]{1,0:T(8,128)S(1)}, u32[]{:S(2)}, u32[]{:S(2)}) collective-permute-start(f32[32,256]{1,0:T(8,128)S(1)} %get-tuple-element.52), channel_id=1, source_target_pairs={{0,3},{1,2},{2,1},{3,0},{4,7},{5,6},{6,5},{7,4},{8,11},{9,10},{10,... | collective-permute-start | bytes 98312 | tf_op jit(solution)/shard_map/ppermute | solution.py:375

commit v10 on v9

--- a/solution.py
+++ b/solution.py
@@ -14,6 +14,7 @@
 EPS = 1e-05
 MIB = 1024 * 1024
 MASKED = -1e30
+LOG2E = 1.4426950408889634
 
 
 def layer_norm(values):
@@ -243,7 +244,7 @@
         spread = dot(layer_norm_half(total).astype(BF16), wrep_ref[...])
         for i in range(chunk):
             bias = jnp.where(query == n * chunk + i, spread[i * res : (i + 1) * res], bias)
-    bias_ref[...] = bias
+    bias_ref[...] = bias * LOG2E
     out_copy.wait()
     done()
 
@@ -281,7 +282,7 @@
             jnp.zeros((), BF16),
         )
         keep = jnp.concatenate([keep_ref[s]] * (wide // LANES), axis=1)
-        score_ref[s] = jnp.where(keep > 0, dot_nt(key_ref[s], query_wide), MASKED)
+        score_ref[s] = jnp.where(keep > 0, dot_nt(key_ref[s], query_wide) * LOG2E, MASKED)
 
 
 def attention_kernel(seqs, res, heads, count_b, *refs):
@@ -298,7 +299,7 @@
     head_pick = (iota((wide, channels), 0) // res == iota((wide, channels), 1) // head_width).astype(F32).astype(BF16)
     for s in range(seqs):
         scores = score_ref[s] + bias
-        raw = jnp.exp(scores - jnp.max(scores, axis=0, keepdims=True))
+        raw = jnp.exp2(scores - jnp.max(scores, axis=0, keepdims=True))
         mass = jnp.sum(raw, axis=0, keepdims=True)
         diag_scr[s * res : (s + 1) * res, :] = jnp.where(diag, 1.0 / mass, 0.0)
         probs = raw.astype(BF16)

time: 40.1 us -> 40.1 us (level)
  no operation moved by 1% of the time
where the time goes in v10:
time: 40.1 us; the launch traced here: 39.9 us
  starting transfers between devices  16.4 us (41%)
  waiting for transfers between devices  13.3 us (33%)
  Pallas kernels  9.55 us (24%)
  between operations  0.74 us (2%)
    ppermute x15, starting transfers between devices, permute(): return lax.ppermute(value, ('aa', 'ba'), pairs)  16.4 us
    ppermute x15, waiting for transfers between devices, permute(): return lax.ppermute(value, ('aa', 'ba'), pairs)  13.3 us
    pallas_call x1, Pallas kernels, per_device(): call(functools.partial(pair_kernel, count_a, res, width), 16, (shape(pair...  3.15 us
    pallas_call x1, Pallas kernels, per_device(): call(functools.partial(attention_kernel, seqs, res, heads, count_b), 16,...  2.02 us
    pallas_call x1, Pallas kernels, per_device(): call(functools.partial(factor_kernel, seqs, res), 4, (shape((seqs * res +...  1.6 us
    pallas_call x1, Pallas kernels, per_device(): call(functools.partial(order_kernel, res, width), 4, (shape(outer_output_...  1.52 us
  transfers between devices with their start and end apart: 15, of which 7 were waited for; matrix products, arithmetic and copies ran while one was open for 0% of the time, Pallas kernels for 15%

profile of v10, /device:TPU:0, one launch (start us, length us, event | category | flops | bytes accessed | tf_op | source)
XLA Modules:
  0.0 39.9 jit_solution(17699608173837336464)
XLA Ops:
  0.6 1.6 %shard_map.149 = (bf16[272,256]{1,0:T(8,128)(2,1)S(1)}, bf16[40,256]{1,0:T(8,128)(2,1)S(1)}, bf16[32,256]{1,0:T(8,128)(2,1)S(1)}) custom-call(bf16[32,256]{1,0:T(8,128)(2,1)} %bitcast.8, bf16[32,256]{1,0:T(8,128)(2,1)} %bitcast.9, s32[8,32]{1,0:T(8,128)} %refs_2_.2, bf16[256,256]{1,0:T(8,128)(2,1)} %bitcast.5), custom_call_target="tpu_custom_call" | custom-call | tf_op jit(solution)/shard_map/pallas_call | solution.py:387
  2.2 0.6 %collective-permute-start.3 = (bf16[40,256]{1,0:T(8,128)(2,1)S(1)}, bf16[40,256]{1,0:T(8,128)(2,1)S(1)}, u32[]{:S(2)}, u32[]{:S(2)}) collective-permute-start(bf16[40,256]{1,0:T(8,128)(2,1)S(1)} %get-tuple-element.35.refs_0_), channel_id=1, source_target_pairs={{0,1},{1,0},{2,3},{3,2},{4,5},{5,4},{6,7},{7,6},{8,9},{9,8},{10,11... | collective-permute-start | bytes 61448 | tf_op jit(solution)/shard_map/ppermute | solution.py:376
  2.8 2.6 %collective-permute-start.4 = (bf16[40,256]{1,0:T(8,128)(2,1)S(1)}, bf16[40,256]{1,0:T(8,128)(2,1)S(1)}, u32[]{:S(2)}, u32[]{:S(2)}) collective-permute-start(bf16[40,256]{1,0:T(8,128)(2,1)S(1)} %get-tuple-element.35.refs_0_), channel_id=1, source_target_pairs={{0,2},{1,3},{2,0},{3,1},{4,6},{5,7},{6,4},{7,5},{8,10},{9,11},{10,... | collective-permute-start | bytes 61448 | tf_op jit(solution)/shard_map/ppermute | solution.py:376
  5.3 0.0 collective-permute-start.5
  5.4 0.0 collective-permute-done.3.refs_1_
  5.4 1.7 %collective-permute-done.4.refs_2_ = bf16[40,256]{1,0:T(8,128)(2,1)S(1)} collective-permute-done((bf16[40,256]{1,0:T(8,128)(2,1)S(1)}, bf16[40,256]{1,0:T(8,128)(2,1)S(1)}, u32[]{:S(2)}, u32[]{:S(2)}) %collective-permute-start.4) | collective-permute-done | bytes 20512 | tf_op jit(solution)/shard_map/ppermute | solution.py:376
  7.1 1.4 %collective-permute-done.5.refs_3_ = bf16[40,256]{1,0:T(8,128)(2,1)S(1)} collective-permute-done((bf16[40,256]{1,0:T(8,128)(2,1)S(1)}, bf16[40,256]{1,0:T(8,128)(2,1)S(1)}, u32[]{:S(2)}, u32[]{:S(2)}) %collective-permute-start.5) | collective-permute-done | bytes 20512 | tf_op jit(solution)/shard_map/ppermute | solution.py:376
  8.6 1.6 %collective-permute-start.6 = (bf16[72,256]{1,0:T(8,128)(2,1)S(1)}, bf16[72,256]{1,0:T(8,128)(2,1)S(1)}, u32[]{:S(2)}, u32[]{:S(2)}) collective-permute-start(bf16[72,256]{1,0:T(8,128)(2,1)S(1)} %get-tuple-element.37), channel_id=1, source_target_pairs={{0,4},{1,5},{2,6},{3,7},{4,0},{5,1},{6,2},{7,3},{8,12},{9,13},{10,... | collective-permute-start | bytes 110600 | tf_op jit(solution)/shard_map/ppermute | solution.py:376
  10.2 0.0 collective-permute-start
  10.2 0.8 %collective-permute-start.1 = (bf16[272,256]{1,0:T(8,128)(2,1)S(1)}, bf16[272,256]{1,0:T(8,128)(2,1)S(1)}, u32[]{:S(2)}, u32[]{:S(2)}) collective-permute-start(bf16[272,256]{1,0:T(8,128)(2,1)S(1)} %get-tuple-element.30.rows_ref.refs_0_), channel_id=1, source_target_pairs={{0,2},{1,3},{2,0},{3,1},{4,6},{5,7},{6,4},{7,5},{8,10},{9,11},{10,... | collective-permute-start | bytes 417800 | tf_op jit(solution)/shard_map/ppermute | solution.py:376
  11.0 1.1 %collective-permute-start.2 = (bf16[272,256]{1,0:T(8,128)(2,1)S(1)}, bf16[272,256]{1,0:T(8,128)(2,1)S(1)}, u32[]{:S(2)}, u32[]{:S(2)}) collective-permute-start(bf16[272,256]{1,0:T(8,128)(2,1)S(1)} %get-tuple-element.30.rows_ref.refs_0_), channel_id=1, source_target_pairs={{0,3},{1,2},{2,1},{3,0},{4,7},{5,6},{6,5},{7,4},{8,11},{9,10},{10,... | collective-permute-start | bytes 417800 | tf_op jit(solution)/shard_map/ppermute | solution.py:376
  12.1 2.6 %collective-permute-start.7 = (bf16[72,256]{1,0:T(8,128)(2,1)S(1)}, bf16[72,256]{1,0:T(8,128)(2,1)S(1)}, u32[]{:S(2)}, u32[]{:S(2)}) collective-permute-start(bf16[72,256]{1,0:T(8,128)(2,1)S(1)} %get-tuple-element.38), channel_id=1, source_target_pairs={{0,8},{1,9},{2,10},{3,11},{4,12},{5,13},{6,14},{7,15},{8,0},{9,1},... | collective-permute-start | bytes 110600 | tf_op jit(solution)/shard_map/ppermute | solution.py:376
  14.7 0.0 collective-permute-done.6.refs_1_
  14.7 1.5 %collective-permute-start.8 = (bf16[72,256]{1,0:T(8,128)(2,1)S(1)}, bf16[72,256]{1,0:T(8,128)(2,1)S(1)}, u32[]{:S(2)}, u32[]{:S(2)}) collective-permute-start(bf16[72,256]{1,0:T(8,128)(2,1)S(1)} %get-tuple-element.39), channel_id=1, source_target_pairs={{0,12},{1,13},{2,14},{3,15},{4,8},{5,9},{6,10},{7,11},{8,4},{9,5},... | collective-permute-start | bytes 110600 | tf_op jit(solution)/shard_map/ppermute | solution.py:376
  16.2 1.5 %shard_map.150 = (bf16[1024,128]{1,0:T(8,128)(2,1)S(1)}, bf16[128,256]{1,0:T(8,128)(2,1)S(1)}, bf16[256,256]{1,0:T(8,128)(2,1)S(1)}, bf16[256,256]{1,0:T(8,128)(2,1)S(1)}) custom-call(bf16[1024,128]{1,0:T(8,128)(2,1)} %refs_0_.1, bf16[8,128]{1,0:T(8,128)(2,1)} %bitcast.10, bf16[256,256]{1,0:T(8,128)(2,1)} %refs_2_.3, bf16[256,256]{1,0:T(8,128)(2,1)} %refs_3_.1), custom_call_target="tpu_custom_call" | custom-call | tf_op jit(solution)/shard_map/pallas_call | solution.py:412
  17.7 0.0 collective-permute-done.7.refs_2_
  17.7 2.7 %collective-permute-done.8.refs_3_ = bf16[72,256]{1,0:T(8,128)(2,1)S(1)} collective-permute-done((bf16[72,256]{1,0:T(8,128)(2,1)S(1)}, bf16[72,256]{1,0:T(8,128)(2,1)S(1)}, u32[]{:S(2)}, u32[]{:S(2)}) %collective-permute-start.8) | collective-permute-done | bytes 36896 | tf_op jit(solution)/shard_map/ppermute | solution.py:376
  20.4 3.1 %shard_map.153 = (bf16[32,32,128]{2,1,0:T(8,128)(2,1)}, f32[32,256]{1,0:T(8,128)S(1)}, bf16[256,256]{1,0:T(8,128)(2,1)S(1)}, bf16[256,256]{1,0:T(8,128)(2,1)S(1)...) custom-call(bf16[72,256]{1,0:T(8,128)(2,1)S(1)} %get-tuple-element.3, ...), custom_call_target="tpu_custom_call" | custom-call | tf_op jit(solution)/shard_map/pallas_call | solution.py:426
  23.6 0.1 collective-permute-start.9
  23.7 2.1 %collective-permute-start.10 = (f32[32,256]{1,0:T(8,128)S(1)}, f32[32,256]{1,0:T(8,128)S(1)}, u32[]{:S(2)}, u32[]{:S(2)}) collective-permute-start(f32[32,256]{1,0:T(8,128)S(1)} %get-tuple-element.48.refs_0_), channel_id=1, source_target_pairs={{0,8},{1,9},{2,10},{3,11},{4,12},{5,13},{6,14},{7,15},{8,0},{9,1},... | collective-permute-start | bytes 98312 | tf_op jit(solution)/shard_map/ppermute | solution.py:376
  25.7 1.8 %collective-permute-done.9.refs_1_ = f32[32,256]{1,0:T(8,128)S(1)} collective-permute-done((f32[32,256]{1,0:T(8,128)S(1)}, f32[32,256]{1,0:T(8,128)S(1)}, u32[]{:S(2)}, u32[]{:S(2)}) %collective-permute-start.9) | collective-permute-done | bytes 32800 | tf_op jit(solution)/shard_map/ppermute | solution.py:376
  27.6 1.5 %collective-permute-start.11 = (f32[32,256]{1,0:T(8,128)S(1)}, f32[32,256]{1,0:T(8,128)S(1)}, u32[]{:S(2)}, u32[]{:S(2)}) collective-permute-start(f32[32,256]{1,0:T(8,128)S(1)} %get-tuple-element.48.refs_0_), channel_id=1, source_target_pairs={{0,12},{1,13},{2,14},{3,15},{4,8},{5,9},{6,10},{7,11},{8,4},{9,5},... | collective-permute-start | bytes 98312 | tf_op jit(solution)/shard_map/ppermute | solution.py:376
  29.1 0.0 collective-permute-done.10.refs_2_
  29.1 4.2 %collective-permute-done.11.refs_3_ = f32[32,256]{1,0:T(8,128)S(1)} collective-permute-done((f32[32,256]{1,0:T(8,128)S(1)}, f32[32,256]{1,0:T(8,128)S(1)}, u32[]{:S(2)}, u32[]{:S(2)}) %collective-permute-start.11) | collective-permute-done | bytes 32800 | tf_op jit(solution)/shard_map/ppermute | solution.py:376
  33.3 0.1 collective-permute-start.12
  33.4 0.8 %collective-permute-start.13 = (f32[32,256]{1,0:T(8,128)S(1)}, f32[32,256]{1,0:T(8,128)S(1)}, u32[]{:S(2)}, u32[]{:S(2)}) collective-permute-start(f32[32,256]{1,0:T(8,128)S(1)} %get-tuple-element.51), channel_id=1, source_target_pairs={{0,2},{1,3},{2,0},{3,1},{4,6},{5,7},{6,4},{7,5},{8,10},{9,11},{10,... | collective-permute-start | bytes 98312 | tf_op jit(solution)/shard_map/ppermute | solution.py:376
  34.2 0.0 collective-permute-done.refs_1_
  34.2 1.0 %collective-permute-start.14 = (f32[32,256]{1,0:T(8,128)S(1)}, f32[32,256]{1,0:T(8,128)S(1)}, u32[]{:S(2)}, u32[]{:S(2)}) collective-permute-start(f32[32,256]{1,0:T(8,128)S(1)} %get-tuple-element.52), channel_id=1, source_target_pairs={{0,3},{1,2},{2,1},{3,0},{4,7},{5,6},{6,5},{7,4},{8,11},{9,10},{10,... | collective-permute-start | bytes 98312 | tf_op jit(solution)/shard_map/ppermute | solution.py:376
  35.2 0.2 shard_map.151
  35.5 0.0 collective-permute-done.1.refs_2_
  35.5 0.0 collective-permute-done.2.refs_3_
  35.5 0.5 %shard_map.154 = (bf16[8,128,256]{2,1,0:T(8,128)(2,1)S(1)}, bf16[8,128,256]{2,1,0:T(8,128)(2,1)S(1)}, f32[8,128,128]{2,1,0:T(8,128)S(1)}) custom-call(bf16[272,256]{1,0:T(8,128)(2,1)S(1)} %get-tuple-element.30.rows_ref.refs_0_, bf16[272,256]{1,0:T(8,128)(2,1)S(1)} %collective-permute-done.refs_1_, bf16[272,256]{1,0:T(8,128)(2,1)S(1)} %collective-permute-done.1.refs_2_, ...), custom_call_target="tpu_custom_call" | custom-call | tf_op jit(solution)/shard_map/pallas_call | solution.py:447
  36.0 0.5 %shard_map.155.refs_0_ = f32[8,128,256]{2,1,0:T(8,128)S(1)} custom-call(bf16[256,256]{1,0:T(8,128)(2,1)S(1)} %get-tuple-element.33.query_ref, bf16[8,128,256]{2,1,0:T(8,128)(2,1)S(1)} %get-tuple-element.44.key_ref, f32[8,128,128]{2,1,0:T(8,128)S(1)} %get-tuple-element.45.keep_ref), custom_call_target="tpu_custom_call" | custom-call | tf_op jit(solution)/shard_map/pallas_call | solution.py:456
  36.5 0.0 collective-permute-done.12.refs_4_
  36.5 1.0 %collective-permute-done.13.refs_5_ = f32[32,256]{1,0:T(8,128)S(1)} collective-permute-done((f32[32,256]{1,0:T(8,128)S(1)}, f32[32,256]{1,0:T(8,128)S(1)}, u32[]{:S(2)}, u32[]{:S(2)}) %collective-permute-start.13) | collective-permute-done | bytes 32800 | tf_op jit(solution)/shard_map/ppermute | solution.py:376
  37.5 0.4 collective-permute-done.14.refs_6_
  37.9 2.0 %shard_map.157 = bf16[256,256]{1,0:T(8,128)(2,1)} custom-call(f32[8,128,256]{2,1,0:T(8,128)S(1)} %shard_map.155.refs_0_, bf16[8,128,256]{2,1,0:T(8,128)(2,1)S(1)} %get-tuple-element.46.refs_1_, f32[256,256]{1,0:T(8,128)S(1)} %get-tuple-element.47.refs_2_, f32[32,256]{1,0:T(8,128)S(1)} %get-tuple-element.49.refs_3_, ...), custom_call_target="tpu_custom_call" | custom-call | tf_op jit(solution)/shard_map/pallas_call | solution.py:470
  (2 shorter events, 0.0 us)
Async XLA Ops:
  2.2 3.2 %collective-permute-start.3 = (bf16[40,256]{1,0:T(8,128)(2,1)S(1)}, bf16[40,256]{1,0:T(8,128)(2,1)S(1)}, u32[]{:S(2)}, u32[]{:S(2)}) collective-permute-start(bf16[40,256]{1,0:T(8,128)(2,1)S(1)} %get-tuple-element.35.refs_0_), channel_id=1, source_target_pairs={{0,1},{1,0},{2,3},{3,2},{4,5},{5,4},{6,7},{7,6},{8,9},{9,8},{10,11... | collective-permute-start | bytes 61448 | tf_op jit(solution)/shard_map/ppermute | solution.py:376
  2.8 4.3 %collective-permute-start.4 = (bf16[40,256]{1,0:T(8,128)(2,1)S(1)}, bf16[40,256]{1,0:T(8,128)(2,1)S(1)}, u32[]{:S(2)}, u32[]{:S(2)}) collective-permute-start(bf16[40,256]{1,0:T(8,128)(2,1)S(1)} %get-tuple-element.35.refs_0_), channel_id=1, source_target_pairs={{0,2},{1,3},{2,0},{3,1},{4,6},{5,7},{6,4},{7,5},{8,10},{9,11},{10,... | collective-permute-start | bytes 61448 | tf_op jit(solution)/shard_map/ppermute | solution.py:376
  5.3 3.2 %collective-permute-start.5 = (bf16[40,256]{1,0:T(8,128)(2,1)S(1)}, bf16[40,256]{1,0:T(8,128)(2,1)S(1)}, u32[]{:S(2)}, u32[]{:S(2)}) collective-permute-start(bf16[40,256]{1,0:T(8,128)(2,1)S(1)} %get-tuple-element.35.refs_0_), channel_id=1, source_target_pairs={{0,3},{1,2},{2,1},{3,0},{4,7},{5,6},{6,5},{7,4},{8,11},{9,10},{10,... | collective-permute-start | bytes 61448 | tf_op jit(solution)/shard_map/ppermute | solution.py:376
  8.6 6.1 %collective-permute-start.6 = (bf16[72,256]{1,0:T(8,128)(2,1)S(1)}, bf16[72,256]{1,0:T(8,128)(2,1)S(1)}, u32[]{:S(2)}, u32[]{:S(2)}) collective-permute-start(bf16[72,256]{1,0:T(8,128)(2,1)S(1)} %get-tuple-element.37), channel_id=1, source_target_pairs={{0,4},{1,5},{2,6},{3,7},{4,0},{5,1},{6,2},{7,3},{8,12},{9,13},{10,... | collective-permute-start | bytes 110600 | tf_op jit(solution)/shard_map/ppermute | solution.py:376
  10.2 24.0 %collective-permute-start = (bf16[272,256]{1,0:T(8,128)(2,1)S(1)}, bf16[272,256]{1,0:T(8,128)(2,1)S(1)}, u32[]{:S(2)}, u32[]{:S(2)}) collective-permute-start(bf16[272,256]{1,0:T(8,128)(2,1)S(1)} %get-tuple-element.30.rows_ref.refs_0_), channel_id=1, source_target_pairs={{0,1},{1,0},{2,3},{3,2},{4,5},{5,4},{6,7},{7,6},{8,9},{9,8},{10,11... | collective-permute-start | bytes 417800 | tf_op jit(solution)/shard_map/ppermute | solution.py:376
  10.2 25.3 %collective-permute-start.1 = (bf16[272,256]{1,0:T(8,128)(2,1)S(1)}, bf16[272,256]{1,0:T(8,128)(2,1)S(1)}, u32[]{:S(2)}, u32[]{:S(2)}) collective-permute-start(bf16[272,256]{1,0:T(8,128)(2,1)S(1)} %get-tuple-element.30.rows_ref.refs_0_), channel_id=1, source_target_pairs={{0,2},{1,3},{2,0},{3,1},{4,6},{5,7},{6,4},{7,5},{8,10},{9,11},{10,... | collective-permute-start | bytes 417800 | tf_op jit(solution)/shard_map/ppermute | solution.py:376
  11.0 24.5 %collective-permute-start.2 = (bf16[272,256]{1,0:T(8,128)(2,1)S(1)}, bf16[272,256]{1,0:T(8,128)(2,1)S(1)}, u32[]{:S(2)}, u32[]{:S(2)}) collective-permute-start(bf16[272,256]{1,0:T(8,128)(2,1)S(1)} %get-tuple-element.30.rows_ref.refs_0_), channel_id=1, source_target_pairs={{0,3},{1,2},{2,1},{3,0},{4,7},{5,6},{6,5},{7,4},{8,11},{9,10},{10,... | collective-permute-start | bytes 417800 | tf_op jit(solution)/shard_map/ppermute | solution.py:376
  12.1 5.6 %collective-permute-start.7 = (bf16[72,256]{1,0:T(8,128)(2,1)S(1)}, bf16[72,256]{1,0:T(8,128)(2,1)S(1)}, u32[]{:S(2)}, u32[]{:S(2)}) collective-permute-start(bf16[72,256]{1,0:T(8,128)(2,1)S(1)} %get-tuple-element.38), channel_id=1, source_target_pairs={{0,8},{1,9},{2,10},{3,11},{4,12},{5,13},{6,14},{7,15},{8,0},{9,1},... | collective-permute-start | bytes 110600 | tf_op jit(solution)/shard_map/ppermute | solution.py:376
  14.7 5.8 %collective-permute-start.8 = (bf16[72,256]{1,0:T(8,128)(2,1)S(1)}, bf16[72,256]{1,0:T(8,128)(2,1)S(1)}, u32[]{:S(2)}, u32[]{:S(2)}) collective-permute-start(bf16[72,256]{1,0:T(8,128)(2,1)S(1)} %get-tuple-element.39), channel_id=1, source_target_pairs={{0,12},{1,13},{2,14},{3,15},{4,8},{5,9},{6,10},{7,11},{8,4},{9,5},... | collective-permute-start | bytes 110600 | tf_op jit(solution)/shard_map/ppermute | solution.py:376
  23.6 4.0 %collective-permute-start.9 = (f32[32,256]{1,0:T(8,128)S(1)}, f32[32,256]{1,0:T(8,128)S(1)}, u32[]{:S(2)}, u32[]{:S(2)}) collective-permute-start(f32[32,256]{1,0:T(8,128)S(1)} %get-tuple-element.48.refs_0_), channel_id=1, source_target_pairs={{0,4},{1,5},{2,6},{3,7},{4,0},{5,1},{6,2},{7,3},{8,12},{9,13},{10,... | collective-permute-start | bytes 98312 | tf_op jit(solution)/shard_map/ppermute | solution.py:376
  23.7 5.4 %collective-permute-start.10 = (f32[32,256]{1,0:T(8,128)S(1)}, f32[32,256]{1,0:T(8,128)S(1)}, u32[]{:S(2)}, u32[]{:S(2)}) collective-permute-start(f32[32,256]{1,0:T(8,128)S(1)} %get-tuple-element.48.refs_0_), channel_id=1, source_target_pairs={{0,8},{1,9},{2,10},{3,11},{4,12},{5,13},{6,14},{7,15},{8,0},{9,1},... | collective-permute-start | bytes 98312 | tf_op jit(solution)/shard_map/ppermute | solution.py:376
  27.6 5.7 %collective-permute-start.11 = (f32[32,256]{1,0:T(8,128)S(1)}, f32[32,256]{1,0:T(8,128)S(1)}, u32[]{:S(2)}, u32[]{:S(2)}) collective-permute-start(f32[32,256]{1,0:T(8,128)S(1)} %get-tuple-element.48.refs_0_), channel_id=1, source_target_pairs={{0,12},{1,13},{2,14},{3,15},{4,8},{5,9},{6,10},{7,11},{8,4},{9,5},... | collective-permute-start | bytes 98312 | tf_op jit(solution)/shard_map/ppermute | solution.py:376
  33.3 3.2 %collective-permute-start.12 = (f32[32,256]{1,0:T(8,128)S(1)}, f32[32,256]{1,0:T(8,128)S(1)}, u32[]{:S(2)}, u32[]{:S(2)}) collective-permute-start(f32[32,256]{1,0:T(8,128)S(1)} %get-tuple-element.50), channel_id=1, source_target_pairs={{0,1},{1,0},{2,3},{3,2},{4,5},{5,4},{6,7},{7,6},{8,9},{9,8},{10,11... | collective-permute-start | bytes 98312 | tf_op jit(solution)/shard_map/ppermute | solution.py:376
  33.4 4.1 %collective-permute-start.13 = (f32[32,256]{1,0:T(8,128)S(1)}, f32[32,256]{1,0:T(8,128)S(1)}, u32[]{:S(2)}, u32[]{:S(2)}) collective-permute-start(f32[32,256]{1,0:T(8,128)S(1)} %get-tuple-element.51), channel_id=1, source_target_pairs={{0,2},{1,3},{2,0},{3,1},{4,6},{5,7},{6,4},{7,5},{8,10},{9,11},{10,... | collective-permute-start | bytes 98312 | tf_op jit(solution)/shard_map/ppermute | solution.py:376
  34.2 3.7 %collective-permute-start.14 = (f32[32,256]{1,0:T(8,128)S(1)}, f32[32,256]{1,0:T(8,128)S(1)}, u32[]{:S(2)}, u32[]{:S(2)}) collective-permute-start(f32[32,256]{1,0:T(8,128)S(1)} %get-tuple-element.52), channel_id=1, source_target_pairs={{0,3},{1,2},{2,1},{3,0},{4,7},{5,6},{6,5},{7,4},{8,11},{9,10},{10,... | collective-permute-start | bytes 98312 | tf_op jit(solution)/shard_map/ppermute | solution.py:376
